TPU v7x, 256 devices: a whole 4x4x8 slice. The times are simulated.
256 devices in a mesh: tok: 32 (over z_lo, y, core), col: 8 (over x, z_hi).
Axes of the slice: x: 4, y: 4, z: 8 (z_hi: 2, z_lo: 4; z = z_hi * 4 + z_lo), core: 2. Of those that a mesh axis runs over, the one named last changes fastest.
Arguments:
- hidden: bfloat16 [8192, 8192], P('tok'), may hold values from -6 to 6
- norm_gain: float32 [8192], replicated, may hold values from 0.1 to 1.9
- token_ids: int32 [8192], P('tok'), may hold values from 0 to 128000, as said below
- owner: int32 [1], replicated, may hold values from 0 to 31
- query_store: bfloat16 [32, 8192, 4096], P('tok', None, 'col'), may hold values from -0.0625 to 0.0625
- key_store: bfloat16 [32, 8192, 512], P('tok', None, 'col'), may hold values from -0.0625 to 0.0625
Outputs:
- queries: bfloat16 [8192, 4096], P('tok', 'col')
- keys: bfloat16 [8192, 512], P('tok', 'col')
- hessian: float32 [8192, 8192], P('col', 'tok')
Inputs may be any that keep to these rules, and one draw needn't show every extreme that they name: `token_ids`: id 128000 marks the first token of a document; every other id is below it.
All inputs are finite; a program needn't handle non-finite values.
Results may differ from a plain program's by a relative error of at most 0.0049.
Values may be sent and summed in bfloat16 or wider, within the bound.
No kernel may reach another device: no remote copies, remote signals or barrier semaphores. Data moves between devices by JAX's collectives and lax.ppermute only.
A program may use at most 128 MiB of HBM per device.

v0:
```python
import functools

import jax
import jax.numpy as jnp
from jax import lax
from jax.experimental import pallas as pl
from jax.experimental.pallas import tpu as pltpu
from jax.sharding import Mesh, PartitionSpec as P

HEAD = 128
SEQ = 128


begin_token = 128000
rope_base = 500000.0

NY, NZ, NC = 4, 4, 8
TOK = ("zl", "y", "k")
COL = ("x", "zh")
ALL = TOK + COL
SIZES = {"y": NY, "zl": NZ, "k": 2}
f32, bf16 = jnp.float32, jnp.bfloat16


def send(array, axis, shift):
    n = SIZES[axis]
    return lax.ppermute(array, axis, [(i, (i + shift) % n) for i in range(n)])


def swap(array, axis, bit):
    return lax.ppermute(array, axis, [(i, i ^ bit) for i in range(SIZES[axis])])


together = lax.optimization_barrier


def pick(array, index):
    return lax.dynamic_index_in_dim(array, index, 0, keepdims=False)


def positions(token_ids):
    samples = token_ids.reshape(-1, SEQ)
    index = jnp.arange(SEQ, dtype=jnp.int32)
    starts = jnp.where(samples == begin_token, index[None, :], 0)
    seen = index[None, :] <= index[:, None]
    latest = jnp.max(jnp.where(seen[None], starts[:, None, :], 0), axis=2)
    return (index[None, :] - latest).reshape(-1)


def turns(place):
    dims = jnp.arange(HEAD, dtype=jnp.int32)
    pair = (dims // 2).astype(f32)
    freq = jnp.power(f32(rope_base), -2.0 * pair / HEAD)
    angle = place.astype(f32)[:, None] * freq[None, :]
    sign = jnp.where(dims % 2 == 0, -1.0, 1.0).astype(f32)
    return jnp.cos(angle), jnp.sin(angle) * sign[None, :]


def normalize_body(x, gain, out):
    wide = x[...].astype(f32)
    meansq = jnp.mean(wide * wide, axis=-1, keepdims=True)
    out[...] = (wide * lax.rsqrt(meansq + 1e-05) * gain[...]).astype(bf16)


def normalize(hidden, norm_gain):
    tokens, depth = hidden.shape
    rows = 32
    return pl.pallas_call(
        normalize_body,
        grid=(tokens // rows,),
        in_specs=[
            pl.BlockSpec((rows, depth), lambda i: (i, 0)),
            pl.BlockSpec((1, depth), lambda i: (0, 0)),
        ],
        out_specs=pl.BlockSpec((rows, depth), lambda i: (i, 0)),
        out_shape=jax.ShapeDtypeStruct(hidden.shape, bf16),
        cost_estimate=pl.CostEstimate(
            flops=5 * tokens * depth, bytes_accessed=4 * tokens * depth, transcendentals=tokens
        ),
        name="normalize",
    )(hidden, norm_gain.reshape(1, depth))


def block_body(role, table, q, kt, *refs):
    n = q.shape[0]
    outs = refs[-2:] if role == "far" else refs[-1:]
    p = pl.program_id(0)

    def value(span, home):
        home = home[...]
        if role == "pack":
            return home
        x = jnp.where(table[1] == 1, home, refs[0][0, span])
        if role == "relay":
            x = jnp.where(table[2] == 1, refs[1][span], x)
        if role == "quarter":
            got = jnp.where(table[3 + p] == 1, refs[1][0, span], refs[2][0, span])
            x = jnp.where(table[2] == 1, x, got)
        return x

    rows, side = value(slice(0, n), q), value(slice(n, n + kt.shape[0]), kt)
    if role == "far":
        for index, out in enumerate(outs):

            @pl.when(p == index)
            def _():
                out[:n] = rows
                out[n:] = side

    elif role == "quarter":
        piece, high = n // 2, kt.shape[0] // 2
        for i in range(2):
            span = slice(i * piece, (i + 1) * piece)
            outs[0][i, :piece] = rows[span]
            outs[0][i, piece:] = jnp.concatenate([side[:high, span], side[high:, span]], axis=1)
    else:
        outs[0][0, :n] = rows
        outs[0][0, n:] = side


def weight_block(role, table, q, kt, *more):
    width, side = q.shape[1], kt.shape[0]
    n = q.shape[0] // (4 * NY)
    rows = n + side
    pair = pl.BlockSpec((1, rows, width), lambda p, tab: (p, 0, 0))
    single = pl.BlockSpec((rows, width), lambda p, tab: (0, 0))
    ins = [
        pl.BlockSpec((n, width), lambda p, tab: (2 * tab[0] + p, 0)),
        pl.BlockSpec((side, width), lambda p, tab: (0, 2 * tab[0] + p)),
    ] + [pair if x.ndim == 3 else single for x in more]
    shape = lambda *dims: jax.ShapeDtypeStruct(dims, bf16)
    if role == "far":
        outs, shapes = [single, single], [shape(rows, width)] * 2
    elif role == "quarter":
        outs = pl.BlockSpec((2, rows // 2, width), lambda p, tab: (p, 0, 0))
        shapes = shape(4, rows // 2, width)
    else:
        outs, shapes = pair, shape(2, rows, width)
    return pl.pallas_call(
        functools.partial(block_body, role),
        grid_spec=pltpu.PrefetchScalarGridSpec(
            num_scalar_prefetch=1, grid=(2,), in_specs=ins, out_specs=outs
        ),
        out_shape=shapes,
        cost_estimate=pl.CostEstimate(
            flops=0, bytes_accessed=4 * rows * width * (2 + len(more)), transcendentals=0
        ),
        name="block_" + role,
    )(table.astype(jnp.int32), q, kt, *more)


def across(left, right):
    return lax.dot_general(left, right, (((0,), (0,)), ((), ())), preferred_element_type=f32)


def gram_body(table, *refs):
    ca, cb, r0a, r0b, r1a, r1b = (ref[...] for ref in refs[:6])
    low, high, base = refs[6:]
    slot = pl.program_id(0)
    half = NZ // 2
    ta, tb = ca.T, cb.T
    dot = functools.partial(jnp.dot, preferred_element_type=f32)
    tile = jnp.concatenate([dot(ta, r0a) + dot(tb, r0b), dot(ta, r1a) + dot(tb, r1b)], axis=1)

    @pl.when(slot < half)
    def _():
        low[0] = tile.astype(bf16)

    @pl.when((slot >= half) & (slot < NZ))
    def _():
        high[0] = tile.astype(bf16)

    @pl.when(slot >= NZ)
    def _():
        base[0] = tile


def gram(table, mine, other):
    tokens, depth = mine.shape
    n = table.shape[1]
    tile = depth // (NY * NZ * 2)
    half = NZ // 2
    at = lambda row: pl.BlockSpec((tokens, tile), lambda s, tab: (0, tab[row, s]))
    block = (1, tile, 2 * tile)
    shape = lambda n, kind: jax.ShapeDtypeStruct((n, tile, 2 * tile), kind)
    return pl.pallas_call(
        gram_body,
        grid_spec=pltpu.PrefetchScalarGridSpec(
            num_scalar_prefetch=1,
            grid=(n,),
            in_specs=[at(0), at(0), at(1), at(1), at(2), at(2)],
            out_specs=[
                pl.BlockSpec(block, lambda s, tab: (jnp.minimum(s, half - 1), 0, 0)),
                pl.BlockSpec(block, lambda s, tab: (jnp.clip(s - half, 0, half - 1), 0, 0)),
                pl.BlockSpec(block, lambda s, tab: (jnp.maximum(s - NZ, 0), 0, 0)),
            ],
        ),
        out_shape=[shape(half, bf16), shape(half, bf16), shape(n - NZ, f32)],
        cost_estimate=pl.CostEstimate(
            flops=8 * tokens * 2 * tile * tile * n,
            bytes_accessed=8 * n * tokens * tile * 2,
            transcendentals=0,
        ),
        name="gram",
    )(table, mine, other, mine, other, mine, other)


def project_body(slots, piece, fresh, table, *refs):
    out = refs[-1]
    ma, mb = refs[:slots], refs[slots : 2 * slots]
    left, right = [], []
    for w in refs[2 * slots : -1 if fresh else -2]:
        if w.shape[2] == piece:
            side = left if len(left) == len(right) else right
            side += [w[i] for i in range(w.shape[0])]
        else:
            left += [w[i, :, :piece] for i in range(w.shape[0])]
            right += [w[i, :, piece:] for i in range(w.shape[0])]
    spans = [slice(0, piece), slice(piece, 2 * piece), slice(2 * piece, 2 * piece + HEAD)]
    for core, tokens in ((0, ma), (1, mb)):
        sums = [0.0 if fresh else refs[-2][core, :, span] for span in spans]
        for x, w0, w1 in zip(tokens, left, right):
            x = x[...]
            kt = [w0[piece:], w1[piece:]]
            kt = jnp.concatenate(kt * (HEAD // (2 * kt[0].shape[0])), axis=0)
            sums[0] += jnp.dot(x, w0[:piece], preferred_element_type=f32)
            sums[1] += jnp.dot(x, w1[:piece], preferred_element_type=f32)
            sums[2] += lax.dot_general(x, kt, (((1,), (1,)), ((), ())), preferred_element_type=f32)
        for span, value in zip(spans, sums):
            out[core, :, span] = value


def project(piece, table, mine, other, weights, sofar=None):
    tokens = mine.shape[0]
    slots = table.shape[0]
    at = [pl.BlockSpec((tokens, piece), lambda s, tab, n=n: (0, tab[n])) for n in range(slots)]
    full = lambda shape: pl.BlockSpec(shape, lambda s, tab: (0, 0, 0))
    whole = (2, tokens, 2 * piece + HEAD)
    fresh = sofar is None
    return pl.pallas_call(
        functools.partial(project_body, slots, piece, fresh),
        grid_spec=pltpu.PrefetchScalarGridSpec(
            num_scalar_prefetch=1,
            grid=(1,),
            in_specs=at + at + [full(w.shape) for w in weights] + ([] if fresh else [full(whole)]),
            out_specs=full(whole),
        ),
        out_shape=jax.ShapeDtypeStruct(whole, f32),
        cost_estimate=pl.CostEstimate(
            flops=8 * tokens * piece * piece * slots,
            bytes_accessed=slots * 8 * tokens * piece + 8 * tokens * piece,
            transcendentals=0,
        ),
        name="project",
    )(table, *[mine] * slots, *[other] * slots, *weights, *([] if fresh else [sofar]))


def rope_body(at, a, b, cosine, sine, queries, keys):
    even = lax.broadcasted_iota(jnp.int32, cosine.shape, 1) % 2 == 0
    width, part = queries.shape[1], keys.shape[0]
    for start in range(0, width + HEAD, HEAD):
        x = a[0, :, start : start + HEAD] + b[:, start : start + HEAD]
        swapped = jnp.where(even, pltpu.roll(x, HEAD - 1, 1), pltpu.roll(x, 1, 1))
        x = x * cosine[...] + swapped * sine[...]
        if start < width:
            queries[:, start : start + HEAD] = x.astype(bf16)
        else:
            x = x.T
            chosen = x[:part]
            for n in range(1, HEAD // part):
                chosen = jnp.where(at[0] == n, x[n * part : (n + 1) * part], chosen)
            keys[...] = chosen.astype(bf16)


def rope(at, part, a, b, cosine, sine):
    tokens, width = b.shape
    full = lambda shape: pl.BlockSpec(shape, lambda i: (0,) * len(shape))
    shapes = [(tokens, width - HEAD), (part, tokens)]
    return pl.pallas_call(
        rope_body,
        grid=(1,),
        in_specs=[pl.BlockSpec(memory_space=pltpu.SMEM), full((1, tokens, width))]
        + [full(x.shape) for x in (b, cosine, sine)],
        out_specs=[full(shape) for shape in shapes],
        out_shape=[jax.ShapeDtypeStruct(shape, bf16) for shape in shapes],
        name="rope",
    )(at, a, b, cosine, sine)


def assemble_body(scale, slots, own, r0, r1, extra, out):
    tile = out.shape[1]

    def put(n, value):
        out[pl.ds(pl.multiple_of(slots[n] * tile, tile), tile), :] = value * scale

    put(0, r1[...].astype(f32))
    put(1, extra[...])
    put(2, r0[...].astype(f32))
    put(3, own[:, :tile].T)
    put(4, own[:, tile:].T)


def assemble(scale, slots, own, r0, r1, extra):
    tile = own.shape[0]
    return pl.pallas_call(
        functools.partial(assemble_body, scale),
        in_specs=[pl.BlockSpec(memory_space=pltpu.SMEM)] + [pl.BlockSpec(memory_space=pltpu.VMEM)] * 4,
        out_shape=jax.ShapeDtypeStruct((4 * tile, tile), f32),
        name="assemble",
    )(slots, own, r0, r1, extra)


def row_pair(t, c):
    u, m = t // 4, t % 4
    p = (t + (c > u)) % 2
    return jnp.where(c == u, m, p), jnp.where(c == u, (m + 1) % 4, p + 2)


def partner_moves(q):
    moves = []
    for t in range(NY * NZ * 2):
        for c in range(NC):
            u, m = t // 4, t % 4
            if c == u:
                r = (m + 1) % 4 if q == 0 else m
            else:
                r = (t + (c > u)) % 2 + 2 * ((q + m // 2) % 2)
            moves.append((t * NC + c, (4 * c + r) * NC + u))
    return moves


def shards(hidden, norm_gain, token_ids, owner, query_store, key_store):
    y, z, k = lax.axis_index("y"), lax.axis_index("zl"), lax.axis_index("k")
    column = lax.axis_index("x") * 2 + lax.axis_index("zh")
    root = owner[0]
    root_z, root_y, root_k = root // 8, (root // 2) % 4, root % 2

    tokens, depth = hidden.shape
    half = depth // 2
    piece = half // (NY * NZ)
    qwidth, kwidth = query_store.shape[2], key_store.shape[2]
    h = NZ // 2
    here = root_k == k

    q = query_store[0]
    kt = key_store[0].T
    one = jnp.int32(1)

    def chip(rel):
        return (y + rel) % NY

    def told(rel, *flags):
        return jnp.stack([k * NY + chip(rel), *[x * one for x in flags]])

    def pack(k, rel):
        return weight_block("pack", jnp.stack([(1 - k) * NY + chip(rel)]), q, kt)

    step_y = (y - root_y) % NY
    far0, far1 = weight_block("far", told(2, here), q, kt, send(pack(k, 2), "k", 1))
    far0, far1, later_k = together((far0, far1, k))
    a = send(far0, "y", 1)
    b = send(far1, "y", -1)
    others = [pack(later_k, rel) for rel in (1, 3)]
    others, later_hidden, last_k = together((others, hidden, later_k))
    others = [send(x, "k", 1) for x in others]
    theirs = send(later_hidden, "k", 1)
    others.append(send(pack(last_k, 0), "k", 1))
    up = weight_block("relay", told(1, here, step_y == 1), q, kt, others[0], a)
    down = weight_block("relay", told(3, here, step_y == 3), q, kt, others[1], b)
    up, down, gain = together((up, down, norm_gain))
    c = send(up, "y", 1)
    d = send(down, "y", -1)

    mine = normalize(hidden, gain)
    other = normalize(theirs, gain)

    zs = (z + jnp.arange(NZ)) % NZ
    t = (zs[None] * (2 * NY) + chip(jnp.array([2, 1, 3, 0])[:, None]) * 2 + k).reshape(-1)
    r0, r1 = row_pair(t, column)
    table = jnp.stack([t, 4 * column + r0, 4 * column + r1]).astype(jnp.int32)
    p_low, p_high, base = gram(table, mine, other)

    tile = depth // (NY * NZ * 2)
    both = [lax.dynamic_slice_in_dim(x, (4 * column + k) * tile, 3 * tile, 1) for x in (mine, other)]
    extra = sum(across(x[:, :tile], x[:, 2 * tile :]) for x in both)

    def butterfly(extra, axis, bit):
        return extra + swap(extra.astype(bf16), axis, bit).astype(f32)

    extra = butterfly(butterfly(extra, "zl", 1), "zl", 2)
    p_low, p_high, base, extra, step_y = together((p_low, p_high, base, extra, step_y))
    flags = told(0, here, step_y == 0, (step_y == 1) | (step_y == 2), step_y == 1)
    quarter = weight_block("quarter", flags, q, kt, others[2], c, d)
    p_low, p_high, quarter = together((p_low, p_high, quarter))

    ga = send(p_low, "y", 1)
    gb = send(p_high, "y", -1)
    quarter = quarter.reshape(2, h, *quarter.shape[1:])
    kept = swap(pick(quarter, 1 - z % 2), "zl", 1)
    first = lax.broadcasted_iota(jnp.int32, (2, 1, 1, 1), 0) == 0
    shape = (2, h, tile, 2 * tile)
    up = base[:NZ].reshape(shape) + jnp.where(first, ga.astype(f32)[None], 0.0)
    down = base[NZ : 2 * NZ].reshape(shape) + jnp.where(first, 0.0, gb.astype(f32)[None])
    kept = jnp.where(z == root_z, pick(quarter, z % 2), kept)
    up, down, kept = together((up.astype(bf16), down.astype(bf16), kept))
    gc = send(up, "y", 1).reshape(NZ, tile, 2 * tile)
    gd = send(down, "y", -1).reshape(NZ, tile, 2 * tile)
    kept = jnp.where(z // 2 == root_z // 2, kept, swap(kept, "zl", 2))
    total = [base[2 * NZ + s] + gc[s].astype(f32) + gd[s].astype(f32) for s in range(NZ)]
    hess, rest = total[0], [x.astype(bf16) for x in total[1:]]
    kept, hess, rest, extra = together((kept, hess, rest, extra))
    strip = jnp.concatenate([kept, swap(kept, "zl", 1)], axis=0)
    extra = butterfly(butterfly(extra, "y", 1), "y", 2)
    strip, extra, rest = together((strip, extra, rest))

    pairs = jnp.concatenate([2 * (z % 2) + jnp.arange(2), 2 * (1 - z % 2) + jnp.arange(2)])

    def depth_tiles(rel):
        return (k * NY * NZ + chip(rel) * NZ + pairs).astype(jnp.int32)

    product = functools.partial(project, piece)
    left, right = send(strip, "y", 1), send(strip, "y", -1)
    parts = [send(rest[s - 1], "zl", s) for s in (1, 2, 3)]
    raw = product(depth_tiles(0), mine, other, [strip])
    cosine, sine = turns(positions(token_ids))
    left, right, parts, raw, cosine, sine = together((left, right, parts, raw, cosine, sine))
    fl, fr = send(left[:h], "y", 1), send(right[h:], "y", -1)

    for x in parts:
        hess = hess + x.astype(f32)
    t = z * (2 * NY) + y * 2 + k
    u, m = t // 4, t % 4
    diagonal = column == u
    r0, r1 = row_pair(t, column)
    tiles = hess.astype(bf16)
    tiles = [tiles[:, :tile], tiles[:, tile:]]
    mirrored = []
    for n in (0, 1):
        second = jnp.where(diagonal, 1, (n + m // 2) % 2) == 1
        mirrored.append(lax.ppermute(jnp.where(second, tiles[1], tiles[0]), ALL, partner_moves(n)))
    missing = 1 - r0 % 2
    slot0 = jnp.where(diagonal, (m + 3) % 4, missing + 2 * ((m // 2) % 2))
    slot1 = jnp.where(diagonal, (m + 2) % 4, missing + 2 * ((m // 2 + 1) % 2))
    slots = jnp.stack([slot1, jnp.where(diagonal, slot1, r0), slot0, r0, r1]).astype(jnp.int32)
    extra = jnp.where(m < 2, extra.T, extra)

    sides = jnp.concatenate([depth_tiles(3), depth_tiles(1)])
    raw = product(sides, mine, other, [left, right], raw)
    mirrored, raw = together((mirrored, raw))
    raw = product(depth_tiles(2), mine, other, [fl, fr], raw)
    all_tokens = tokens * NY * NZ * 2
    hessian = assemble(2.0 / all_tokens, slots, hess, mirrored[0], mirrored[1], extra)
    at = ((column * kwidth) % HEAD) // kwidth
    queries, keys = rope(at.reshape(1), kwidth, raw, send(raw[1], "k", 1), cosine, sine)
    return (queries, keys.T, hessian)


def solution(mesh):
    fine = Mesh(mesh.devices.reshape(NZ, NY, 2, 4, 2), ALL)
    placed = (P(TOK, None), P(), P(TOK), P(), P(TOK, None, COL), P(TOK, None, COL))
    return jax.shard_map(
        shards,
        mesh=fine,
        in_specs=placed,
        out_specs=(P(TOK, COL), P(TOK, COL), P(COL, TOK)),
        check_vma=False,
    )
```

profile of v0, /device:TPU:29, one launch (start us, length us, event | category | flops | bytes accessed | tf_op | source)
XLA Modules:
  0.0 234.9 jit_solution(8869181682520364801)
XLA Ops:
  0.6 2.2 block_pack.4
  4.9 1.3 collective-permute-done.refs_0_
  7.3 3.4 %block_far.1 = (bf16[576,512]{1,0:T(8,128)(2,1)}, bf16[576,512]{1,0:T(8,128)(2,1)}) custom-call(s32[2]{0:T(128)} %pad_add_fusion.3.table, bf16[8192,512]{1,0:T(8,128)(2,1)} %bitcast.56, bf16[64,8192]{1,0:T(8,128)(2,1)} %bitcast.64, bf16[2,576,512]{2,1,0:T(8,128)(2,1)} %copy-done.11), custom_call_target="tpu_custom_call" | custom-call | bytes 3538944 | tf_op jit(solution)/shard_map/block_far/pallas_call | solution.py:139
  10.7 2.1 block_pack.6
  12.8 2.2 block_pack.5
  16.4 2.2 collective-permute-start.2
  19.6 2.1 block_pack.7
  21.7 10.6 %collective-permute-done.4.refs_1_ = bf16[576,512]{1,0:T(8,128)(2,1)} collective-permute-done((bf16[576,512]{1,0:T(8,128)(2,1)}, bf16[576,512]{1,0:T(8,128)(2,1)}, u32[]{:S(2)}, u32[]{:S(2)}) %collective-permute-start.4) | collective-permute-done | bytes 589856 | tf_op jit(solution)/shard_map/ppermute | solution.py:27
  34.3 3.4 %block_relay.3 = bf16[2,576,512]{2,1,0:T(8,128)(2,1)} custom-call(s32[3]{0:T(128)} %get-tuple-element.132.table, bf16[8192,512]{1,0:T(8,128)(2,1)} %bitcast.60, bf16[64,8192]{1,0:T(8,128)(2,1)} %bitcast.68, bf16[2,576,512]{2,1,0:T(8,128)(2,1)} %copy-done.7, bf16[576,512]{1,0:T(8,128)(2,1)} %collective-permute-done.4.refs_1_), custom_call_target="tpu_custom_call" | custom-call | bytes 4718592 | tf_op jit(solution)/shard_map/block_relay/pallas_call | solution.py:139
  38.7 3.5 %block_relay.2 = bf16[2,576,512]{2,1,0:T(8,128)(2,1)} custom-call(s32[3]{0:T(128)} %get-tuple-element.131.table, bf16[8192,512]{1,0:T(8,128)(2,1)} %bitcast.61, bf16[64,8192]{1,0:T(8,128)(2,1)} %bitcast.69, bf16[2,576,512]{2,1,0:T(8,128)(2,1)} %copy-done.6, bf16[576,512]{1,0:T(8,128)(2,1)} %collective-permute-done.2.refs_1_), custom_call_target="tpu_custom_call" | custom-call | bytes 4718592 | tf_op jit(solution)/shard_map/block_relay/pallas_call | solution.py:139
  42.2 2.7 %collective-permute-start.9 = (bf16[2,576,512]{2,1,0:T(8,128)(2,1)}, bf16[2,576,512]{2,1,0:T(8,128)(2,1)}, u32[]{:S(2)}, u32[]{:S(2)}) collective-permute-start(bf16[2,576,512]{2,1,0:T(8,128)(2,1)} %block_relay.2), channel_id=1, source_target_pairs={{0,16},{16,32},{32,48},{48,0},{1,17},{17,33},{33,49},{49,1},{2,18}... | collective-permute-start | bytes 3538952 | tf_op jit(solution)/shard_map/ppermute | solution.py:27
  44.9 7.6 %normalize.2.refs_0_.refs_2_.refs_4_.refs_1_.refs_3_.refs_5_.refs_6_.refs_7_ = bf16[256,8192]{1,0:T(8,128)(2,1)} custom-call(bf16[256,8192]{1,0:T(8,128)(2,1)} %x.1, f32[1,8192]{1,0:T(1,128)} %bitcast.76), custom_call_target="tpu_custom_call" | custom-call | flops 10485760 | bytes 8388608 | tf_op jit(solution)/shard_map/normalize/pallas_call | solution.py:68
  52.5 1.2 fusion.8
  53.7 7.6 %normalize.3.refs_1_.refs_3_.refs_5_.refs_4_.refs_6_.refs_7_.refs_8_.refs_9_.refs_10_.refs_11_.refs_12_.refs_13_.refs_14_.refs_15_ = bf16[256,8192]{1,0:T(8,128)(2,1)} custom-call(bf16[256,8192]{1,0:T(8,128)(2,1)} %collective-permute-done.5.x, f32[1,8192]{1,0:T(1,128)} %bitcast.77), custom_call_target="tpu_custom_call" | custom-call | flops 10485760 | bytes 8388608 | tf_op jit(solution)/shard_map/normalize/pallas_call | solution.py:68
  61.3 1.2 fusion.27
  62.5 1.7 collective-permute-start.6
  64.9 2.7 %collective-permute-done.6 = bf16[256,256]{1,0:T(8,128)(2,1)S(1)} collective-permute-done((bf16[256,256]{1,0:T(8,128)(2,1)S(1)}, bf16[256,256]{1,0:T(8,128)(2,1)S(1)}, u32[]{:S(2)}, u32[]{:S(2)}) %collective-permute-start.6) | collective-permute-done | bytes 131104 | tf_op jit(solution)/shard_map/ppermute | solution.py:31
  67.6 3.1 %collective-permute-start.7 = (bf16[256,256]{1,0:T(8,128)(2,1)S(1)}, bf16[256,256]{1,0:T(8,128)(2,1)S(1)}, u32[]{:S(2)}, u32[]{:S(2)}) collective-permute-start(bf16[256,256]{1,0:T(8,128)(2,1)S(1)} %fusion.3), channel_id=1, source_target_pairs={{0,128},{64,192},{128,0},{192,64},{1,129},{65,193},{129,1},{193,65... | collective-permute-start | bytes 393224 | tf_op jit(solution)/shard_map/ppermute | solution.py:31
  70.7 15.9 %gram.1 = (bf16[2,256,512]{2,1,0:T(8,128)(2,1)}, bf16[2,256,512]{2,1,0:T(8,128)(2,1)}, f32[12,256,512]{2,1,0:T(8,128)}) custom-call(s32[3,16]{1,0:T(4,128)} %pad_add_fusion.table, bf16[256,8192]{1,0:T(8,128)(2,1)} %normalize.2.refs_0_.refs_2_.refs_4_.refs_1_.refs_3_.refs_5_.refs_6_.refs_7_, ...), custom_call_target="tpu_custom_call" | custom-call | flops 4294967296 | bytes 16777216 | tf_op jit(solution)/shard_map/gram/pallas_call | solution.py:186
  88.3 3.9 %block_quarter.1 = bf16[4,288,512]{2,1,0:T(8,128)(2,1)} custom-call(s32[5]{0:T(128)} %stack.121.table, bf16[8192,512]{1,0:T(8,128)(2,1)} %bitcast.62, bf16[64,8192]{1,0:T(8,128)(2,1)} %bitcast.70, bf16[2,576,512]{2,1,0:T(8,128)(2,1)} %collective-permute-done.8.refs_0_, bf16[2,576,512]{2,1,0:T(8,128)(2,1)} %collective-permute-done.9.refs_1_, ...), custom_call_target="tpu_custom_call" | custom-call | bytes 5898240 | tf_op jit(solution)/shard_map/block_quarter/pallas_call | solution.py:139
  94.8 1.5 collective-permute-start.13
  96.3 2.7 %fusion.26 = (f32[4,256,512]{2,1,0:T(8,128)S(1)}, f32[4,256,512]{2,1,0:T(8,128)S(1)}) fusion(f32[12,256,512]{2,1,0:T(8,128)} %get-tuple-element.65), kind=kLoop, calls=%fused_computation.92 | loop fusion | bytes 8388608 | tf_op jit(solution)/shard_map/slice | solution.py:403
  99.0 5.5 %collective-permute-done.11 = bf16[2,256,512]{2,1,0:T(8,128)(2,1)S(1)} collective-permute-done((bf16[2,256,512]{2,1,0:T(8,128)(2,1)}, bf16[2,256,512]{2,1,0:T(8,128)(2,1)S(1)}, u32[]{:S(2)}, u32[]{:S(2)}) %collective-permute-start.11) | collective-permute-done | bytes 524320 | tf_op jit(solution)/shard_map/ppermute | solution.py:27
  104.6 1.7 collective-permute-done.12
  106.4 1.9 add_convert_fusion
  108.5 1.8 collective-permute-start.15
  110.2 28.5 %collective-permute-done.14 = bf16[2,288,512]{2,1,0:T(8,128)(2,1)S(1)} collective-permute-done((bf16[2,288,512]{2,1,0:T(8,128)(2,1)S(1)}, bf16[2,288,512]{2,1,0:T(8,128)(2,1)S(1)}, u32[]{:S(2)}, u32[]{:S(2)}) %collective-permute-start.14) | collective-permute-done | bytes 589856 | tf_op jit(solution)/shard_map/ppermute | solution.py:31
  138.8 3.5 %fusion.2 = (bf16[256,512]{1,0:T(8,128)(2,1)}, bf16[256,512]{1,0:T(8,128)(2,1)}, bf16[256,512]{1,0:T(8,128)(2,1)}, f32[256,512]{1,0:T(8,128)}) fusion(f32[12,256,512]{2,1,0:T(8,128)} %get-tuple-element.65, bf16[4,256,512]{2,1,0:T(8,128)(2,1)} %bitcast.27, bf16[4,256,512]{2,1,0:T(8,128)(2,1)} %bitcast.26), kind=kLoop, calls=%fused_computation.15 | loop fusion | flops 2490368 | bytes 5505024 | tf_op jit(solution)/shard_map/convert_element_type | solution.py:410
  143.0 3.6 %collective-permute-done.18 = bf16[256,256]{1,0:T(8,128)(2,1)S(1)} collective-permute-done((bf16[256,256]{1,0:T(8,128)(2,1)S(1)}, bf16[256,256]{1,0:T(8,128)(2,1)S(1)}, u32[]{:S(2)}, u32[]{:S(2)}) %collective-permute-start.18) | collective-permute-done | bytes 131104 | tf_op jit(solution)/shard_map/ppermute | solution.py:31
  146.6 2.8 %collective-permute-start.19 = (bf16[256,256]{1,0:T(8,128)(2,1)S(1)}, bf16[256,256]{1,0:T(8,128)(2,1)S(1)}, u32[]{:S(2)}, u32[]{:S(2)}) collective-permute-start(bf16[256,256]{1,0:T(8,128)(2,1)S(1)} %fusion.4), channel_id=1, source_target_pairs={{0,32},{16,48},{32,0},{48,16},{1,33},{17,49},{33,1},{49,17},{2,34}... | collective-permute-start | bytes 393224 | tf_op jit(solution)/shard_map/ppermute | solution.py:31
  149.5 2.6 %collective-permute-done.19 = bf16[256,256]{1,0:T(8,128)(2,1)S(1)} collective-permute-done((bf16[256,256]{1,0:T(8,128)(2,1)S(1)}, bf16[256,256]{1,0:T(8,128)(2,1)S(1)}, u32[]{:S(2)}, u32[]{:S(2)}) %collective-permute-start.19) | collective-permute-done | bytes 131104 | tf_op jit(solution)/shard_map/ppermute | solution.py:31
  152.8 4.2 %collective-permute-done.17 = bf16[2,288,512]{2,1,0:T(8,128)(2,1)S(1)} collective-permute-done((bf16[2,288,512]{2,1,0:T(8,128)(2,1)S(1)}, bf16[2,288,512]{2,1,0:T(8,128)(2,1)S(1)}, u32[]{:S(2)}, u32[]{:S(2)}) %collective-permute-start.17) | collective-permute-done | bytes 589856 | tf_op jit(solution)/shard_map/ppermute | solution.py:31
  157.1 2.8 %collective-permute-start.20 = (bf16[4,288,512]{2,1,0:T(8,128)(2,1)S(1)}, bf16[4,288,512]{2,1,0:T(8,128)(2,1)S(1)}, u32[]{:S(2)}, u32[]{:S(2)}) collective-permute-start(bf16[4,288,512]{2,1,0:T(8,128)(2,1)S(1)} %pad_maximum_fusion.refs_8_), channel_id=1, source_target_pairs={{0,16},{16,32},{32,48},{48,0},{1,17},{17,33},{33,49},{49,1},{2,18}... | collective-permute-start | bytes 3538952 | tf_op jit(solution)/shard_map/ppermute | solution.py:27
  160.6 1.3 fusion.5
  163.0 2.1 collective-permute-start.24
  165.7 4.5 %project.3.refs_18_ = f32[2,256,640]{2,1,0:T(8,128)} custom-call(s32[4]{0:T(128)} %get-tuple-element.121.table, bf16[256,8192]{1,0:T(8,128)(2,1)} %normalize.2.refs_0_.refs_2_.refs_4_.refs_1_.refs_3_.refs_5_.refs_6_.refs_7_, bf16[256,8192]{1,0:T(8,128)(2,1)} %normalize.2.refs_0_.refs_2_.refs_4_.refs_1_.refs_3_.refs_5_.refs_6_.refs_7_, ...), custom_call_target="tpu_custom_call" | custom-call | flops 536870912 | bytes 2621440 | tf_op jit(solution)/shard_map/project/pallas_call | solution.py:240
  170.2 12.1 %collective-permute-done.23 = bf16[256,512]{1,0:T(8,128)(2,1)} collective-permute-done((bf16[256,512]{1,0:T(8,128)(2,1)}, bf16[256,512]{1,0:T(8,128)(2,1)}, u32[]{:S(2)}, u32[]{:S(2)}) %collective-permute-start.23) | collective-permute-done | bytes 262176 | tf_op jit(solution)/shard_map/ppermute | solution.py:27
  182.3 1.2 collective-permute-done.20.refs_16_
  183.4 3.1 %collective-permute-done.21.refs_17_ = bf16[4,288,512]{2,1,0:T(8,128)(2,1)S(1)} collective-permute-done((bf16[4,288,512]{2,1,0:T(8,128)(2,1)S(1)}, bf16[4,288,512]{2,1,0:T(8,128)(2,1)S(1)}, u32[]{:S(2)}, u32[]{:S(2)}) %collective-permute-start.21) | collective-permute-done | bytes 1179680 | tf_op jit(solution)/shard_map/ppermute | solution.py:27
  187.0 1.5 collective-permute-start.26
  188.5 2.0 fusion.25
  190.6 5.5 %collective-permute-start.27 = (bf16[256,256]{1,0:T(8,128)(2,1)S(1)}, bf16[256,256]{1,0:T(8,128)(2,1)S(1)}, u32[]{:S(2)}, u32[]{:S(2)}) collective-permute-start(bf16[256,256]{1,0:T(8,128)(2,1)S(1)} %get-tuple-element.117), channel_id=1, source_target_pairs={{0,8},{1,40},{2,72},{3,104},{4,136},{5,168},{6,200},{7,232},{8,16}... | collective-permute-start | bytes 393224 | tf_op jit(solution)/shard_map/ppermute | solution.py:440
  196.1 7.6 %collective-permute-start.28 = (bf16[256,256]{1,0:T(8,128)(2,1)S(1)}, bf16[256,256]{1,0:T(8,128)(2,1)S(1)}, u32[]{:S(2)}, u32[]{:S(2)}) collective-permute-start(bf16[256,256]{1,0:T(8,128)(2,1)S(1)} %get-tuple-element.116), channel_id=1, source_target_pairs={{0,0},{1,56},{2,88},{3,120},{4,152},{5,184},{6,216},{7,248},{8,8},... | collective-permute-start | bytes 393224 | tf_op jit(solution)/shard_map/ppermute | solution.py:440
  204.3 6.3 %project.4.refs_10_ = f32[2,256,640]{2,1,0:T(8,128)} custom-call(s32[8]{0:T(128)} %pad_add_fusion.5.table, bf16[256,8192]{1,0:T(8,128)(2,1)} %normalize.2.refs_0_.refs_2_.refs_4_.refs_1_.refs_3_.refs_5_.refs_6_.refs_7_, bf16[256,8192]{1,0:T(8,128)(2,1)} %normalize.2.refs_0_.refs_2_.refs_4_.refs_1_.refs_3_.refs_5_.refs_6_.refs_7_, ...), custom_call_target="tpu_custom_call" | custom-call | flops 1073741824 | bytes 4718592 | tf_op jit(solution)/shard_map/project/pallas_call | solution.py:240
  210.7 10.0 %collective-permute-done.28.r1 = bf16[256,256]{1,0:T(8,128)(2,1)S(1)} collective-permute-done((bf16[256,256]{1,0:T(8,128)(2,1)S(1)}, bf16[256,256]{1,0:T(8,128)(2,1)S(1)}, u32[]{:S(2)}, u32[]{:S(2)}) %collective-permute-start.28) | collective-permute-done | bytes 131104 | tf_op jit(solution)/shard_map/ppermute | solution.py:440
  220.7 5.0 %project.5.a = f32[2,256,640]{2,1,0:T(8,128)} custom-call(s32[4]{0:T(128)} %get-tuple-element.122.table, bf16[256,8192]{1,0:T(8,128)(2,1)} %normalize.2.refs_0_.refs_2_.refs_4_.refs_1_.refs_3_.refs_5_.refs_6_.refs_7_, bf16[256,8192]{1,0:T(8,128)(2,1)} %normalize.2.refs_0_.refs_2_.refs_4_.refs_1_.refs_3_.refs_5_.refs_6_.refs_7_, ...), custom_call_target="tpu_custom_call" | custom-call | flops 536870912 | bytes 2621440 | tf_op jit(solution)/shard_map/project/pallas_call | solution.py:240
  229.3 2.4 %assemble.1 = f32[1024,256]{1,0:T(8,128)} custom-call(s32[5]{0:T(128)} %stack.128.slots, f32[256,512]{1,0:T(8,128)} %get-tuple-element.106.own, bf16[256,256]{1,0:T(8,128)(2,1)} %copy-done.13, bf16[256,256]{1,0:T(8,128)(2,1)} %copy-done.14, f32[256,256]{1,0:T(8,128)} %broadcast_select_fusion.1.extra), custom_call_target="tpu_custom_call" | custom-call | tf_op jit(solution)/shard_map/assemble/pallas_call | solution.py:305
  232.5 2.4 %rope.1 = (bf16[256,512]{1,0:T(8,128)(2,1)}, bf16[64,256]{1,0:T(8,128)(2,1)}) custom-call(s32[1]{0:T(128)} %bitcast.at, f32[2,256,640]{2,1,0:T(8,128)} %project.5.a, f32[256,640]{1,0:T(8,128)} %copy-done.12, f32[256,128]{1,0:T(8,128)} %get-tuple-element.96.cosine, f32[256,128]{1,0:T(8,128)} %get-tuple-element.97.sine), custom_call_target="tpu_custom_call" | custom-call | tf_op jit(solution)/shard_map/rope/pallas_call | solution.py:279
  (110 shorter events, 22.5 us)
Async XLA Ops:
  2.8 3.4 %collective-permute-start = (bf16[2,576,512]{2,1,0:T(8,128)(2,1)}, bf16[2,576,512]{2,1,0:T(8,128)(2,1)S(1)}, u32[]{:S(2)}, u32[]{:S(2)}) collective-permute-start(bf16[2,576,512]{2,1,0:T(8,128)(2,1)} %block_pack.4), channel_id=1, source_target_pairs={{0,8},{8,0},{1,9},{9,1},{2,10},{10,2},{3,11},{11,3},{4,12},{12,4},... | collective-permute-start | bytes 3538952 | tf_op jit(solution)/shard_map/ppermute | solution.py:27
  6.2 1.1 copy-start.11
  12.8 2.6 %copy-start.9 = (bf16[2,576,512]{2,1,0:T(8,128)(2,1)S(1)}, bf16[2,576,512]{2,1,0:T(8,128)(2,1)}, u32[]{:S(2)}) copy-start(bf16[2,576,512]{2,1,0:T(8,128)(2,1)} %block_pack.6) | copy-start | bytes 3538948
  12.8 5.8 %copy-start.17 = (s32[4]{0:T(128)S(1)}, s32[4]{0:T(128)}, u32[]{:S(2)}) copy-start(s32[4]{0:T(128)} %constant.311.clone) | copy-start | bytes 52
  15.0 38.7 %collective-permute-start.5 = (bf16[256,8192]{1,0:T(8,128)(2,1)}, bf16[256,8192]{1,0:T(8,128)(2,1)}, u32[]{:S(2)}, u32[]{:S(2)}) collective-permute-start(bf16[256,8192]{1,0:T(8,128)(2,1)} %x.1), channel_id=1, source_target_pairs={{0,8},{8,0},{1,9},{9,1},{2,10},{10,2},{3,11},{11,3},{4,12},{12,4},... | collective-permute-start | bytes 12582920 | tf_op jit(solution)/shard_map/ppermute | solution.py:27
  15.4 17.8 %collective-permute-start.3 = (bf16[2,576,512]{2,1,0:T(8,128)(2,1)S(1)}, bf16[2,576,512]{2,1,0:T(8,128)(2,1)S(1)}, u32[]{:S(2)}, u32[]{:S(2)}) collective-permute-start(bf16[2,576,512]{2,1,0:T(8,128)(2,1)S(1)} %copy-done.9), channel_id=1, source_target_pairs={{0,8},{8,0},{1,9},{9,1},{2,10},{10,2},{3,11},{11,3},{4,12},{12,4},... | collective-permute-start | bytes 3538952 | tf_op jit(solution)/shard_map/ppermute | solution.py:27
  15.6 22.1 %collective-permute-start.1 = (bf16[2,576,512]{2,1,0:T(8,128)(2,1)}, bf16[2,576,512]{2,1,0:T(8,128)(2,1)S(1)}, u32[]{:S(2)}, u32[]{:S(2)}) collective-permute-start(bf16[2,576,512]{2,1,0:T(8,128)(2,1)} %block_pack.5), channel_id=1, source_target_pairs={{0,8},{8,0},{1,9},{9,1},{2,10},{10,2},{3,11},{11,3},{4,12},{12,4},... | collective-permute-start | bytes 3538952 | tf_op jit(solution)/shard_map/ppermute | solution.py:27
  15.9 16.3 %collective-permute-start.4 = (bf16[576,512]{1,0:T(8,128)(2,1)}, bf16[576,512]{1,0:T(8,128)(2,1)}, u32[]{:S(2)}, u32[]{:S(2)}) collective-permute-start(bf16[576,512]{1,0:T(8,128)(2,1)} %get-tuple-element.59), channel_id=1, source_target_pairs={{0,48},{16,0},{32,16},{48,32},{1,49},{17,1},{33,17},{49,33},{2,50}... | collective-permute-start | bytes 1769480 | tf_op jit(solution)/shard_map/ppermute | solution.py:27
  16.4 21.3 %collective-permute-start.2 = (bf16[576,512]{1,0:T(8,128)(2,1)}, bf16[576,512]{1,0:T(8,128)(2,1)}, u32[]{:S(2)}, u32[]{:S(2)}) collective-permute-start(bf16[576,512]{1,0:T(8,128)(2,1)} %get-tuple-element.57), channel_id=1, source_target_pairs={{0,16},{16,32},{32,48},{48,0},{1,17},{17,33},{33,49},{49,1},{2,18}... | collective-permute-start | bytes 1769480 | tf_op jit(solution)/shard_map/ppermute | solution.py:27
  32.2 55.0 %collective-permute-start.8 = (bf16[2,576,512]{2,1,0:T(8,128)(2,1)}, bf16[2,576,512]{2,1,0:T(8,128)(2,1)}, u32[]{:S(2)}, u32[]{:S(2)}) collective-permute-start(bf16[2,576,512]{2,1,0:T(8,128)(2,1)} %block_pack.7), channel_id=1, source_target_pairs={{0,8},{8,0},{1,9},{9,1},{2,10},{10,2},{3,11},{11,3},{4,12},{12,4},... | collective-permute-start | bytes 3538952 | tf_op jit(solution)/shard_map/ppermute | solution.py:27
  33.2 1.1 copy-start.7
  37.7 1.1 copy-start.6
  38.7 3.5 %copy-start.8 = (bf16[2,576,512]{2,1,0:T(8,128)(2,1)S(1)}, bf16[2,576,512]{2,1,0:T(8,128)(2,1)}, u32[]{:S(2)}) copy-start(bf16[2,576,512]{2,1,0:T(8,128)(2,1)} %block_relay.3) | copy-start | bytes 3538948
  42.2 45.0 %collective-permute-start.10 = (bf16[2,576,512]{2,1,0:T(8,128)(2,1)S(1)}, bf16[2,576,512]{2,1,0:T(8,128)(2,1)S(1)}, u32[]{:S(2)}, u32[]{:S(2)}) collective-permute-start(bf16[2,576,512]{2,1,0:T(8,128)(2,1)S(1)} %copy-done.8), channel_id=1, source_target_pairs={{0,48},{16,0},{32,16},{48,32},{1,49},{17,1},{33,17},{49,33},{2,50}... | collective-permute-start | bytes 3538952 | tf_op jit(solution)/shard_map/ppermute | solution.py:27
  42.2 45.0 %collective-permute-start.9 = (bf16[2,576,512]{2,1,0:T(8,128)(2,1)}, bf16[2,576,512]{2,1,0:T(8,128)(2,1)}, u32[]{:S(2)}, u32[]{:S(2)}) collective-permute-start(bf16[2,576,512]{2,1,0:T(8,128)(2,1)} %block_relay.2), channel_id=1, source_target_pairs={{0,16},{16,32},{32,48},{48,0},{1,17},{17,33},{33,49},{49,1},{2,18}... | collective-permute-start | bytes 3538952 | tf_op jit(solution)/shard_map/ppermute | solution.py:27
  62.5 5.1 %collective-permute-start.6 = (bf16[256,256]{1,0:T(8,128)(2,1)S(1)}, bf16[256,256]{1,0:T(8,128)(2,1)S(1)}, u32[]{:S(2)}, u32[]{:S(2)}) collective-permute-start(bf16[256,256]{1,0:T(8,128)(2,1)S(1)} %get-tuple-element.125), channel_id=1, source_target_pairs={{0,64},{64,0},{128,192},{192,128},{1,65},{65,1},{129,193},{193,129... | collective-permute-start | bytes 393224 | tf_op jit(solution)/shard_map/ppermute | solution.py:31
  67.6 19.0 %collective-permute-start.7 = (bf16[256,256]{1,0:T(8,128)(2,1)S(1)}, bf16[256,256]{1,0:T(8,128)(2,1)S(1)}, u32[]{:S(2)}, u32[]{:S(2)}) collective-permute-start(bf16[256,256]{1,0:T(8,128)(2,1)S(1)} %fusion.3), channel_id=1, source_target_pairs={{0,128},{64,192},{128,0},{192,64},{1,129},{65,193},{129,1},{193,65... | collective-permute-start | bytes 393224 | tf_op jit(solution)/shard_map/ppermute | solution.py:31
  87.3 1.0 copy-start.10
  92.2 12.2 %collective-permute-start.11 = (bf16[2,256,512]{2,1,0:T(8,128)(2,1)}, bf16[2,256,512]{2,1,0:T(8,128)(2,1)S(1)}, u32[]{:S(2)}, u32[]{:S(2)}) collective-permute-start(bf16[2,256,512]{2,1,0:T(8,128)(2,1)} %get-tuple-element.72), channel_id=1, source_target_pairs={{0,16},{16,32},{32,48},{48,0},{1,17},{17,33},{33,49},{49,1},{2,18}... | collective-permute-start | bytes 1572872 | tf_op jit(solution)/shard_map/ppermute | solution.py:27
  92.7 13.6 %collective-permute-start.12 = (bf16[2,256,512]{2,1,0:T(8,128)(2,1)}, bf16[2,256,512]{2,1,0:T(8,128)(2,1)S(1)}, u32[]{:S(2)}, u32[]{:S(2)}) collective-permute-start(bf16[2,256,512]{2,1,0:T(8,128)(2,1)} %get-tuple-element.73), channel_id=1, source_target_pairs={{0,48},{16,0},{32,16},{48,32},{1,49},{17,1},{33,17},{49,33},{2,50}... | collective-permute-start | bytes 1572872 | tf_op jit(solution)/shard_map/ppermute | solution.py:27
  94.8 13.6 %collective-permute-start.13 = (bf16[2,288,512]{2,1,0:T(8,128)(2,1)S(1)}, bf16[2,288,512]{2,1,0:T(8,128)(2,1)S(1)}, u32[]{:S(2)}, u32[]{:S(2)}) collective-permute-start(bf16[2,288,512]{2,1,0:T(8,128)(2,1)S(1)} %dynamic-slice_bitcast_fusion), channel_id=1, source_target_pairs={{0,64},{64,0},{128,192},{192,128},{1,65},{65,1},{129,193},{193,129... | collective-permute-start | bytes 1769480 | tf_op jit(solution)/shard_map/ppermute | solution.py:31
  106.4 2.0 copy-start.1
  108.5 30.3 %collective-permute-start.15 = (bf16[2,2,256,512]{3,2,1,0:T(8,128)(2,1)}, bf16[2,2,256,512]{3,2,1,0:T(8,128)(2,1)}, u32[]{:S(2)}, u32[]{:S(2)}) collective-permute-start(bf16[2,2,256,512]{3,2,1,0:T(8,128)(2,1)} %get-tuple-element.76), channel_id=1, source_target_pairs={{0,16},{16,32},{32,48},{48,0},{1,17},{17,33},{33,49},{49,1},{2,18}... | collective-permute-start | bytes 3145736 | tf_op jit(solution)/shard_map/ppermute | solution.py:27
  110.2 28.5 %collective-permute-start.16 = (bf16[2,2,256,512]{3,2,1,0:T(8,128)(2,1)S(1)}, bf16[2,2,256,512]{3,2,1,0:T(8,128)(2,1)}, u32[]{:S(2)}, u32[]{:S(2)}) collective-permute-start(bf16[2,2,256,512]{3,2,1,0:T(8,128)(2,1)S(1)} %get-tuple-element.77), channel_id=1, source_target_pairs={{0,48},{16,0},{32,16},{48,32},{1,49},{17,1},{33,17},{49,33},{2,50}... | collective-permute-start | bytes 3145736 | tf_op jit(solution)/shard_map/ppermute | solution.py:27
  110.2 28.5 %collective-permute-start.14 = (bf16[2,288,512]{2,1,0:T(8,128)(2,1)S(1)}, bf16[2,288,512]{2,1,0:T(8,128)(2,1)S(1)}, u32[]{:S(2)}, u32[]{:S(2)}) collective-permute-start(bf16[2,288,512]{2,1,0:T(8,128)(2,1)S(1)} %bitcast_select_fusion), channel_id=1, source_target_pairs={{0,128},{64,192},{128,0},{192,64},{1,129},{65,193},{129,1},{193,65... | collective-permute-start | bytes 1769480 | tf_op jit(solution)/shard_map/ppermute | solution.py:31
  142.3 18.2 %copy-start.15 = (s32[256]{0:T(256)S(1)}, s32[256]{0:T(256)}, u32[]{:S(2)}) copy-start(s32[256]{0:T(256)} %param.9) | copy-start | bytes 3076
  142.3 4.3 %collective-permute-start.18 = (bf16[256,256]{1,0:T(8,128)(2,1)S(1)}, bf16[256,256]{1,0:T(8,128)(2,1)S(1)}, u32[]{:S(2)}, u32[]{:S(2)}) collective-permute-start(bf16[256,256]{1,0:T(8,128)(2,1)S(1)} %convert_element_type.164), channel_id=1, source_target_pairs={{0,16},{16,0},{32,48},{48,32},{1,17},{17,1},{33,49},{49,33},{2,18}... | collective-permute-start | bytes 393224 | tf_op jit(solution)/shard_map/ppermute | solution.py:31
  143.0 14.0 %collective-permute-start.17 = (bf16[2,288,512]{2,1,0:T(8,128)(2,1)S(1)}, bf16[2,288,512]{2,1,0:T(8,128)(2,1)S(1)}, u32[]{:S(2)}, u32[]{:S(2)}) collective-permute-start(bf16[2,288,512]{2,1,0:T(8,128)(2,1)S(1)} %broadcast_select_fusion), channel_id=1, source_target_pairs={{0,64},{64,0},{128,192},{192,128},{1,65},{65,1},{129,193},{193,129... | collective-permute-start | bytes 1769480 | tf_op jit(solution)/shard_map/ppermute | solution.py:31
  146.6 5.4 %collective-permute-start.19 = (bf16[256,256]{1,0:T(8,128)(2,1)S(1)}, bf16[256,256]{1,0:T(8,128)(2,1)S(1)}, u32[]{:S(2)}, u32[]{:S(2)}) collective-permute-start(bf16[256,256]{1,0:T(8,128)(2,1)S(1)} %fusion.4), channel_id=1, source_target_pairs={{0,32},{16,48},{32,0},{48,16},{1,33},{17,49},{33,1},{49,17},{2,34}... | collective-permute-start | bytes 393224 | tf_op jit(solution)/shard_map/ppermute | solution.py:31
  149.4 11.2 %copy-start.16 = (f32[128]{0:T(128)S(1)}, f32[128]{0:T(128)}, u32[]{:S(2)}) copy-start(f32[128]{0:T(128)} %get-tuple-element.128) | copy-start | bytes 1540
  157.1 8.7 %copy-start = (bf16[4,288,512]{2,1,0:T(8,128)(2,1)}, bf16[4,288,512]{2,1,0:T(8,128)(2,1)S(1)}, u32[]{:S(2)}) copy-start(bf16[4,288,512]{2,1,0:T(8,128)(2,1)S(1)} %pad_maximum_fusion.refs_8_) | copy-start | bytes 3538948
  157.1 26.4 %collective-permute-start.20 = (bf16[4,288,512]{2,1,0:T(8,128)(2,1)S(1)}, bf16[4,288,512]{2,1,0:T(8,128)(2,1)S(1)}, u32[]{:S(2)}, u32[]{:S(2)}) collective-permute-start(bf16[4,288,512]{2,1,0:T(8,128)(2,1)S(1)} %pad_maximum_fusion.refs_8_), channel_id=1, source_target_pairs={{0,16},{16,32},{32,48},{48,0},{1,17},{17,33},{33,49},{49,1},{2,18}... | collective-permute-start | bytes 3538952 | tf_op jit(solution)/shard_map/ppermute | solution.py:27
  159.9 26.7 %collective-permute-start.21 = (bf16[4,288,512]{2,1,0:T(8,128)(2,1)S(1)}, bf16[4,288,512]{2,1,0:T(8,128)(2,1)S(1)}, u32[]{:S(2)}, u32[]{:S(2)}) collective-permute-start(bf16[4,288,512]{2,1,0:T(8,128)(2,1)S(1)} %pad_maximum_fusion.refs_8_), channel_id=1, source_target_pairs={{0,48},{16,0},{32,16},{48,32},{1,49},{17,1},{33,17},{49,33},{2,50}... | collective-permute-start | bytes 3538952 | tf_op jit(solution)/shard_map/ppermute | solution.py:27
  161.9 8.3 %collective-permute-start.22 = (bf16[256,512]{1,0:T(8,128)(2,1)}, bf16[256,512]{1,0:T(8,128)(2,1)}, u32[]{:S(2)}, u32[]{:S(2)}) collective-permute-start(bf16[256,512]{1,0:T(8,128)(2,1)} %get-tuple-element.85), channel_id=1, source_target_pairs={{0,64},{64,128},{128,192},{192,0},{1,65},{65,129},{129,193},{193,1... | collective-permute-start | bytes 786440 | tf_op jit(solution)/shard_map/ppermute | solution.py:27
  162.2 20.1 %collective-permute-start.23 = (bf16[256,512]{1,0:T(8,128)(2,1)}, bf16[256,512]{1,0:T(8,128)(2,1)}, u32[]{:S(2)}, u32[]{:S(2)}) collective-permute-start(bf16[256,512]{1,0:T(8,128)(2,1)} %get-tuple-element.86), channel_id=1, source_target_pairs={{0,128},{64,192},{128,0},{192,64},{1,129},{65,193},{129,1},{193,65... | collective-permute-start | bytes 786440 | tf_op jit(solution)/shard_map/ppermute | solution.py:27
  163.0 19.2 %collective-permute-start.24 = (bf16[256,512]{1,0:T(8,128)(2,1)}, bf16[256,512]{1,0:T(8,128)(2,1)}, u32[]{:S(2)}, u32[]{:S(2)}) collective-permute-start(bf16[256,512]{1,0:T(8,128)(2,1)} %get-tuple-element.87), channel_id=1, source_target_pairs={{0,192},{64,0},{128,64},{192,128},{1,193},{65,1},{129,65},{193,129... | collective-permute-start | bytes 786440 | tf_op jit(solution)/shard_map/ppermute | solution.py:27
  170.2 18.3 %copy-start.5 = (f32[256,512]{1,0:T(8,128)S(1)}, f32[256,512]{1,0:T(8,128)}, u32[]{:S(2)}) copy-start(f32[256,512]{1,0:T(8,128)} %get-tuple-element.90) | copy-start | bytes 1572868
  183.4 7.1 %copy-start.2 = (bf16[4,288,512]{2,1,0:T(8,128)(2,1)}, bf16[4,288,512]{2,1,0:T(8,128)(2,1)S(1)}, u32[]{:S(2)}) copy-start(bf16[4,288,512]{2,1,0:T(8,128)(2,1)S(1)} %collective-permute-done.20.refs_16_) | copy-start | bytes 3538948
  186.6 4.0 %copy-start.3 = (bf16[4,288,512]{2,1,0:T(8,128)(2,1)}, bf16[4,288,512]{2,1,0:T(8,128)(2,1)S(1)}, u32[]{:S(2)}) copy-start(bf16[4,288,512]{2,1,0:T(8,128)(2,1)S(1)} %collective-permute-done.21.refs_17_) | copy-start | bytes 3538948
  186.6 17.1 %copy-start.18 = (s32[4]{0:T(128)S(1)}, s32[4]{0:T(128)}, u32[]{:S(2)}) copy-start(s32[4]{0:T(128)} %get-tuple-element.103) | copy-start | bytes 52
  186.6 34.1 %collective-permute-start.25 = (bf16[2,288,512]{2,1,0:T(8,128)(2,1)S(1)}, bf16[2,288,512]{2,1,0:T(8,128)(2,1)}, u32[]{:S(2)}, u32[]{:S(2)}) collective-permute-start(bf16[2,288,512]{2,1,0:T(8,128)(2,1)S(1)} %slice.87), channel_id=1, source_target_pairs={{0,16},{16,32},{32,48},{48,0},{1,17},{17,33},{33,49},{49,1},{2,18}... | collective-permute-start | bytes 1769480 | tf_op jit(solution)/shard_map/ppermute | solution.py:27
  187.0 33.7 %collective-permute-start.26 = (bf16[2,288,512]{2,1,0:T(8,128)(2,1)S(1)}, bf16[2,288,512]{2,1,0:T(8,128)(2,1)}, u32[]{:S(2)}, u32[]{:S(2)}) collective-permute-start(bf16[2,288,512]{2,1,0:T(8,128)(2,1)S(1)} %slice.88), channel_id=1, source_target_pairs={{0,48},{16,0},{32,16},{48,32},{1,49},{17,1},{33,17},{49,33},{2,50}... | collective-permute-start | bytes 1769480 | tf_op jit(solution)/shard_map/ppermute | solution.py:27
  190.6 20.1 %collective-permute-start.27 = (bf16[256,256]{1,0:T(8,128)(2,1)S(1)}, bf16[256,256]{1,0:T(8,128)(2,1)S(1)}, u32[]{:S(2)}, u32[]{:S(2)}) collective-permute-start(bf16[256,256]{1,0:T(8,128)(2,1)S(1)} %get-tuple-element.117), channel_id=1, source_target_pairs={{0,8},{1,40},{2,72},{3,104},{4,136},{5,168},{6,200},{7,232},{8,16}... | collective-permute-start | bytes 393224 | tf_op jit(solution)/shard_map/ppermute | solution.py:440
  196.1 24.6 %collective-permute-start.28 = (bf16[256,256]{1,0:T(8,128)(2,1)S(1)}, bf16[256,256]{1,0:T(8,128)(2,1)S(1)}, u32[]{:S(2)}, u32[]{:S(2)}) collective-permute-start(bf16[256,256]{1,0:T(8,128)(2,1)S(1)} %get-tuple-element.116), channel_id=1, source_target_pairs={{0,0},{1,56},{2,88},{3,120},{4,152},{5,184},{6,216},{7,248},{8,8},... | collective-permute-start | bytes 393224 | tf_op jit(solution)/shard_map/ppermute | solution.py:440
  210.7 15.0 %copy-start.13 = (bf16[256,256]{1,0:T(8,128)(2,1)}, bf16[256,256]{1,0:T(8,128)(2,1)S(1)}, u32[]{:S(2)}) copy-start(bf16[256,256]{1,0:T(8,128)(2,1)S(1)} %collective-permute-done.27.r0) | copy-start | bytes 393220
  220.7 5.0 %copy-start.14 = (bf16[256,256]{1,0:T(8,128)(2,1)}, bf16[256,256]{1,0:T(8,128)(2,1)S(1)}, u32[]{:S(2)}) copy-start(bf16[256,256]{1,0:T(8,128)(2,1)S(1)} %collective-permute-done.28.r1) | copy-start | bytes 393220
  220.7 7.7 %copy-start.4 = (f32[256,256]{1,0:T(8,128)S(1)}, f32[256,256]{1,0:T(8,128)}, u32[]{:S(2)}) copy-start(f32[256,256]{1,0:T(8,128)} %convert_add_fusion.1) | copy-start | bytes 786436
  226.8 4.8 %collective-permute-start.29 = (f32[256,640]{1,0:T(8,128)S(1)}, f32[256,640]{1,0:T(8,128)S(1)}, u32[]{:S(2)}, u32[]{:S(2)}) collective-permute-start(f32[256,640]{1,0:T(8,128)S(1)} %slice_bitcast_fusion), channel_id=1, source_target_pairs={{0,8},{8,0},{1,9},{9,1},{2,10},{10,2},{3,11},{11,3},{4,12},{12,4},... | collective-permute-start | bytes 1966088 | tf_op jit(solution)/shard_map/ppermute | solution.py:27
  (1 other events, 0.8 us)
where the time goes:
time: 236 us; the launch traced here: 235 us
  waiting for transfers between devices  87 us (37%)
  Pallas kernels  74.6 us (32%)
  starting transfers between devices  42.2 us (18%)
  other arithmetic  15.3 us (6%)
  local copies, waits for them, and re-layouts  11.6 us (5%)
  matrix products  2.38 us (1%)
    ppermute x7, waiting for transfers between devices, swap(): return lax.ppermute(array, axis, [(i, i ^ bit) for i in range(SIZES[axis])])  41.6 us
    ppermute x21, waiting for transfers between devices, send(): return lax.ppermute(array, axis, [(i, (i + shift) % n) for i in range(n)])  35.5 us
    pallas_call x8, Pallas kernels, weight_block(): pl.pallas_call(functools.partial(block_body, role), grid_spec=pltpu.Prefe...  22.9 us
    ppermute x21, starting transfers between devices, send(): return lax.ppermute(array, axis, [(i, (i + shift) % n) for i in range(n)])  19.9 us
    pallas_call x1, Pallas kernels, gram(): pl.pallas_call(gram_body, grid_spec=pltpu.PrefetchScalarGridSpec(num_scal...  15.9 us
    pallas_call x3, Pallas kernels, project(): pl.pallas_call(functools.partial(project_body, slots, piece, fresh), grid...  15.8 us
    pallas_call x2, Pallas kernels, normalize(): pl.pallas_call(normalize_body, grid=(tokens // rows,), in_specs=[pl.Block...  15.2 us
    ppermute x2, starting transfers between devices, shards(): lax.ppermute(jnp.where(second, tiles[1], tiles[0]), ALL, partner_moves(n))  13.2 us
  transfers between devices with their start and end apart: 30, of which 13 were waited for; matrix products, arithmetic and copies ran while one was open for 8% of the time, Pallas kernels for 23%

commit v1 on v0

--- a/solution.py
+++ b/solution.py
@@ -56,29 +56,10 @@
     return jnp.cos(angle), jnp.sin(angle) * sign[None, :]
 
 
-def normalize_body(x, gain, out):
-    wide = x[...].astype(f32)
+def normalize(hidden, norm_gain):
+    wide = hidden.astype(f32)
     meansq = jnp.mean(wide * wide, axis=-1, keepdims=True)
-    out[...] = (wide * lax.rsqrt(meansq + 1e-05) * gain[...]).astype(bf16)
-
-
-def normalize(hidden, norm_gain):
-    tokens, depth = hidden.shape
-    rows = 32
-    return pl.pallas_call(
-        normalize_body,
-        grid=(tokens // rows,),
-        in_specs=[
-            pl.BlockSpec((rows, depth), lambda i: (i, 0)),
-            pl.BlockSpec((1, depth), lambda i: (0, 0)),
-        ],
-        out_specs=pl.BlockSpec((rows, depth), lambda i: (i, 0)),
-        out_shape=jax.ShapeDtypeStruct(hidden.shape, bf16),
-        cost_estimate=pl.CostEstimate(
-            flops=5 * tokens * depth, bytes_accessed=4 * tokens * depth, transcendentals=tokens
-        ),
-        name="normalize",
-    )(hidden, norm_gain.reshape(1, depth))
+    return (wide * lax.rsqrt(meansq + 1e-05) * norm_gain[None, :]).astype(bf16)
 
 
 def block_body(role, table, q, kt, *refs):
@@ -153,26 +134,33 @@
     return lax.dot_general(left, right, (((0,), (0,)), ((), ())), preferred_element_type=f32)
 
 
-def gram_body(table, *refs):
-    ca, cb, r0a, r0b, r1a, r1b = (ref[...] for ref in refs[:6])
-    low, high, base = refs[6:]
+def gram_body(table, ca, cb, ra, rb, low, high, base, turned):
     slot = pl.program_id(0)
     half = NZ // 2
-    ta, tb = ca.T, cb.T
-    dot = functools.partial(jnp.dot, preferred_element_type=f32)
-    tile = jnp.concatenate([dot(ta, r0a) + dot(tb, r0b), dot(ta, r1a) + dot(tb, r1b)], axis=1)
+    tokens, tile = ca.shape
+
+    @pl.when(slot == 0)
+    def _():
+        for n in range(4):
+            span = slice(n * tile, (n + 1) * tile)
+            turned[n, :, :tokens] = ra[:, span].T
+            turned[n, :, tokens:] = rb[:, span].T
+
+    columns = jnp.concatenate([ca[...], cb[...]], axis=0)
+    rows = [turned[table[n, slot]] for n in (1, 2)]
+    tiles = [jnp.dot(x, columns, preferred_element_type=f32) for x in rows]
 
     @pl.when(slot < half)
     def _():
-        low[0] = tile.astype(bf16)
+        low[0, :tile], low[0, tile:] = (x.astype(bf16) for x in tiles)
 
     @pl.when((slot >= half) & (slot < NZ))
     def _():
-        high[0] = tile.astype(bf16)
+        high[0, :tile], high[0, tile:] = (x.astype(bf16) for x in tiles)
 
     @pl.when(slot >= NZ)
     def _():
-        base[0] = tile
+        base[0, :tile], base[0, tile:] = tiles
 
 
 def gram(table, mine, other):
@@ -180,20 +168,22 @@
     n = table.shape[1]
     tile = depth // (NY * NZ * 2)
     half = NZ // 2
-    at = lambda row: pl.BlockSpec((tokens, tile), lambda s, tab: (0, tab[row, s]))
-    block = (1, tile, 2 * tile)
-    shape = lambda n, kind: jax.ShapeDtypeStruct((n, tile, 2 * tile), kind)
+    cols = pl.BlockSpec((tokens, tile), lambda s, tab: (0, tab[0, s]))
+    rows = pl.BlockSpec((tokens, 4 * tile), lambda s, tab: (0, tab[3, 0]))
+    block = (1, 2 * tile, tile)
+    shape = lambda n, kind: jax.ShapeDtypeStruct((n, 2 * tile, tile), kind)
     return pl.pallas_call(
         gram_body,
         grid_spec=pltpu.PrefetchScalarGridSpec(
             num_scalar_prefetch=1,
             grid=(n,),
-            in_specs=[at(0), at(0), at(1), at(1), at(2), at(2)],
+            in_specs=[cols, cols, rows, rows],
             out_specs=[
                 pl.BlockSpec(block, lambda s, tab: (jnp.minimum(s, half - 1), 0, 0)),
                 pl.BlockSpec(block, lambda s, tab: (jnp.clip(s - half, 0, half - 1), 0, 0)),
                 pl.BlockSpec(block, lambda s, tab: (jnp.maximum(s - NZ, 0), 0, 0)),
             ],
+            scratch_shapes=[pltpu.VMEM((4, tile, 2 * tokens), bf16)],
         ),
         out_shape=[shape(half, bf16), shape(half, bf16), shape(n - NZ, f32)],
         cost_estimate=pl.CostEstimate(
@@ -202,7 +192,7 @@
             transcendentals=0,
         ),
         name="gram",
-    )(table, mine, other, mine, other, mine, other)
+    )(table, mine, other, mine, other)
 
 
 def project_body(slots, piece, fresh, table, *refs):
@@ -293,15 +283,15 @@
     def put(n, value):
         out[pl.ds(pl.multiple_of(slots[n] * tile, tile), tile), :] = value * scale
 
-    put(0, r1[...].astype(f32))
+    put(0, r1[...].astype(f32).T)
     put(1, extra[...])
-    put(2, r0[...].astype(f32))
-    put(3, own[:, :tile].T)
-    put(4, own[:, tile:].T)
+    put(2, r0[...].astype(f32).T)
+    put(3, own[:tile])
+    put(4, own[tile:])
 
 
 def assemble(scale, slots, own, r0, r1, extra):
-    tile = own.shape[0]
+    tile = own.shape[1]
     return pl.pallas_call(
         functools.partial(assemble_body, scale),
         in_specs=[pl.BlockSpec(memory_space=pltpu.SMEM)] + [pl.BlockSpec(memory_space=pltpu.VMEM)] * 4,
@@ -377,7 +367,7 @@
     zs = (z + jnp.arange(NZ)) % NZ
     t = (zs[None] * (2 * NY) + chip(jnp.array([2, 1, 3, 0])[:, None]) * 2 + k).reshape(-1)
     r0, r1 = row_pair(t, column)
-    table = jnp.stack([t, 4 * column + r0, 4 * column + r1]).astype(jnp.int32)
+    table = jnp.stack([t, r0, r1, jnp.full_like(t, column)]).astype(jnp.int32)
     p_low, p_high, base = gram(table, mine, other)
 
     tile = depth // (NY * NZ * 2)
@@ -398,20 +388,19 @@
     quarter = quarter.reshape(2, h, *quarter.shape[1:])
     kept = swap(pick(quarter, 1 - z % 2), "zl", 1)
     first = lax.broadcasted_iota(jnp.int32, (2, 1, 1, 1), 0) == 0
-    shape = (2, h, tile, 2 * tile)
+    shape = (2, h, 2 * tile, tile)
     up = base[:NZ].reshape(shape) + jnp.where(first, ga.astype(f32)[None], 0.0)
     down = base[NZ : 2 * NZ].reshape(shape) + jnp.where(first, 0.0, gb.astype(f32)[None])
     kept = jnp.where(z == root_z, pick(quarter, z % 2), kept)
-    up, down, kept = together((up.astype(bf16), down.astype(bf16), kept))
-    gc = send(up, "y", 1).reshape(NZ, tile, 2 * tile)
-    gd = send(down, "y", -1).reshape(NZ, tile, 2 * tile)
+    extra = butterfly(extra, "y", 1)
+    up, down, kept, extra = together((up.astype(bf16), down.astype(bf16), kept, extra))
+    gc = send(up, "y", 1).reshape(NZ, 2 * tile, tile)
+    gd = send(down, "y", -1).reshape(NZ, 2 * tile, tile)
     kept = jnp.where(z // 2 == root_z // 2, kept, swap(kept, "zl", 2))
+    extra = butterfly(extra, "y", 2)
     total = [base[2 * NZ + s] + gc[s].astype(f32) + gd[s].astype(f32) for s in range(NZ)]
     hess, rest = total[0], [x.astype(bf16) for x in total[1:]]
     kept, hess, rest, extra = together((kept, hess, rest, extra))
-    strip = jnp.concatenate([kept, swap(kept, "zl", 1)], axis=0)
-    extra = butterfly(butterfly(extra, "y", 1), "y", 2)
-    strip, extra, rest = together((strip, extra, rest))
 
     pairs = jnp.concatenate([2 * (z % 2) + jnp.arange(2), 2 * (1 - z % 2) + jnp.arange(2)])
 
@@ -419,12 +408,21 @@
         return (k * NY * NZ + chip(rel) * NZ + pairs).astype(jnp.int32)
 
     product = functools.partial(project, piece)
-    left, right = send(strip, "y", 1), send(strip, "y", -1)
-    parts = [send(rest[s - 1], "zl", s) for s in (1, 2, 3)]
-    raw = product(depth_tiles(0), mine, other, [strip])
+    crossed = swap(kept, "zl", 1)
+    left0, right0 = send(kept, "y", 1), send(kept, "y", -1)
     cosine, sine = turns(positions(token_ids))
-    left, right, parts, raw, cosine, sine = together((left, right, parts, raw, cosine, sine))
-    fl, fr = send(left[:h], "y", 1), send(right[h:], "y", -1)
+    crossed, left0, right0, rest, cosine, sine = together(
+        (crossed, left0, right0, rest, cosine, sine)
+    )
+    left1, right1 = send(crossed, "y", 1), send(crossed, "y", -1)
+    parts = [send(rest[1], "zl", 2)]
+    raw = product(depth_tiles(0), mine, other, [kept, crossed])
+    left0, left1, right1, parts, raw, rest = together((left0, left1, right1, parts, raw, rest))
+    fl, fr = send(left0, "y", 1), send(right1, "y", -1)
+    parts += [send(rest[0], "zl", 1), send(rest[2], "zl", 3)]
+    sides = jnp.concatenate([depth_tiles(3), depth_tiles(1)])
+    raw = product(sides, mine, other, [left0, left1, right0, right1], raw)
+    fl, fr, parts, raw = together((fl, fr, parts, raw))
 
     for x in parts:
         hess = hess + x.astype(f32)
@@ -432,8 +430,8 @@
     u, m = t // 4, t % 4
     diagonal = column == u
     r0, r1 = row_pair(t, column)
-    tiles = hess.astype(bf16)
-    tiles = [tiles[:, :tile], tiles[:, tile:]]
+    tiles, raw = together((hess.astype(bf16), raw))
+    tiles = [tiles[:tile], tiles[tile:]]
     mirrored = []
     for n in (0, 1):
         second = jnp.where(diagonal, 1, (n + m // 2) % 2) == 1
@@ -444,9 +442,6 @@
     slots = jnp.stack([slot1, jnp.where(diagonal, slot1, r0), slot0, r0, r1]).astype(jnp.int32)
     extra = jnp.where(m < 2, extra.T, extra)
 
-    sides = jnp.concatenate([depth_tiles(3), depth_tiles(1)])
-    raw = product(sides, mine, other, [left, right], raw)
-    mirrored, raw = together((mirrored, raw))
     raw = product(depth_tiles(2), mine, other, [fl, fr], raw)
     all_tokens = tokens * NY * NZ * 2
     hessian = assemble(2.0 / all_tokens, slots, hess, mirrored[0], mirrored[1], extra)

time: 236 us -> 239 us (1.013)
  the two profiles are of different devices: /device:TPU:29 before, /device:TPU:132 now
where the time goes in v1:
time: 239 us; the launch traced here: 235 us
  waiting for transfers between devices  89.2 us (37%)
  Pallas kernels  58.2 us (24%)
  starting transfers between devices  44.6 us (19%)
  other arithmetic  24.7 us (10%)
  local copies, waits for them, and re-layouts  16.3 us (7%)
    ppermute x7, waiting for transfers between devices, swap(): return lax.ppermute(array, axis, [(i, i ^ bit) for i in range(SIZES[axis])])  37.4 us
    ppermute x23, waiting for transfers between devices, send(): return lax.ppermute(array, axis, [(i, (i + shift) % n) for i in range(n)])  30.4 us
    ppermute x23, starting transfers between devices, send(): return lax.ppermute(array, axis, [(i, (i + shift) % n) for i in range(n)])  29.2 us
    pallas_call x8, Pallas kernels, weight_block(): pl.pallas_call(functools.partial(block_body, role), grid_spec=pltpu.Prefe...  22.8 us
    ppermute x2, waiting for transfers between devices, shards(): lax.ppermute(jnp.where(second, tiles[1], tiles[0]), ALL, partner_moves(n))  21.4 us
    pallas_call x3, Pallas kernels, project(): pl.pallas_call(functools.partial(project_body, slots, piece, fresh), grid...  15.7 us
    pallas_call x1, Pallas kernels, gram(): pl.pallas_call(gram_body, grid_spec=pltpu.PrefetchScalarGridSpec(num_scal...  14.9 us
    unnamed x54, local copies, waits for them, and re-layouts  10 us
  transfers between devices with their start and end apart: 32, of which 14 were waited for; matrix products, arithmetic and copies ran while one was open for 11% of the time, Pallas kernels for 17%

profile of v1, /device:TPU:132, one launch (start us, length us, event | category | flops | bytes accessed | tf_op | source)
XLA Modules:
  0.0 235.4 jit_solution(5468004115758560495)
XLA Ops:
  0.6 2.2 block_pack.4
  4.1 1.8 collective-permute-done.refs_0_
  6.9 3.4 %block_far.1 = (bf16[576,512]{1,0:T(8,128)(2,1)}, bf16[576,512]{1,0:T(8,128)(2,1)}) custom-call(s32[2]{0:T(128)} %pad_add_fusion.3.table, bf16[8192,512]{1,0:T(8,128)(2,1)} %bitcast.55, bf16[64,8192]{1,0:T(8,128)(2,1)} %bitcast.63, bf16[2,576,512]{2,1,0:T(8,128)(2,1)} %copy-done.10), custom_call_target="tpu_custom_call" | custom-call | bytes 3538944 | tf_op jit(solution)/shard_map/block_far/pallas_call | solution.py:120
  10.3 2.1 block_pack.6
  12.4 2.2 block_pack.5
  15.5 3.1 %fusion = f32[256]{0:T(256)S(1)} fusion(bf16[256,8192]{1,0:T(8,128)(2,1)} %param.7), kind=kLoop, calls=%fused_computation.4 | loop fusion | flops 6291200 | bytes 4195328 | tf_op jit(solution)/shard_map/reduce_sum | solution.py:61
  18.6 3.1 %collective-permute-start.4 = (bf16[576,512]{1,0:T(8,128)(2,1)}, bf16[576,512]{1,0:T(8,128)(2,1)}, u32[]{:S(2)}, u32[]{:S(2)}) collective-permute-start(bf16[576,512]{1,0:T(8,128)(2,1)} %get-tuple-element.67), channel_id=1, source_target_pairs={{0,48},{16,0},{32,16},{48,32},{1,49},{17,1},{33,17},{49,33},{2,50}... | collective-permute-start | bytes 1769480 | tf_op jit(solution)/shard_map/ppermute | solution.py:27
  23.0 2.1 block_pack.7
  25.1 10.0 %collective-permute-done.4.refs_1_ = bf16[576,512]{1,0:T(8,128)(2,1)} collective-permute-done((bf16[576,512]{1,0:T(8,128)(2,1)}, bf16[576,512]{1,0:T(8,128)(2,1)}, u32[]{:S(2)}, u32[]{:S(2)}) %collective-permute-start.4) | collective-permute-done | bytes 589856 | tf_op jit(solution)/shard_map/ppermute | solution.py:27
  36.3 3.4 %block_relay.3 = bf16[2,576,512]{2,1,0:T(8,128)(2,1)} custom-call(s32[3]{0:T(128)} %get-tuple-element.150.table, bf16[8192,512]{1,0:T(8,128)(2,1)} %bitcast.59, bf16[64,8192]{1,0:T(8,128)(2,1)} %bitcast.67, bf16[2,576,512]{2,1,0:T(8,128)(2,1)} %copy-done.6, bf16[576,512]{1,0:T(8,128)(2,1)} %collective-permute-done.4.refs_1_), custom_call_target="tpu_custom_call" | custom-call | bytes 4718592 | tf_op jit(solution)/shard_map/block_relay/pallas_call | solution.py:120
  40.7 3.5 %block_relay.2 = bf16[2,576,512]{2,1,0:T(8,128)(2,1)} custom-call(s32[3]{0:T(128)} %get-tuple-element.149.table, bf16[8192,512]{1,0:T(8,128)(2,1)} %bitcast.60, bf16[64,8192]{1,0:T(8,128)(2,1)} %bitcast.68, bf16[2,576,512]{2,1,0:T(8,128)(2,1)} %copy-done.5, bf16[576,512]{1,0:T(8,128)(2,1)} %collective-permute-done.2.refs_1_), custom_call_target="tpu_custom_call" | custom-call | bytes 4718592 | tf_op jit(solution)/shard_map/block_relay/pallas_call | solution.py:120
  44.2 3.8 %collective-permute-start.10 = (bf16[2,576,512]{2,1,0:T(8,128)(2,1)S(1)}, bf16[2,576,512]{2,1,0:T(8,128)(2,1)S(1)}, u32[]{:S(2)}, u32[]{:S(2)}) collective-permute-start(bf16[2,576,512]{2,1,0:T(8,128)(2,1)S(1)} %copy-done.7), channel_id=1, source_target_pairs={{0,48},{16,0},{32,16},{48,32},{1,49},{17,1},{33,17},{49,33},{2,50}... | collective-permute-start | bytes 3538952 | tf_op jit(solution)/shard_map/ppermute | solution.py:27
  47.9 3.1 %fusion.3 = f32[256]{0:T(256)S(1)} fusion(bf16[256,8192]{1,0:T(8,128)(2,1)} %collective-permute-done.5), kind=kLoop, calls=%fused_computation.7 | loop fusion | flops 6291200 | bytes 4195328 | tf_op jit(solution)/shard_map/reduce_sum | solution.py:61
  51.1 4.0 %fusion.5 = (bf16[256,8192]{1,0:T(8,128)(2,1)S(1)}, bf16[256,8192]{1,0:T(8,128)(2,1)S(1)}) fusion(bf16[256,8192]{1,0:T(8,128)(2,1)} %collective-permute-done.5, f32[256]{0:T(256)S(1)} %add_rsqrt_fusion, f32[8192]{0:T(1024)S(1)} %copy-done.22, f32[256]{0:T(256)S(1)} %add_rsqrt_fusion.1, bf16[256,8192]{1,0:T(8,128)(2,1)S(1)} %copy-done.2), kind=kLoop, calls=%fused_computation.9 | loop fusion | flops 16777216 | bytes 16812032 | tf_op jit(solution)/shard_map/convert_element_type | solution.py:62
  55.4 1.8 copy-done
  60.1 4.0 %collective-permute-done.6 = bf16[256,256]{1,0:T(8,128)(2,1)S(1)} collective-permute-done((bf16[256,256]{1,0:T(8,128)(2,1)S(1)}, bf16[256,256]{1,0:T(8,128)(2,1)S(1)}, u32[]{:S(2)}, u32[]{:S(2)}) %collective-permute-start.6) | collective-permute-done | bytes 131104 | tf_op jit(solution)/shard_map/ppermute | solution.py:31
  64.1 1.7 collective-permute-start.7
  65.8 14.9 %gram.1 = (bf16[2,512,256]{2,1,0:T(8,128)(2,1)}, bf16[2,512,256]{2,1,0:T(8,128)(2,1)}, f32[12,512,256]{2,1,0:T(8,128)}) custom-call(s32[4,16]{1,0:T(4,128)} %pad_add_fusion.table, bf16[256,8192]{1,0:T(8,128)(2,1)} %copy-done.1, bf16[256,8192]{1,0:T(8,128)(2,1)} %copy-done, bf16[256,8192]{1,0:T(8,128)(2,1)} %copy-done.1, bf16[256,8192]{1,0:T(8,128)(2,1)} %copy-done), custom_call_target="tpu_custom_call" | custom-call | flops 4294967296 | bytes 16777216 | tf_op jit(solution)/shard_map/gram/pallas_call | solution.py:175
  82.6 3.9 %block_quarter.1 = bf16[4,288,512]{2,1,0:T(8,128)(2,1)} custom-call(s32[5]{0:T(128)} %stack.121.table, bf16[8192,512]{1,0:T(8,128)(2,1)} %bitcast.61, bf16[64,8192]{1,0:T(8,128)(2,1)} %bitcast.69, bf16[2,576,512]{2,1,0:T(8,128)(2,1)} %collective-permute-done.8.refs_0_, bf16[2,576,512]{2,1,0:T(8,128)(2,1)} %collective-permute-done.9.refs_1_, ...), custom_call_target="tpu_custom_call" | custom-call | bytes 5898240 | tf_op jit(solution)/shard_map/block_quarter/pallas_call | solution.py:120
  88.7 2.0 collective-permute-start.11
  92.0 2.5 %fusion.29 = (f32[4,512,256]{2,1,0:T(8,128)S(1)}, f32[4,512,256]{2,1,0:T(8,128)S(1)}) fusion(f32[12,512,256]{2,1,0:T(8,128)} %get-tuple-element.73), kind=kLoop, calls=%fused_computation.100 | loop fusion | bytes 8388608 | tf_op jit(solution)/shard_map/slice | solution.py:393
  94.5 8.4 %collective-permute-done.11 = bf16[2,512,256]{2,1,0:T(8,128)(2,1)S(1)} collective-permute-done((bf16[2,512,256]{2,1,0:T(8,128)(2,1)}, bf16[2,512,256]{2,1,0:T(8,128)(2,1)S(1)}, u32[]{:S(2)}, u32[]{:S(2)}) %collective-permute-start.11) | collective-permute-done | bytes 524320 | tf_op jit(solution)/shard_map/ppermute | solution.py:27
  103.4 1.6 add_convert_fusion
  105.1 1.8 collective-permute-start.16
  106.9 1.5 collective-permute-start.17
  108.4 1.5 collective-permute-start.15
  111.1 21.7 %collective-permute-done.18 = bf16[256,256]{1,0:T(8,128)(2,1)S(1)} collective-permute-done((bf16[256,256]{1,0:T(8,128)(2,1)S(1)}, bf16[256,256]{1,0:T(8,128)(2,1)S(1)}, u32[]{:S(2)}, u32[]{:S(2)}) %collective-permute-start.18) | collective-permute-done | bytes 131104 | tf_op jit(solution)/shard_map/ppermute | solution.py:31
  132.9 1.6 collective-permute-done.15
  135.7 3.4 %fusion.8 = (bf16[512,256]{1,0:T(8,128)(2,1)}, bf16[512,256]{1,0:T(8,128)(2,1)}, bf16[512,256]{1,0:T(8,128)(2,1)}, f32[512,256]{1,0:T(8,128)S(1)}) fusion(f32[12,512,256]{2,1,0:T(8,128)} %get-tuple-element.73, bf16[4,512,256]{2,1,0:T(8,128)(2,1)} %bitcast.26, bf16[4,512,256]{2,1,0:T(8,128)(2,1)} %bitcast.25), kind=kLoop, calls=%fused_computation.24 | loop fusion | flops 2490368 | bytes 5505024 | tf_op jit(solution)/shard_map/convert_element_type | solution.py:402
  139.4 3.0 %collective-permute-start.21 = (bf16[2,288,512]{2,1,0:T(8,128)(2,1)S(1)}, bf16[2,288,512]{2,1,0:T(8,128)(2,1)S(1)}, u32[]{:S(2)}, u32[]{:S(2)}) collective-permute-start(bf16[2,288,512]{2,1,0:T(8,128)(2,1)S(1)} %broadcast_select_fusion.refs_8_), channel_id=1, source_target_pairs={{0,48},{16,0},{32,16},{48,32},{1,49},{17,1},{33,17},{49,33},{2,50}... | collective-permute-start | bytes 1769480 | tf_op jit(solution)/shard_map/ppermute | solution.py:27
  142.5 1.3 fusion.10
  143.8 10.0 %collective-permute-done.19.refs_9_ = bf16[2,288,512]{2,1,0:T(8,128)(2,1)S(1)} collective-permute-done((bf16[2,288,512]{2,1,0:T(8,128)(2,1)S(1)}, bf16[2,288,512]{2,1,0:T(8,128)(2,1)S(1)}, u32[]{:S(2)}, u32[]{:S(2)}) %collective-permute-start.19) | collective-permute-done | bytes 589856 | tf_op jit(solution)/shard_map/ppermute | solution.py:31
  155.2 3.2 %collective-permute-start.23 = (bf16[2,288,512]{2,1,0:T(8,128)(2,1)S(1)}, bf16[2,288,512]{2,1,0:T(8,128)(2,1)}, u32[]{:S(2)}, u32[]{:S(2)}) collective-permute-start(bf16[2,288,512]{2,1,0:T(8,128)(2,1)S(1)} %collective-permute-done.19.refs_9_), channel_id=1, source_target_pairs={{0,48},{16,0},{32,16},{48,32},{1,49},{17,1},{33,17},{49,33},{2,50}... | collective-permute-start | bytes 1769480 | tf_op jit(solution)/shard_map/ppermute | solution.py:27
  158.5 1.3 collective-permute-start.24
  160.4 4.4 %project.3.refs_20_ = f32[2,256,640]{2,1,0:T(8,128)} custom-call(s32[4]{0:T(128)} %get-tuple-element.139.table, bf16[256,8192]{1,0:T(8,128)(2,1)} %copy-done.1, bf16[256,8192]{1,0:T(8,128)(2,1)} %copy-done.1, bf16[256,8192]{1,0:T(8,128)(2,1)} %copy-done.1, bf16[256,8192]{1,0:T(8,128)(2,1)} %copy-done.1, bf16[256,8192]{1,0:T(8,128)(2,1)} %copy-done, ...), custom_call_target="tpu_custom_call" | custom-call | flops 536870912 | bytes 2621440 | tf_op jit(solution)/shard_map/project/pallas_call | solution.py:230
  164.8 6.9 %collective-permute-done.24 = bf16[512,256]{1,0:T(8,128)(2,1)S(1)} collective-permute-done((bf16[512,256]{1,0:T(8,128)(2,1)}, bf16[512,256]{1,0:T(8,128)(2,1)S(1)}, u32[]{:S(2)}, u32[]{:S(2)}) %collective-permute-start.24) | collective-permute-done | bytes 262176 | tf_op jit(solution)/shard_map/ppermute | solution.py:27
  172.4 3.2 %collective-permute-start.26 = (bf16[2,288,512]{2,1,0:T(8,128)(2,1)}, bf16[2,288,512]{2,1,0:T(8,128)(2,1)S(1)}, u32[]{:S(2)}, u32[]{:S(2)}) collective-permute-start(bf16[2,288,512]{2,1,0:T(8,128)(2,1)} %collective-permute-done.23.refs_19_), channel_id=1, source_target_pairs={{0,48},{16,0},{32,16},{48,32},{1,49},{17,1},{33,17},{49,33},{2,50}... | collective-permute-start | bytes 1769480 | tf_op jit(solution)/shard_map/ppermute | solution.py:27
  175.7 3.8 %collective-permute-start.28 = (bf16[512,256]{1,0:T(8,128)(2,1)}, bf16[512,256]{1,0:T(8,128)(2,1)S(1)}, u32[]{:S(2)}, u32[]{:S(2)}) collective-permute-start(bf16[512,256]{1,0:T(8,128)(2,1)} %get-tuple-element.101), channel_id=1, source_target_pairs={{0,192},{64,0},{128,64},{192,128},{1,193},{65,1},{129,65},{193,129... | collective-permute-start | bytes 786440 | tf_op jit(solution)/shard_map/ppermute | solution.py:27
  180.1 6.4 %project.4.refs_10_ = f32[2,256,640]{2,1,0:T(8,128)} custom-call(s32[8]{0:T(128)} %pad_add_fusion.5.table, bf16[256,8192]{1,0:T(8,128)(2,1)} %copy-done.1, bf16[256,8192]{1,0:T(8,128)(2,1)} %copy-done.1, bf16[256,8192]{1,0:T(8,128)(2,1)} %copy-done.1, bf16[256,8192]{1,0:T(8,128)(2,1)} %copy-done.1, bf16[256,8192]{1,0:T(8,128)(2,1)} %copy-done.1, ...), custom_call_target="tpu_custom_call" | custom-call | flops 1073741824 | bytes 4718592 | tf_op jit(solution)/shard_map/project/pallas_call | solution.py:230
  186.9 1.3 collective-permute-done.28
  189.0 2.1 fusion.28
  191.0 4.8 %project.5.a = f32[2,256,640]{2,1,0:T(8,128)} custom-call(s32[4]{0:T(128)} %get-tuple-element.140.table, bf16[256,8192]{1,0:T(8,128)(2,1)} %copy-done.1, bf16[256,8192]{1,0:T(8,128)(2,1)} %copy-done.1, bf16[256,8192]{1,0:T(8,128)(2,1)} %copy-done.1, bf16[256,8192]{1,0:T(8,128)(2,1)} %copy-done.1, bf16[256,8192]{1,0:T(8,128)(2,1)} %copy-done, ...), custom_call_target="tpu_custom_call" | custom-call | flops 536870912 | bytes 2621440 | tf_op jit(solution)/shard_map/project/pallas_call | solution.py:230
  198.2 1.7 collective-permute-start.30
  199.9 7.0 %collective-permute-start.31 = (bf16[256,256]{1,0:T(8,128)(2,1)S(1)}, bf16[256,256]{1,0:T(8,128)(2,1)S(1)}, u32[]{:S(2)}, u32[]{:S(2)}) collective-permute-start(bf16[256,256]{1,0:T(8,128)(2,1)S(1)} %get-tuple-element.132), channel_id=1, source_target_pairs={{0,0},{1,56},{2,88},{3,120},{4,152},{5,184},{6,216},{7,248},{8,8},... | collective-permute-start | bytes 393224 | tf_op jit(solution)/shard_map/ppermute | solution.py:438
  207.7 18.1 %collective-permute-done.30.r0 = bf16[256,256]{1,0:T(8,128)(2,1)S(1)} collective-permute-done((bf16[256,256]{1,0:T(8,128)(2,1)S(1)}, bf16[256,256]{1,0:T(8,128)(2,1)S(1)}, u32[]{:S(2)}, u32[]{:S(2)}) %collective-permute-start.30) | collective-permute-done | bytes 131104 | tf_op jit(solution)/shard_map/ppermute | solution.py:438
  225.8 3.3 %collective-permute-done.31.r1 = bf16[256,256]{1,0:T(8,128)(2,1)S(1)} collective-permute-done((bf16[256,256]{1,0:T(8,128)(2,1)S(1)}, bf16[256,256]{1,0:T(8,128)(2,1)S(1)}, u32[]{:S(2)}, u32[]{:S(2)}) %collective-permute-start.31) | collective-permute-done | bytes 131104 | tf_op jit(solution)/shard_map/ppermute | solution.py:438
  229.7 2.4 %assemble.1 = f32[1024,256]{1,0:T(8,128)} custom-call(s32[5]{0:T(128)} %stack.128.slots, f32[512,256]{1,0:T(8,128)} %get-tuple-element.120.own, bf16[256,256]{1,0:T(8,128)(2,1)} %copy-done.20, bf16[256,256]{1,0:T(8,128)(2,1)} %copy-done.21, f32[256,256]{1,0:T(8,128)} %broadcast_select_fusion.1.extra), custom_call_target="tpu_custom_call" | custom-call | tf_op jit(solution)/shard_map/assemble/pallas_call | solution.py:295
  233.0 2.4 %rope.1 = (bf16[256,512]{1,0:T(8,128)(2,1)}, bf16[64,256]{1,0:T(8,128)(2,1)}) custom-call(s32[1]{0:T(128)} %bitcast.at, f32[2,256,640]{2,1,0:T(8,128)} %project.5.a, f32[256,640]{1,0:T(8,128)} %copy-done.11, f32[256,128]{1,0:T(8,128)} %get-tuple-element.113.cosine, f32[256,128]{1,0:T(8,128)} %get-tuple-element.114.sine), custom_call_target="tpu_custom_call" | custom-call | tf_op jit(solution)/shard_map/rope/pallas_call | solution.py:269
  (132 shorter events, 26.5 us)
Async XLA Ops:
  2.8 3.1 %collective-permute-start = (bf16[2,576,512]{2,1,0:T(8,128)(2,1)}, bf16[2,576,512]{2,1,0:T(8,128)(2,1)S(1)}, u32[]{:S(2)}, u32[]{:S(2)}) collective-permute-start(bf16[2,576,512]{2,1,0:T(8,128)(2,1)} %block_pack.4), channel_id=1, source_target_pairs={{0,8},{8,0},{1,9},{9,1},{2,10},{10,2},{3,11},{11,3},{4,12},{12,4},... | collective-permute-start | bytes 3538952 | tf_op jit(solution)/shard_map/ppermute | solution.py:27
  12.4 2.4 %copy-start.25 = (s32[4]{0:T(128)S(1)}, s32[4]{0:T(128)}, u32[]{:S(2)}) copy-start(s32[4]{0:T(128)} %constant.317.clone) | copy-start | bytes 52
  12.4 2.4 %copy-start.8 = (bf16[2,576,512]{2,1,0:T(8,128)(2,1)S(1)}, bf16[2,576,512]{2,1,0:T(8,128)(2,1)}, u32[]{:S(2)}) copy-start(bf16[2,576,512]{2,1,0:T(8,128)(2,1)} %block_pack.6) | copy-start | bytes 3538948
  14.7 33.3 %collective-permute-start.5 = (bf16[256,8192]{1,0:T(8,128)(2,1)}, bf16[256,8192]{1,0:T(8,128)(2,1)}, u32[]{:S(2)}, u32[]{:S(2)}) collective-permute-start(bf16[256,8192]{1,0:T(8,128)(2,1)} %param.7), channel_id=1, source_target_pairs={{0,8},{8,0},{1,9},{9,1},{2,10},{10,2},{3,11},{11,3},{4,12},{12,4},... | collective-permute-start | bytes 12582920 | tf_op jit(solution)/shard_map/ppermute | solution.py:27
  14.8 20.3 %collective-permute-start.3 = (bf16[2,576,512]{2,1,0:T(8,128)(2,1)S(1)}, bf16[2,576,512]{2,1,0:T(8,128)(2,1)S(1)}, u32[]{:S(2)}, u32[]{:S(2)}) collective-permute-start(bf16[2,576,512]{2,1,0:T(8,128)(2,1)S(1)} %copy-done.8), channel_id=1, source_target_pairs={{0,8},{8,0},{1,9},{9,1},{2,10},{10,2},{3,11},{11,3},{4,12},{12,4},... | collective-permute-start | bytes 3538952 | tf_op jit(solution)/shard_map/ppermute | solution.py:27
  15.3 24.4 %collective-permute-start.1 = (bf16[2,576,512]{2,1,0:T(8,128)(2,1)}, bf16[2,576,512]{2,1,0:T(8,128)(2,1)S(1)}, u32[]{:S(2)}, u32[]{:S(2)}) collective-permute-start(bf16[2,576,512]{2,1,0:T(8,128)(2,1)} %block_pack.5), channel_id=1, source_target_pairs={{0,8},{8,0},{1,9},{9,1},{2,10},{10,2},{3,11},{11,3},{4,12},{12,4},... | collective-permute-start | bytes 3538952 | tf_op jit(solution)/shard_map/ppermute | solution.py:27
  18.6 16.5 %collective-permute-start.4 = (bf16[576,512]{1,0:T(8,128)(2,1)}, bf16[576,512]{1,0:T(8,128)(2,1)}, u32[]{:S(2)}, u32[]{:S(2)}) collective-permute-start(bf16[576,512]{1,0:T(8,128)(2,1)} %get-tuple-element.67), channel_id=1, source_target_pairs={{0,48},{16,0},{32,16},{48,32},{1,49},{17,1},{33,17},{49,33},{2,50}... | collective-permute-start | bytes 1769480 | tf_op jit(solution)/shard_map/ppermute | solution.py:27
  21.7 17.9 %collective-permute-start.2 = (bf16[576,512]{1,0:T(8,128)(2,1)}, bf16[576,512]{1,0:T(8,128)(2,1)}, u32[]{:S(2)}, u32[]{:S(2)}) collective-permute-start(bf16[576,512]{1,0:T(8,128)(2,1)} %get-tuple-element.65), channel_id=1, source_target_pairs={{0,16},{16,32},{32,48},{48,0},{1,17},{17,33},{33,49},{49,1},{2,18}... | collective-permute-start | bytes 1769480 | tf_op jit(solution)/shard_map/ppermute | solution.py:27
  35.1 46.5 %collective-permute-start.8 = (bf16[2,576,512]{2,1,0:T(8,128)(2,1)}, bf16[2,576,512]{2,1,0:T(8,128)(2,1)}, u32[]{:S(2)}, u32[]{:S(2)}) collective-permute-start(bf16[2,576,512]{2,1,0:T(8,128)(2,1)} %block_pack.7), channel_id=1, source_target_pairs={{0,8},{8,0},{1,9},{9,1},{2,10},{10,2},{3,11},{11,3},{4,12},{12,4},... | collective-permute-start | bytes 3538952 | tf_op jit(solution)/shard_map/ppermute | solution.py:27
  40.7 3.5 %copy-start.7 = (bf16[2,576,512]{2,1,0:T(8,128)(2,1)S(1)}, bf16[2,576,512]{2,1,0:T(8,128)(2,1)}, u32[]{:S(2)}) copy-start(bf16[2,576,512]{2,1,0:T(8,128)(2,1)} %block_relay.3) | copy-start | bytes 3538948
  40.7 10.4 %copy-start.22 = (f32[8192]{0:T(1024)S(1)}, f32[8192]{0:T(1024)}, u32[]{:S(2)}) copy-start(f32[8192]{0:T(1024)} %param.8) | copy-start | bytes 98308
  44.2 6.9 %copy-start.2 = (bf16[256,8192]{1,0:T(8,128)(2,1)S(1)}, bf16[256,8192]{1,0:T(8,128)(2,1)}, u32[]{:S(2)}) copy-start(bf16[256,8192]{1,0:T(8,128)(2,1)} %param.7) | copy-start | bytes 12582916
  44.2 37.4 %collective-permute-start.10 = (bf16[2,576,512]{2,1,0:T(8,128)(2,1)S(1)}, bf16[2,576,512]{2,1,0:T(8,128)(2,1)S(1)}, u32[]{:S(2)}, u32[]{:S(2)}) collective-permute-start(bf16[2,576,512]{2,1,0:T(8,128)(2,1)S(1)} %copy-done.7), channel_id=1, source_target_pairs={{0,48},{16,0},{32,16},{48,32},{1,49},{17,1},{33,17},{49,33},{2,50}... | collective-permute-start | bytes 3538952 | tf_op jit(solution)/shard_map/ppermute | solution.py:27
  47.9 33.7 %collective-permute-start.9 = (bf16[2,576,512]{2,1,0:T(8,128)(2,1)}, bf16[2,576,512]{2,1,0:T(8,128)(2,1)}, u32[]{:S(2)}, u32[]{:S(2)}) collective-permute-start(bf16[2,576,512]{2,1,0:T(8,128)(2,1)} %block_relay.2), channel_id=1, source_target_pairs={{0,16},{16,32},{32,48},{48,0},{1,17},{17,33},{33,49},{49,1},{2,18}... | collective-permute-start | bytes 3538952 | tf_op jit(solution)/shard_map/ppermute | solution.py:27
  51.1 8.4 %copy-start.23 = (s32[1,16]{1,0:T(1,128)S(1)}, s32[1,16]{1,0:T(1,128)}, u32[]{:S(2)}) copy-start(s32[1,16]{1,0:T(1,128)} %compare_select_fusion.12) | copy-start | bytes 196
  55.1 3.3 %copy-start.1 = (bf16[256,8192]{1,0:T(8,128)(2,1)}, bf16[256,8192]{1,0:T(8,128)(2,1)S(1)}, u32[]{:S(2)}) copy-start(bf16[256,8192]{1,0:T(8,128)(2,1)S(1)} %get-tuple-element.135.ca.ra.refs_0_.refs_1_.refs_2_.refs_3_.refs_4_.refs_5_.refs_6_.refs_7_) | copy-start | bytes 12582916
  58.4 5.6 %collective-permute-start.6 = (bf16[256,256]{1,0:T(8,128)(2,1)S(1)}, bf16[256,256]{1,0:T(8,128)(2,1)S(1)}, u32[]{:S(2)}, u32[]{:S(2)}) collective-permute-start(bf16[256,256]{1,0:T(8,128)(2,1)S(1)} %get-tuple-element.143), channel_id=1, source_target_pairs={{0,64},{64,0},{128,192},{192,128},{1,65},{65,1},{129,193},{193,129... | collective-permute-start | bytes 393224 | tf_op jit(solution)/shard_map/ppermute | solution.py:31
  64.1 16.7 %collective-permute-start.7 = (bf16[256,256]{1,0:T(8,128)(2,1)S(1)}, bf16[256,256]{1,0:T(8,128)(2,1)S(1)}, u32[]{:S(2)}, u32[]{:S(2)}) collective-permute-start(bf16[256,256]{1,0:T(8,128)(2,1)S(1)} %fusion.9), channel_id=1, source_target_pairs={{0,128},{64,192},{128,0},{192,64},{1,129},{65,193},{129,1},{193,65... | collective-permute-start | bytes 393224 | tf_op jit(solution)/shard_map/ppermute | solution.py:31
  80.8 13.7 %collective-permute-start.14 = (bf16[256,256]{1,0:T(8,128)(2,1)S(1)}, bf16[256,256]{1,0:T(8,128)(2,1)S(1)}, u32[]{:S(2)}, u32[]{:S(2)}) collective-permute-start(bf16[256,256]{1,0:T(8,128)(2,1)S(1)} %convert_element_type.166), channel_id=1, source_target_pairs={{0,16},{16,0},{32,48},{48,32},{1,17},{17,1},{33,49},{49,33},{2,18}... | collective-permute-start | bytes 393224 | tf_op jit(solution)/shard_map/ppermute | solution.py:31
  81.6 9.2 %copy-start.26 = (bf16[2,512,256]{2,1,0:T(8,128)(2,1)S(1)}, bf16[2,512,256]{2,1,0:T(8,128)(2,1)}, u32[]{:S(2)}) copy-start(bf16[2,512,256]{2,1,0:T(8,128)(2,1)} %get-tuple-element.81) | copy-start | bytes 1572868
  87.6 17.4 %collective-permute-start.13 = (bf16[2,288,512]{2,1,0:T(8,128)(2,1)S(1)}, bf16[2,288,512]{2,1,0:T(8,128)(2,1)S(1)}, u32[]{:S(2)}, u32[]{:S(2)}) collective-permute-start(bf16[2,288,512]{2,1,0:T(8,128)(2,1)S(1)} %dynamic-slice_bitcast_fusion), channel_id=1, source_target_pairs={{0,64},{64,0},{128,192},{192,128},{1,65},{65,1},{129,193},{193,129... | collective-permute-start | bytes 1769480 | tf_op jit(solution)/shard_map/ppermute | solution.py:31
  88.7 14.2 %collective-permute-start.11 = (bf16[2,512,256]{2,1,0:T(8,128)(2,1)}, bf16[2,512,256]{2,1,0:T(8,128)(2,1)S(1)}, u32[]{:S(2)}, u32[]{:S(2)}) collective-permute-start(bf16[2,512,256]{2,1,0:T(8,128)(2,1)} %get-tuple-element.80), channel_id=1, source_target_pairs={{0,16},{16,32},{32,48},{48,0},{1,17},{17,33},{33,49},{49,1},{2,18}... | collective-permute-start | bytes 1572872 | tf_op jit(solution)/shard_map/ppermute | solution.py:27
  90.7 12.5 %collective-permute-start.12 = (bf16[2,512,256]{2,1,0:T(8,128)(2,1)S(1)}, bf16[2,512,256]{2,1,0:T(8,128)(2,1)S(1)}, u32[]{:S(2)}, u32[]{:S(2)}) collective-permute-start(bf16[2,512,256]{2,1,0:T(8,128)(2,1)S(1)} %copy-done.26), channel_id=1, source_target_pairs={{0,48},{16,0},{32,16},{48,32},{1,49},{17,1},{33,17},{49,33},{2,50}... | collective-permute-start | bytes 1572872 | tf_op jit(solution)/shard_map/ppermute | solution.py:27
  103.3 7.8 %copy-start.24 = (s32[256]{0:T(256)S(1)}, s32[256]{0:T(256)}, u32[]{:S(2)}) copy-start(s32[256]{0:T(256)} %param.9) | copy-start | bytes 3076
  105.1 30.6 %collective-permute-start.16 = (bf16[2,2,512,256]{3,2,1,0:T(8,128)(2,1)}, bf16[2,2,512,256]{3,2,1,0:T(8,128)(2,1)}, u32[]{:S(2)}, u32[]{:S(2)}) collective-permute-start(bf16[2,2,512,256]{3,2,1,0:T(8,128)(2,1)} %get-tuple-element.85), channel_id=1, source_target_pairs={{0,16},{16,32},{32,48},{48,0},{1,17},{17,33},{33,49},{49,1},{2,18}... | collective-permute-start | bytes 3145736 | tf_op jit(solution)/shard_map/ppermute | solution.py:27
  106.9 28.8 %collective-permute-start.17 = (bf16[2,2,512,256]{3,2,1,0:T(8,128)(2,1)S(1)}, bf16[2,2,512,256]{3,2,1,0:T(8,128)(2,1)}, u32[]{:S(2)}, u32[]{:S(2)}) collective-permute-start(bf16[2,2,512,256]{3,2,1,0:T(8,128)(2,1)S(1)} %get-tuple-element.86), channel_id=1, source_target_pairs={{0,48},{16,0},{32,16},{48,32},{1,49},{17,1},{33,17},{49,33},{2,50}... | collective-permute-start | bytes 3145736 | tf_op jit(solution)/shard_map/ppermute | solution.py:27
  108.4 26.1 %collective-permute-start.15 = (bf16[2,288,512]{2,1,0:T(8,128)(2,1)S(1)}, bf16[2,288,512]{2,1,0:T(8,128)(2,1)}, u32[]{:S(2)}, u32[]{:S(2)}) collective-permute-start(bf16[2,288,512]{2,1,0:T(8,128)(2,1)S(1)} %bitcast_select_fusion), channel_id=1, source_target_pairs={{0,128},{64,192},{128,0},{192,64},{1,129},{65,193},{129,1},{193,65... | collective-permute-start | bytes 1769480 | tf_op jit(solution)/shard_map/ppermute | solution.py:31
  109.9 23.0 %collective-permute-start.18 = (bf16[256,256]{1,0:T(8,128)(2,1)S(1)}, bf16[256,256]{1,0:T(8,128)(2,1)S(1)}, u32[]{:S(2)}, u32[]{:S(2)}) collective-permute-start(bf16[256,256]{1,0:T(8,128)(2,1)S(1)} %convert_element_type.182), channel_id=1, source_target_pairs={{0,32},{16,48},{32,0},{48,16},{1,33},{17,49},{33,1},{49,17},{2,34}... | collective-permute-start | bytes 393224 | tf_op jit(solution)/shard_map/ppermute | solution.py:31
  135.7 24.7 %copy-start.4 = (bf16[2,288,512]{2,1,0:T(8,128)(2,1)}, bf16[2,288,512]{2,1,0:T(8,128)(2,1)S(1)}, u32[]{:S(2)}) copy-start(bf16[2,288,512]{2,1,0:T(8,128)(2,1)S(1)} %broadcast_select_fusion.refs_8_) | copy-start | bytes 1769476
  139.1 14.7 %collective-permute-start.19 = (bf16[2,288,512]{2,1,0:T(8,128)(2,1)S(1)}, bf16[2,288,512]{2,1,0:T(8,128)(2,1)S(1)}, u32[]{:S(2)}, u32[]{:S(2)}) collective-permute-start(bf16[2,288,512]{2,1,0:T(8,128)(2,1)S(1)} %broadcast_select_fusion.refs_8_), channel_id=1, source_target_pairs={{0,64},{64,0},{128,192},{192,128},{1,65},{65,1},{129,193},{193,129... | collective-permute-start | bytes 1769480 | tf_op jit(solution)/shard_map/ppermute | solution.py:31
  139.1 16.0 %collective-permute-start.20 = (bf16[2,288,512]{2,1,0:T(8,128)(2,1)S(1)}, bf16[2,288,512]{2,1,0:T(8,128)(2,1)S(1)}, u32[]{:S(2)}, u32[]{:S(2)}) collective-permute-start(bf16[2,288,512]{2,1,0:T(8,128)(2,1)S(1)} %broadcast_select_fusion.refs_8_), channel_id=1, source_target_pairs={{0,16},{16,32},{32,48},{48,0},{1,17},{17,33},{33,49},{49,1},{2,18}... | collective-permute-start | bytes 1769480 | tf_op jit(solution)/shard_map/ppermute | solution.py:27
  139.4 15.7 %collective-permute-start.21 = (bf16[2,288,512]{2,1,0:T(8,128)(2,1)S(1)}, bf16[2,288,512]{2,1,0:T(8,128)(2,1)S(1)}, u32[]{:S(2)}, u32[]{:S(2)}) collective-permute-start(bf16[2,288,512]{2,1,0:T(8,128)(2,1)S(1)} %broadcast_select_fusion.refs_8_), channel_id=1, source_target_pairs={{0,48},{16,0},{32,16},{48,32},{1,49},{17,1},{33,17},{49,33},{2,50}... | collective-permute-start | bytes 1769480 | tf_op jit(solution)/shard_map/ppermute | solution.py:27
  153.9 6.6 %copy-start.12 = (bf16[2,288,512]{2,1,0:T(8,128)(2,1)}, bf16[2,288,512]{2,1,0:T(8,128)(2,1)S(1)}, u32[]{:S(2)}) copy-start(bf16[2,288,512]{2,1,0:T(8,128)(2,1)S(1)} %collective-permute-done.19.refs_9_) | copy-start | bytes 1769476
  155.1 16.6 %copy-start.15 = (bf16[2,288,512]{2,1,0:T(8,128)(2,1)}, bf16[2,288,512]{2,1,0:T(8,128)(2,1)S(1)}, u32[]{:S(2)}) copy-start(bf16[2,288,512]{2,1,0:T(8,128)(2,1)S(1)} %collective-permute-done.20.refs_16_) | copy-start | bytes 1769476
  155.1 9.7 %copy-start.16 = (bf16[2,288,512]{2,1,0:T(8,128)(2,1)}, bf16[2,288,512]{2,1,0:T(8,128)(2,1)S(1)}, u32[]{:S(2)}) copy-start(bf16[2,288,512]{2,1,0:T(8,128)(2,1)S(1)} %collective-permute-done.21.refs_18_) | copy-start | bytes 1769476
  155.1 16.6 %collective-permute-start.22 = (bf16[2,288,512]{2,1,0:T(8,128)(2,1)S(1)}, bf16[2,288,512]{2,1,0:T(8,128)(2,1)}, u32[]{:S(2)}, u32[]{:S(2)}) collective-permute-start(bf16[2,288,512]{2,1,0:T(8,128)(2,1)S(1)} %collective-permute-done.19.refs_9_), channel_id=1, source_target_pairs={{0,16},{16,32},{32,48},{48,0},{1,17},{17,33},{33,49},{49,1},{2,18}... | collective-permute-start | bytes 1769480 | tf_op jit(solution)/shard_map/ppermute | solution.py:27
  155.2 16.5 %collective-permute-start.23 = (bf16[2,288,512]{2,1,0:T(8,128)(2,1)S(1)}, bf16[2,288,512]{2,1,0:T(8,128)(2,1)}, u32[]{:S(2)}, u32[]{:S(2)}) collective-permute-start(bf16[2,288,512]{2,1,0:T(8,128)(2,1)S(1)} %collective-permute-done.19.refs_9_), channel_id=1, source_target_pairs={{0,48},{16,0},{32,16},{48,32},{1,49},{17,1},{33,17},{49,33},{2,50}... | collective-permute-start | bytes 1769480 | tf_op jit(solution)/shard_map/ppermute | solution.py:27
  158.5 13.2 %collective-permute-start.24 = (bf16[512,256]{1,0:T(8,128)(2,1)}, bf16[512,256]{1,0:T(8,128)(2,1)S(1)}, u32[]{:S(2)}, u32[]{:S(2)}) collective-permute-start(bf16[512,256]{1,0:T(8,128)(2,1)} %get-tuple-element.94), channel_id=1, source_target_pairs={{0,128},{64,192},{128,0},{192,64},{1,129},{65,193},{129,1},{193,65... | collective-permute-start | bytes 786440 | tf_op jit(solution)/shard_map/ppermute | solution.py:27
  172.4 15.8 %collective-permute-start.25 = (bf16[2,288,512]{2,1,0:T(8,128)(2,1)S(1)}, bf16[2,288,512]{2,1,0:T(8,128)(2,1)S(1)}, u32[]{:S(2)}, u32[]{:S(2)}) collective-permute-start(bf16[2,288,512]{2,1,0:T(8,128)(2,1)S(1)} %collective-permute-done.20.refs_16_), channel_id=1, source_target_pairs={{0,16},{16,32},{32,48},{48,0},{1,17},{17,33},{33,49},{49,1},{2,18}... | collective-permute-start | bytes 1769480 | tf_op jit(solution)/shard_map/ppermute | solution.py:27
  172.4 16.5 %collective-permute-start.26 = (bf16[2,288,512]{2,1,0:T(8,128)(2,1)}, bf16[2,288,512]{2,1,0:T(8,128)(2,1)S(1)}, u32[]{:S(2)}, u32[]{:S(2)}) collective-permute-start(bf16[2,288,512]{2,1,0:T(8,128)(2,1)} %collective-permute-done.23.refs_19_), channel_id=1, source_target_pairs={{0,48},{16,0},{32,16},{48,32},{1,49},{17,1},{33,17},{49,33},{2,50}... | collective-permute-start | bytes 1769480 | tf_op jit(solution)/shard_map/ppermute | solution.py:27
  175.7 11.3 %collective-permute-start.27 = (bf16[512,256]{1,0:T(8,128)(2,1)}, bf16[512,256]{1,0:T(8,128)(2,1)S(1)}, u32[]{:S(2)}, u32[]{:S(2)}) collective-permute-start(bf16[512,256]{1,0:T(8,128)(2,1)} %get-tuple-element.100), channel_id=1, source_target_pairs={{0,64},{64,128},{128,192},{192,0},{1,65},{65,129},{129,193},{193,1... | collective-permute-start | bytes 786440 | tf_op jit(solution)/shard_map/ppermute | solution.py:27
  175.7 12.6 %collective-permute-start.28 = (bf16[512,256]{1,0:T(8,128)(2,1)}, bf16[512,256]{1,0:T(8,128)(2,1)S(1)}, u32[]{:S(2)}, u32[]{:S(2)}) collective-permute-start(bf16[512,256]{1,0:T(8,128)(2,1)} %get-tuple-element.101), channel_id=1, source_target_pairs={{0,192},{64,0},{128,64},{192,128},{1,193},{65,1},{129,65},{193,129... | collective-permute-start | bytes 786440 | tf_op jit(solution)/shard_map/ppermute | solution.py:27
  180.1 8.9 %copy-start.18 = (bf16[512,256]{1,0:T(8,128)(2,1)S(1)}, bf16[512,256]{1,0:T(8,128)(2,1)}, u32[]{:S(2)}) copy-start(bf16[512,256]{1,0:T(8,128)(2,1)} %copy-done.17) | copy-start | bytes 786436
  188.9 2.1 copy-start.13
  197.0 35.1 %collective-permute-start.29 = (f32[256,640]{1,0:T(8,128)S(1)}, f32[256,640]{1,0:T(8,128)S(1)}, u32[]{:S(2)}, u32[]{:S(2)}) collective-permute-start(f32[256,640]{1,0:T(8,128)S(1)} %slice_bitcast_fusion), channel_id=1, source_target_pairs={{0,8},{8,0},{1,9},{9,1},{2,10},{10,2},{3,11},{11,3},{4,12},{12,4},... | collective-permute-start | bytes 1966088 | tf_op jit(solution)/shard_map/ppermute | solution.py:27
  198.2 27.6 %collective-permute-start.30 = (bf16[256,256]{1,0:T(8,128)(2,1)S(1)}, bf16[256,256]{1,0:T(8,128)(2,1)S(1)}, u32[]{:S(2)}, u32[]{:S(2)}) collective-permute-start(bf16[256,256]{1,0:T(8,128)(2,1)S(1)} %get-tuple-element.133), channel_id=1, source_target_pairs={{0,8},{1,40},{2,72},{3,104},{4,136},{5,168},{6,200},{7,232},{8,16}... | collective-permute-start | bytes 393224 | tf_op jit(solution)/shard_map/ppermute | solution.py:438
  199.9 29.2 %collective-permute-start.31 = (bf16[256,256]{1,0:T(8,128)(2,1)S(1)}, bf16[256,256]{1,0:T(8,128)(2,1)S(1)}, u32[]{:S(2)}, u32[]{:S(2)}) collective-permute-start(bf16[256,256]{1,0:T(8,128)(2,1)S(1)} %get-tuple-element.132), channel_id=1, source_target_pairs={{0,0},{1,56},{2,88},{3,120},{4,152},{5,184},{6,216},{7,248},{8,8},... | collective-permute-start | bytes 393224 | tf_op jit(solution)/shard_map/ppermute | solution.py:438
  225.8 3.3 %copy-start.20 = (bf16[256,256]{1,0:T(8,128)(2,1)}, bf16[256,256]{1,0:T(8,128)(2,1)S(1)}, u32[]{:S(2)}) copy-start(bf16[256,256]{1,0:T(8,128)(2,1)S(1)} %collective-permute-done.30.r0) | copy-start | bytes 393220
  (11 other events, 12.9 us)

commit v2 on v1

--- a/solution.py
+++ b/solution.py
@@ -63,104 +63,146 @@
 
 
 def block_body(role, table, q, kt, *refs):
-    n = q.shape[0]
-    outs = refs[-2:] if role == "far" else refs[-1:]
-    p = pl.program_id(0)
-
-    def value(span, home):
-        home = home[...]
-        if role == "pack":
-            return home
-        x = jnp.where(table[1] == 1, home, refs[0][0, span])
+    side = kt.shape[0]
+    width = q.shape[1]
+    n = q.shape[0] // (4 * NY)
+    piece, high = n // 2, side // 2
+    if role == "quarter":
+        there, c, d, out, found, turned, sems = refs
+    elif role == "far":
+        there, *outs, sems = refs
+    elif role == "relay":
+        there, relay, out, sems = refs
+    else:
+        out, sems = refs
+    if role in ("pack", "relay"):
+        outs = [out.at[0], out.at[1]]
+
+    def home(p):
+        at = 2 * table[0] + p
+        rows = q.at[pl.ds(pl.multiple_of(at * n, n), n), :]
+        return rows, kt.at[:, pl.ds(pl.multiple_of(at * width, width), width)]
+
+    def received(x, p):
+        return x.at[p, pl.ds(0, n), :], x.at[p, pl.ds(n, side), :]
+
+    def run(pairs):
+        copies = [pltpu.make_async_copy(a, b, sems.at[i]) for i, (a, b) in enumerate(pairs)]
+        for copy in copies:
+            copy.start()
+        for copy in copies:
+            copy.wait()
+
+    def put(p, source):
+        rows, keys = source
+        if role == "quarter":
+            pairs = [
+                (rows.at[pl.ds(i * piece, piece), :], out.at[2 * p + i, pl.ds(0, piece), :])
+                for i in range(2)
+            ]
+            return pairs + [(keys, found.at[p])]
+        to = outs[p]
+        return [(rows, to.at[pl.ds(0, n), :]), (keys, to.at[pl.ds(n, side), :])]
+
+    def choose(cases):
+        left = True
+        for when, pairs in cases:
+            pl.when(when & left)(functools.partial(run, pairs))
+            left = left & ~when
+
+    yes = table[0] >= 0
+    if role == "pack":
+        run(put(0, home(0)) + put(1, home(1)))
+    elif role in ("far", "relay"):
+        cases = [
+            (table[1] == 1, put(0, home(0)) + put(1, home(1))),
+            (yes, [(there.at[p], outs[p]) for p in range(2)]),
+        ]
         if role == "relay":
-            x = jnp.where(table[2] == 1, refs[1][span], x)
-        if role == "quarter":
-            got = jnp.where(table[3 + p] == 1, refs[1][0, span], refs[2][0, span])
-            x = jnp.where(table[2] == 1, x, got)
-        return x
-
-    rows, side = value(slice(0, n), q), value(slice(n, n + kt.shape[0]), kt)
-    if role == "far":
-        for index, out in enumerate(outs):
-
-            @pl.when(p == index)
-            def _():
-                out[:n] = rows
-                out[n:] = side
-
-    elif role == "quarter":
-        piece, high = n // 2, kt.shape[0] // 2
-        for i in range(2):
-            span = slice(i * piece, (i + 1) * piece)
-            outs[0][i, :piece] = rows[span]
-            outs[0][i, piece:] = jnp.concatenate([side[:high, span], side[high:, span]], axis=1)
+            cases = [(table[2] == 1, [(relay, outs[p]) for p in range(2)])] + cases
+        choose(cases)
     else:
-        outs[0][0, :n] = rows
-        outs[0][0, n:] = side
+        for p in range(2):
+            mine = table[2] == 1
+            choose(
+                [
+                    (mine & (table[1] == 1), put(p, home(p))),
+                    (mine, put(p, received(there, p))),
+                    (table[3 + p] == 1, put(p, received(c, p))),
+                    (yes, put(p, received(d, p))),
+                ]
+            )
+        for p in range(2):
+            for i in range(2):
+                span = slice(i * piece, (i + 1) * piece)
+                turned[2 * p + i] = jnp.concatenate(
+                    [found[p, :high, span], found[p, high:, span]], axis=1
+                )
+        run([(turned.at[i], out.at[i, pl.ds(piece, high), :]) for i in range(4)])
 
 
 def weight_block(role, table, q, kt, *more):
     width, side = q.shape[1], kt.shape[0]
-    n = q.shape[0] // (4 * NY)
-    rows = n + side
-    pair = pl.BlockSpec((1, rows, width), lambda p, tab: (p, 0, 0))
-    single = pl.BlockSpec((rows, width), lambda p, tab: (0, 0))
-    ins = [
-        pl.BlockSpec((n, width), lambda p, tab: (2 * tab[0] + p, 0)),
-        pl.BlockSpec((side, width), lambda p, tab: (0, 2 * tab[0] + p)),
-    ] + [pair if x.ndim == 3 else single for x in more]
+    rows = q.shape[0] // (4 * NY) + side
     shape = lambda *dims: jax.ShapeDtypeStruct(dims, bf16)
-    if role == "far":
-        outs, shapes = [single, single], [shape(rows, width)] * 2
-    elif role == "quarter":
-        outs = pl.BlockSpec((2, rows // 2, width), lambda p, tab: (p, 0, 0))
-        shapes = shape(4, rows // 2, width)
-    else:
-        outs, shapes = pair, shape(2, rows, width)
-    return pl.pallas_call(
+    shapes = {"far": [shape(rows, width)] * 2, "quarter": [shape(4, rows // 2, width)]}
+    shapes = shapes.get(role, [shape(2, rows, width)])
+    scratch = [pltpu.SemaphoreType.DMA((4,))]
+    if role == "quarter":
+        scratch = [
+            pltpu.VMEM((2, side, width), bf16),
+            pltpu.VMEM((4, side // 2, width), bf16),
+        ] + scratch
+    anywhere = pl.BlockSpec(memory_space=pl.ANY)
+    out = pl.pallas_call(
         functools.partial(block_body, role),
         grid_spec=pltpu.PrefetchScalarGridSpec(
-            num_scalar_prefetch=1, grid=(2,), in_specs=ins, out_specs=outs
+            num_scalar_prefetch=1,
+            grid=(1,),
+            in_specs=[anywhere] * (2 + len(more)),
+            out_specs=[anywhere] * len(shapes),
+            scratch_shapes=scratch,
         ),
         out_shape=shapes,
         cost_estimate=pl.CostEstimate(
-            flops=0, bytes_accessed=4 * rows * width * (2 + len(more)), transcendentals=0
+            flops=0, bytes_accessed=8 * rows * width, transcendentals=0
         ),
         name="block_" + role,
     )(table.astype(jnp.int32), q, kt, *more)
+    return out if role == "far" else out[0]
 
 
 def across(left, right):
     return lax.dot_general(left, right, (((0,), (0,)), ((), ())), preferred_element_type=f32)
 
 
-def gram_body(table, ca, cb, ra, rb, low, high, base, turned):
-    slot = pl.program_id(0)
+def gram_body(table, *refs):
+    cas, cbs = refs[:NZ], refs[NZ : 2 * NZ]
+    ra, rb, low, high, base, turned = refs[2 * NZ :]
+    group = pl.program_id(0)
     half = NZ // 2
-    tokens, tile = ca.shape
-
-    @pl.when(slot == 0)
+    tokens, tile = cas[0].shape
+
+    @pl.when(group == 0)
     def _():
         for n in range(4):
             span = slice(n * tile, (n + 1) * tile)
             turned[n, :, :tokens] = ra[:, span].T
             turned[n, :, tokens:] = rb[:, span].T
 
-    columns = jnp.concatenate([ca[...], cb[...]], axis=0)
-    rows = [turned[table[n, slot]] for n in (1, 2)]
-    tiles = [jnp.dot(x, columns, preferred_element_type=f32) for x in rows]
-
-    @pl.when(slot < half)
-    def _():
-        low[0, :tile], low[0, tile:] = (x.astype(bf16) for x in tiles)
-
-    @pl.when((slot >= half) & (slot < NZ))
-    def _():
-        high[0, :tile], high[0, tile:] = (x.astype(bf16) for x in tiles)
-
-    @pl.when(slot >= NZ)
-    def _():
-        base[0, :tile], base[0, tile:] = tiles
+    for n in range(NZ):
+        columns = jnp.concatenate([cas[n][...], cbs[n][...]], axis=0)
+        rows = [turned[table[i, NZ * group + n]] for i in (1, 2)]
+        tiles = [jnp.dot(x, columns, preferred_element_type=f32) for x in rows]
+        far, at = (low, n) if n < half else (high, n - half)
+
+        @pl.when(group == 0)
+        def _(far=far, at=at, tiles=tiles):
+            far[at, :tile], far[at, tile:] = (x.astype(bf16) for x in tiles)
+
+        @pl.when(group > 0)
+        def _(n=n, tiles=tiles):
+            base[n, :tile], base[n, tile:] = tiles
 
 
 def gram(table, mine, other):
@@ -168,21 +210,20 @@
     n = table.shape[1]
     tile = depth // (NY * NZ * 2)
     half = NZ // 2
-    cols = pl.BlockSpec((tokens, tile), lambda s, tab: (0, tab[0, s]))
+    cols = [
+        pl.BlockSpec((tokens, tile), lambda s, tab, i=i: (0, tab[0, NZ * s + i])) for i in range(NZ)
+    ]
     rows = pl.BlockSpec((tokens, 4 * tile), lambda s, tab: (0, tab[3, 0]))
-    block = (1, 2 * tile, tile)
+    fixed = pl.BlockSpec((half, 2 * tile, tile), lambda s, tab: (0, 0, 0))
+    moving = pl.BlockSpec((NZ, 2 * tile, tile), lambda s, tab: (jnp.maximum(s - 1, 0), 0, 0))
     shape = lambda n, kind: jax.ShapeDtypeStruct((n, 2 * tile, tile), kind)
     return pl.pallas_call(
         gram_body,
         grid_spec=pltpu.PrefetchScalarGridSpec(
             num_scalar_prefetch=1,
-            grid=(n,),
-            in_specs=[cols, cols, rows, rows],
-            out_specs=[
-                pl.BlockSpec(block, lambda s, tab: (jnp.minimum(s, half - 1), 0, 0)),
-                pl.BlockSpec(block, lambda s, tab: (jnp.clip(s - half, 0, half - 1), 0, 0)),
-                pl.BlockSpec(block, lambda s, tab: (jnp.maximum(s - NZ, 0), 0, 0)),
-            ],
+            grid=(n // NZ,),
+            in_specs=cols + cols + [rows, rows],
+            out_specs=[fixed, fixed, moving],
             scratch_shapes=[pltpu.VMEM((4, tile, 2 * tokens), bf16)],
         ),
         out_shape=[shape(half, bf16), shape(half, bf16), shape(n - NZ, f32)],
@@ -192,7 +233,7 @@
             transcendentals=0,
         ),
         name="gram",
-    )(table, mine, other, mine, other)
+    )(table, *[mine] * NZ, *[other] * NZ, mine, other)
 
 
 def project_body(slots, piece, fresh, table, *refs):
@@ -273,6 +314,7 @@
         + [full(x.shape) for x in (b, cosine, sine)],
         out_specs=[full(shape) for shape in shapes],
         out_shape=[jax.ShapeDtypeStruct(shape, bf16) for shape in shapes],
+        compiler_params=pltpu.CompilerParams(vmem_limit_bytes=12 * 2**20),
         name="rope",
     )(at, a, b, cosine, sine)
 
@@ -296,6 +338,7 @@
         functools.partial(assemble_body, scale),
         in_specs=[pl.BlockSpec(memory_space=pltpu.SMEM)] + [pl.BlockSpec(memory_space=pltpu.VMEM)] * 4,
         out_shape=jax.ShapeDtypeStruct((4 * tile, tile), f32),
+        compiler_params=pltpu.CompilerParams(vmem_limit_bytes=12 * 2**20),
         name="assemble",
     )(slots, own, r0, r1, extra)
 
@@ -357,11 +400,11 @@
     others.append(send(pack(last_k, 0), "k", 1))
     up = weight_block("relay", told(1, here, step_y == 1), q, kt, others[0], a)
     down = weight_block("relay", told(3, here, step_y == 3), q, kt, others[1], b)
-    up, down, gain = together((up, down, norm_gain))
+    up, down, gain, ours = together((up, down, norm_gain, hidden))
     c = send(up, "y", 1)
     d = send(down, "y", -1)
 
-    mine = normalize(hidden, gain)
+    mine = normalize(ours, gain)
     other = normalize(theirs, gain)
 
     zs = (z + jnp.arange(NZ)) % NZ

time: 239 us -> 492 us (2.06)
  Pallas kernels: 58.2 us -> 325 us
  waiting for transfers between devices: 89.2 us -> 79.6 us
    pallas_call x8, Pallas kernels: 22.8 us -> 296 us  [weight_block(): pl.pallas_call(functools.partial(block_body, role), grid_spec=pltpu.Prefe...]
    ppermute x23, waiting for transfers between devices: 30.4 us -> 19 us  [send(): return lax.ppermute(array, axis, [(i, (i + shift) % n) for i in range(n)])]
    unnamed x54 -> x44, local copies, waits for them, and re-layouts: 10 us -> 8 us
  transfers between devices with their start and end apart: 32 -> 32, of which waited for: 14 -> 13; matrix products, arithmetic and copies ran while one was open for 11% -> 4% of each run, Pallas kernels for 17% -> 35%
where the time goes in v2:
time: 492 us; the launch traced here: 489 us
  Pallas kernels  325 us (66%)
  waiting for transfers between devices  79.6 us (16%)
  starting transfers between devices  46.4 us (9%)
  other arithmetic  21.4 us (4%)
  local copies, waits for them, and re-layouts  14.6 us (3%)
    pallas_call x8, Pallas kernels, weight_block(): pl.pallas_call(functools.partial(block_body, role), grid_spec=pltpu.Prefe...  296 us
    ppermute x7, waiting for transfers between devices, swap(): return lax.ppermute(array, axis, [(i, i ^ bit) for i in range(SIZES[axis])])  38.1 us
    ppermute x23, starting transfers between devices, send(): return lax.ppermute(array, axis, [(i, (i + shift) % n) for i in range(n)])  30.8 us
    ppermute x2, waiting for transfers between devices, shards(): lax.ppermute(jnp.where(second, tiles[1], tiles[0]), ALL, partner_moves(n))  22.5 us
    ppermute x23, waiting for transfers between devices, send(): return lax.ppermute(array, axis, [(i, (i + shift) % n) for i in range(n)])  19 us
    pallas_call x3, Pallas kernels, project(): pl.pallas_call(functools.partial(project_body, slots, piece, fresh), grid...  15.6 us
    pallas_call x1, Pallas kernels, gram(): pl.pallas_call(gram_body, grid_spec=pltpu.PrefetchScalarGridSpec(num_scal...  10.8 us
  transfers between devices with their start and end apart: 32, of which 13 were waited for; matrix products, arithmetic and copies ran while one was open for 4% of the time, Pallas kernels for 35%

profile of v2, /device:TPU:132, one launch (start us, length us, event | category | flops | bytes accessed | tf_op | source)
XLA Modules:
  0.0 489.1 jit_solution(951060050429113456)
XLA Ops:
  0.6 36.9 %block_pack.4 = bf16[2,576,512]{2,1,0:T(8,128)(2,1)} custom-call(s32[1]{0:T(128)} %bitcast.10.table, bf16[8192,512]{1,0:T(8,128)(2,1)} %bitcast.54, bf16[64,8192]{1,0:T(8,128)(2,1)} %bitcast.62), custom_call_target="tpu_custom_call" | custom-call | bytes 2359296 | tf_op jit(solution)/shard_map/block_pack/pallas_call | solution.py:157
  39.0 1.7 collective-permute-done.refs_0_
  41.7 37.5 %block_far.1 = (bf16[576,512]{1,0:T(8,128)(2,1)}, bf16[576,512]{1,0:T(8,128)(2,1)}) custom-call(s32[2]{0:T(128)} %pad_add_fusion.3.table, bf16[8192,512]{1,0:T(8,128)(2,1)} %bitcast.55, bf16[64,8192]{1,0:T(8,128)(2,1)} %bitcast.63, bf16[2,576,512]{2,1,0:T(8,128)(2,1)} %copy-done.11), custom_call_target="tpu_custom_call" | custom-call | bytes 2359296 | tf_op jit(solution)/shard_map/block_far/pallas_call | solution.py:157
  79.3 36.9 %block_pack.6 = bf16[2,576,512]{2,1,0:T(8,128)(2,1)} custom-call(s32[1]{0:T(128)} %bitcast.12.table, bf16[8192,512]{1,0:T(8,128)(2,1)} %bitcast.56, bf16[64,8192]{1,0:T(8,128)(2,1)} %bitcast.64), custom_call_target="tpu_custom_call" | custom-call | bytes 2359296 | tf_op jit(solution)/shard_map/block_pack/pallas_call | solution.py:157
  116.2 36.9 %block_pack.5 = bf16[2,576,512]{2,1,0:T(8,128)(2,1)} custom-call(s32[1]{0:T(128)} %bitcast.11.table, bf16[8192,512]{1,0:T(8,128)(2,1)} %bitcast.57, bf16[64,8192]{1,0:T(8,128)(2,1)} %bitcast.65), custom_call_target="tpu_custom_call" | custom-call | bytes 2359296 | tf_op jit(solution)/shard_map/block_pack/pallas_call | solution.py:157
  153.9 3.1 collective-permute-start.4
  157.8 36.9 %block_pack.7 = bf16[2,576,512]{2,1,0:T(8,128)(2,1)} custom-call(s32[1]{0:T(128)} %bitcast.20.table, bf16[8192,512]{1,0:T(8,128)(2,1)} %bitcast.58, bf16[64,8192]{1,0:T(8,128)(2,1)} %bitcast.66), custom_call_target="tpu_custom_call" | custom-call | bytes 2359296 | tf_op jit(solution)/shard_map/block_pack/pallas_call | solution.py:157
  196.0 37.5 %block_relay.3 = bf16[2,576,512]{2,1,0:T(8,128)(2,1)} custom-call(s32[3]{0:T(128)} %get-tuple-element.152.table, bf16[8192,512]{1,0:T(8,128)(2,1)} %bitcast.59, bf16[64,8192]{1,0:T(8,128)(2,1)} %bitcast.67, bf16[2,576,512]{2,1,0:T(8,128)(2,1)} %copy-done.7, bf16[576,512]{1,0:T(8,128)(2,1)} %collective-permute-done.4.refs_1_), custom_call_target="tpu_custom_call" | custom-call | bytes 2359296 | tf_op jit(solution)/shard_map/block_relay/pallas_call | solution.py:157
  234.6 37.7 %block_relay.2 = bf16[2,576,512]{2,1,0:T(8,128)(2,1)} custom-call(s32[3]{0:T(128)} %get-tuple-element.151.table, bf16[8192,512]{1,0:T(8,128)(2,1)} %bitcast.60, bf16[64,8192]{1,0:T(8,128)(2,1)} %bitcast.68, bf16[2,576,512]{2,1,0:T(8,128)(2,1)} %copy-done.6, bf16[576,512]{1,0:T(8,128)(2,1)} %collective-permute-done.2.refs_1_), custom_call_target="tpu_custom_call" | custom-call | bytes 2359296 | tf_op jit(solution)/shard_map/block_relay/pallas_call | solution.py:157
  272.3 3.3 collective-permute-start.10
  275.6 3.1 fusion
  278.7 3.1 fusion.3
  281.9 4.0 fusion.5
  286.1 1.8 copy-done.1
  290.8 4.0 collective-permute-done.6
  294.9 1.7 collective-permute-start.7
  296.6 10.8 %gram.1 = (bf16[2,512,256]{2,1,0:T(8,128)(2,1)}, bf16[2,512,256]{2,1,0:T(8,128)(2,1)}, f32[12,512,256]{2,1,0:T(8,128)}) custom-call(s32[4,16]{1,0:T(4,128)} %pad_add_fusion.table, bf16[256,8192]{1,0:T(8,128)(2,1)} %copy-done.2, bf16[256,8192]{1,0:T(8,128)(2,1)} %copy-done.2, bf16[256,8192]{1,0:T(8,128)(2,1)} %copy-done.2, bf16[256,8192]{1,0:T(8,128)(2,1)} %copy-done.2, ...), custom_call_target="tpu_custom_call" | custom-call | flops 4294967296 | bytes 16777216 | tf_op jit(solution)/shard_map/gram/pallas_call | solution.py:220
  309.2 35.3 %block_quarter.1 = bf16[4,288,512]{2,1,0:T(8,128)(2,1)} custom-call(s32[5]{0:T(128)} %stack.121.table, bf16[8192,512]{1,0:T(8,128)(2,1)} %bitcast.61, bf16[64,8192]{1,0:T(8,128)(2,1)} %bitcast.69, bf16[2,576,512]{2,1,0:T(8,128)(2,1)} %collective-permute-done.8.refs_0_, bf16[2,576,512]{2,1,0:T(8,128)(2,1)} %collective-permute-done.9.refs_1_, ...), custom_call_target="tpu_custom_call" | custom-call | bytes 2359296 | tf_op jit(solution)/shard_map/block_quarter/pallas_call | solution.py:157
  346.8 2.0 collective-permute-start.11
  348.8 1.2 collective-permute-start.12
  350.0 2.5 fusion.29
  352.6 8.4 %collective-permute-done.11 = bf16[2,512,256]{2,1,0:T(8,128)(2,1)S(1)} collective-permute-done((bf16[2,512,256]{2,1,0:T(8,128)(2,1)}, bf16[2,512,256]{2,1,0:T(8,128)(2,1)S(1)}, u32[]{:S(2)}, u32[]{:S(2)}) %collective-permute-start.11) | collective-permute-done | bytes 524320 | tf_op jit(solution)/shard_map/ppermute | solution.py:27
  361.6 1.6 add_convert_fusion
  363.3 1.8 collective-permute-start.16
  365.2 1.5 collective-permute-start.17
  366.7 1.5 collective-permute-start.15
  369.2 21.9 %collective-permute-done.18 = bf16[256,256]{1,0:T(8,128)(2,1)S(1)} collective-permute-done((bf16[256,256]{1,0:T(8,128)(2,1)S(1)}, bf16[256,256]{1,0:T(8,128)(2,1)S(1)}, u32[]{:S(2)}, u32[]{:S(2)}) %collective-permute-start.18) | collective-permute-done | bytes 131104 | tf_op jit(solution)/shard_map/ppermute | solution.py:31
  391.2 1.4 collective-permute-done.15
  392.7 3.4 fusion.8
  396.7 2.8 collective-permute-start.21
  400.1 10.8 %collective-permute-done.19.refs_9_ = bf16[2,288,512]{2,1,0:T(8,128)(2,1)S(1)} collective-permute-done((bf16[2,288,512]{2,1,0:T(8,128)(2,1)S(1)}, bf16[2,288,512]{2,1,0:T(8,128)(2,1)S(1)}, u32[]{:S(2)}, u32[]{:S(2)}) %collective-permute-start.19) | collective-permute-done | bytes 589856 | tf_op jit(solution)/shard_map/ppermute | solution.py:31
  410.9 1.3 collective-permute-done.20.refs_16_
  413.0 3.2 collective-permute-start.23
  416.3 3.2 collective-permute-start.24
  420.1 4.4 project.3.refs_20_
  424.5 4.9 collective-permute-done.24
  429.5 3.2 collective-permute-start.26
  432.8 3.7 collective-permute-start.28
  437.1 6.3 %project.4.refs_10_ = f32[2,256,640]{2,1,0:T(8,128)} custom-call(s32[8]{0:T(128)} %pad_add_fusion.5.table, bf16[256,8192]{1,0:T(8,128)(2,1)} %copy-done.2, bf16[256,8192]{1,0:T(8,128)(2,1)} %copy-done.2, bf16[256,8192]{1,0:T(8,128)(2,1)} %copy-done.2, bf16[256,8192]{1,0:T(8,128)(2,1)} %copy-done.2, bf16[256,8192]{1,0:T(8,128)(2,1)} %copy-done.2, ...), custom_call_target="tpu_custom_call" | custom-call | flops 1073741824 | bytes 4718592 | tf_op jit(solution)/shard_map/project/pallas_call | solution.py:271
  443.9 1.7 collective-permute-done.28
  445.7 1.6 fusion.28
  447.3 4.8 project.5.a
  452.2 2.1 slice_bitcast_fusion
  454.5 1.4 collective-permute-start.30
  456.0 7.8 %collective-permute-start.31 = (bf16[256,256]{1,0:T(8,128)(2,1)S(1)}, bf16[256,256]{1,0:T(8,128)(2,1)S(1)}, u32[]{:S(2)}, u32[]{:S(2)}) collective-permute-start(bf16[256,256]{1,0:T(8,128)(2,1)S(1)} %get-tuple-element.134), channel_id=1, source_target_pairs={{0,0},{1,56},{2,88},{3,120},{4,152},{5,184},{6,216},{7,248},{8,8},... | collective-permute-start | bytes 393224 | tf_op jit(solution)/shard_map/ppermute | solution.py:481
  463.8 18.4 %collective-permute-done.30.r0 = bf16[256,256]{1,0:T(8,128)(2,1)S(1)} collective-permute-done((bf16[256,256]{1,0:T(8,128)(2,1)S(1)}, bf16[256,256]{1,0:T(8,128)(2,1)S(1)}, u32[]{:S(2)}, u32[]{:S(2)}) %collective-permute-start.30) | collective-permute-done | bytes 131104 | tf_op jit(solution)/shard_map/ppermute | solution.py:481
  482.2 4.0 collective-permute-done.31.r1
  486.3 1.7 assemble.1
  (122 shorter events, 20.2 us)
Async XLA Ops:
  37.5 3.1 collective-permute-start
  116.2 37.1 %copy-start.9 = (bf16[2,576,512]{2,1,0:T(8,128)(2,1)S(1)}, bf16[2,576,512]{2,1,0:T(8,128)(2,1)}, u32[]{:S(2)}) copy-start(bf16[2,576,512]{2,1,0:T(8,128)(2,1)} %block_pack.6) | copy-start | bytes 3538948
  116.2 37.6 %copy-start.21 = (s32[4]{0:T(128)S(1)}, s32[4]{0:T(128)}, u32[]{:S(2)}) copy-start(s32[4]{0:T(128)} %constant.317.clone) | copy-start | bytes 52
  153.1 125.6 %collective-permute-start.5 = (bf16[256,8192]{1,0:T(8,128)(2,1)}, bf16[256,8192]{1,0:T(8,128)(2,1)}, u32[]{:S(2)}, u32[]{:S(2)}) collective-permute-start(bf16[256,8192]{1,0:T(8,128)(2,1)} %param.7), channel_id=1, source_target_pairs={{0,8},{8,0},{1,9},{9,1},{2,10},{10,2},{3,11},{11,3},{4,12},{12,4},... | collective-permute-start | bytes 12582920 | tf_op jit(solution)/shard_map/ppermute | solution.py:27
  153.3 41.6 %collective-permute-start.3 = (bf16[2,576,512]{2,1,0:T(8,128)(2,1)S(1)}, bf16[2,576,512]{2,1,0:T(8,128)(2,1)S(1)}, u32[]{:S(2)}, u32[]{:S(2)}) collective-permute-start(bf16[2,576,512]{2,1,0:T(8,128)(2,1)S(1)} %copy-done.9), channel_id=1, source_target_pairs={{0,8},{8,0},{1,9},{9,1},{2,10},{10,2},{3,11},{11,3},{4,12},{12,4},... | collective-permute-start | bytes 3538952 | tf_op jit(solution)/shard_map/ppermute | solution.py:27
  153.7 79.9 %collective-permute-start.1 = (bf16[2,576,512]{2,1,0:T(8,128)(2,1)}, bf16[2,576,512]{2,1,0:T(8,128)(2,1)S(1)}, u32[]{:S(2)}, u32[]{:S(2)}) collective-permute-start(bf16[2,576,512]{2,1,0:T(8,128)(2,1)} %block_pack.5), channel_id=1, source_target_pairs={{0,8},{8,0},{1,9},{9,1},{2,10},{10,2},{3,11},{11,3},{4,12},{12,4},... | collective-permute-start | bytes 3538952 | tf_op jit(solution)/shard_map/ppermute | solution.py:27
  153.9 40.9 %collective-permute-start.4 = (bf16[576,512]{1,0:T(8,128)(2,1)}, bf16[576,512]{1,0:T(8,128)(2,1)}, u32[]{:S(2)}, u32[]{:S(2)}) collective-permute-start(bf16[576,512]{1,0:T(8,128)(2,1)} %get-tuple-element.68), channel_id=1, source_target_pairs={{0,48},{16,0},{32,16},{48,32},{1,49},{17,1},{33,17},{49,33},{2,50}... | collective-permute-start | bytes 1769480 | tf_op jit(solution)/shard_map/ppermute | solution.py:27
  157.0 76.6 %collective-permute-start.2 = (bf16[576,512]{1,0:T(8,128)(2,1)}, bf16[576,512]{1,0:T(8,128)(2,1)}, u32[]{:S(2)}, u32[]{:S(2)}) collective-permute-start(bf16[576,512]{1,0:T(8,128)(2,1)} %get-tuple-element.66), channel_id=1, source_target_pairs={{0,16},{16,32},{32,48},{48,0},{1,17},{17,33},{33,49},{49,1},{2,18}... | collective-permute-start | bytes 1769480 | tf_op jit(solution)/shard_map/ppermute | solution.py:27
  194.7 113.5 %collective-permute-start.8 = (bf16[2,576,512]{2,1,0:T(8,128)(2,1)}, bf16[2,576,512]{2,1,0:T(8,128)(2,1)}, u32[]{:S(2)}, u32[]{:S(2)}) collective-permute-start(bf16[2,576,512]{2,1,0:T(8,128)(2,1)} %block_pack.7), channel_id=1, source_target_pairs={{0,8},{8,0},{1,9},{9,1},{2,10},{10,2},{3,11},{11,3},{4,12},{12,4},... | collective-permute-start | bytes 3538952 | tf_op jit(solution)/shard_map/ppermute | solution.py:27
  234.6 37.7 %copy-start.8 = (bf16[2,576,512]{2,1,0:T(8,128)(2,1)S(1)}, bf16[2,576,512]{2,1,0:T(8,128)(2,1)}, u32[]{:S(2)}) copy-start(bf16[2,576,512]{2,1,0:T(8,128)(2,1)} %block_relay.3) | copy-start | bytes 3538948
  272.3 9.5 %copy-start.3 = (bf16[256,8192]{1,0:T(8,128)(2,1)S(1)}, bf16[256,8192]{1,0:T(8,128)(2,1)}, u32[]{:S(2)}) copy-start(bf16[256,8192]{1,0:T(8,128)(2,1)} %param.7) | copy-start | bytes 12582916
  272.3 9.5 %copy-start.19 = (f32[8192]{0:T(1024)S(1)}, f32[8192]{0:T(1024)}, u32[]{:S(2)}) copy-start(f32[8192]{0:T(1024)} %param.8) | copy-start | bytes 98308
  272.3 35.9 %collective-permute-start.10 = (bf16[2,576,512]{2,1,0:T(8,128)(2,1)S(1)}, bf16[2,576,512]{2,1,0:T(8,128)(2,1)S(1)}, u32[]{:S(2)}, u32[]{:S(2)}) collective-permute-start(bf16[2,576,512]{2,1,0:T(8,128)(2,1)S(1)} %copy-done.8), channel_id=1, source_target_pairs={{0,48},{16,0},{32,16},{48,32},{1,49},{17,1},{33,17},{49,33},{2,50}... | collective-permute-start | bytes 3538952 | tf_op jit(solution)/shard_map/ppermute | solution.py:27
  275.6 32.6 %collective-permute-start.9 = (bf16[2,576,512]{2,1,0:T(8,128)(2,1)}, bf16[2,576,512]{2,1,0:T(8,128)(2,1)}, u32[]{:S(2)}, u32[]{:S(2)}) collective-permute-start(bf16[2,576,512]{2,1,0:T(8,128)(2,1)} %block_relay.2), channel_id=1, source_target_pairs={{0,16},{16,32},{32,48},{48,0},{1,17},{17,33},{33,49},{49,1},{2,18}... | collective-permute-start | bytes 3538952 | tf_op jit(solution)/shard_map/ppermute | solution.py:27
  285.9 2.0 copy-start.1
  285.9 3.3 copy-start.2
  289.2 5.6 %collective-permute-start.6 = (bf16[256,256]{1,0:T(8,128)(2,1)S(1)}, bf16[256,256]{1,0:T(8,128)(2,1)S(1)}, u32[]{:S(2)}, u32[]{:S(2)}) collective-permute-start(bf16[256,256]{1,0:T(8,128)(2,1)S(1)} %get-tuple-element.145), channel_id=1, source_target_pairs={{0,64},{64,0},{128,192},{192,128},{1,65},{65,1},{129,193},{193,129... | collective-permute-start | bytes 393224 | tf_op jit(solution)/shard_map/ppermute | solution.py:31
  294.9 12.5 %collective-permute-start.7 = (bf16[256,256]{1,0:T(8,128)(2,1)S(1)}, bf16[256,256]{1,0:T(8,128)(2,1)S(1)}, u32[]{:S(2)}, u32[]{:S(2)}) collective-permute-start(bf16[256,256]{1,0:T(8,128)(2,1)S(1)} %fusion.9), channel_id=1, source_target_pairs={{0,128},{64,192},{128,0},{192,64},{1,129},{65,193},{129,1},{193,65... | collective-permute-start | bytes 393224 | tf_op jit(solution)/shard_map/ppermute | solution.py:31
  307.5 45.1 %collective-permute-start.14 = (bf16[256,256]{1,0:T(8,128)(2,1)S(1)}, bf16[256,256]{1,0:T(8,128)(2,1)S(1)}, u32[]{:S(2)}, u32[]{:S(2)}) collective-permute-start(bf16[256,256]{1,0:T(8,128)(2,1)S(1)} %convert_element_type.166), channel_id=1, source_target_pairs={{0,16},{16,0},{32,48},{48,32},{1,17},{17,1},{33,49},{49,33},{2,18}... | collective-permute-start | bytes 393224 | tf_op jit(solution)/shard_map/ppermute | solution.py:31
  345.7 17.6 %collective-permute-start.13 = (bf16[2,288,512]{2,1,0:T(8,128)(2,1)S(1)}, bf16[2,288,512]{2,1,0:T(8,128)(2,1)S(1)}, u32[]{:S(2)}, u32[]{:S(2)}) collective-permute-start(bf16[2,288,512]{2,1,0:T(8,128)(2,1)S(1)} %dynamic-slice_bitcast_fusion), channel_id=1, source_target_pairs={{0,64},{64,0},{128,192},{192,128},{1,65},{65,1},{129,193},{193,129... | collective-permute-start | bytes 1769480 | tf_op jit(solution)/shard_map/ppermute | solution.py:31
  346.8 14.2 %collective-permute-start.11 = (bf16[2,512,256]{2,1,0:T(8,128)(2,1)}, bf16[2,512,256]{2,1,0:T(8,128)(2,1)S(1)}, u32[]{:S(2)}, u32[]{:S(2)}) collective-permute-start(bf16[2,512,256]{2,1,0:T(8,128)(2,1)} %get-tuple-element.82), channel_id=1, source_target_pairs={{0,16},{16,32},{32,48},{48,0},{1,17},{17,33},{33,49},{49,1},{2,18}... | collective-permute-start | bytes 1572872 | tf_op jit(solution)/shard_map/ppermute | solution.py:27
  348.8 12.7 %collective-permute-start.12 = (bf16[2,512,256]{2,1,0:T(8,128)(2,1)}, bf16[2,512,256]{2,1,0:T(8,128)(2,1)S(1)}, u32[]{:S(2)}, u32[]{:S(2)}) collective-permute-start(bf16[2,512,256]{2,1,0:T(8,128)(2,1)} %get-tuple-element.83), channel_id=1, source_target_pairs={{0,48},{16,0},{32,16},{48,32},{1,49},{17,1},{33,17},{49,33},{2,50}... | collective-permute-start | bytes 1572872 | tf_op jit(solution)/shard_map/ppermute | solution.py:27
  361.6 7.6 %copy-start.20 = (s32[256]{0:T(256)S(1)}, s32[256]{0:T(256)}, u32[]{:S(2)}) copy-start(s32[256]{0:T(256)} %param.9) | copy-start | bytes 3076
  363.3 29.3 %collective-permute-start.16 = (bf16[2,2,512,256]{3,2,1,0:T(8,128)(2,1)}, bf16[2,2,512,256]{3,2,1,0:T(8,128)(2,1)}, u32[]{:S(2)}, u32[]{:S(2)}) collective-permute-start(bf16[2,2,512,256]{3,2,1,0:T(8,128)(2,1)} %get-tuple-element.87), channel_id=1, source_target_pairs={{0,16},{16,32},{32,48},{48,0},{1,17},{17,33},{33,49},{49,1},{2,18}... | collective-permute-start | bytes 3145736 | tf_op jit(solution)/shard_map/ppermute | solution.py:27
  365.2 27.5 %collective-permute-start.17 = (bf16[2,2,512,256]{3,2,1,0:T(8,128)(2,1)S(1)}, bf16[2,2,512,256]{3,2,1,0:T(8,128)(2,1)}, u32[]{:S(2)}, u32[]{:S(2)}) collective-permute-start(bf16[2,2,512,256]{3,2,1,0:T(8,128)(2,1)S(1)} %get-tuple-element.88), channel_id=1, source_target_pairs={{0,48},{16,0},{32,16},{48,32},{1,49},{17,1},{33,17},{49,33},{2,50}... | collective-permute-start | bytes 3145736 | tf_op jit(solution)/shard_map/ppermute | solution.py:27
  366.7 25.9 %collective-permute-start.15 = (bf16[2,288,512]{2,1,0:T(8,128)(2,1)S(1)}, bf16[2,288,512]{2,1,0:T(8,128)(2,1)}, u32[]{:S(2)}, u32[]{:S(2)}) collective-permute-start(bf16[2,288,512]{2,1,0:T(8,128)(2,1)S(1)} %bitcast_select_fusion), channel_id=1, source_target_pairs={{0,128},{64,192},{128,0},{192,64},{1,129},{65,193},{129,1},{193,65... | collective-permute-start | bytes 1769480 | tf_op jit(solution)/shard_map/ppermute | solution.py:31
  368.1 23.0 %collective-permute-start.18 = (bf16[256,256]{1,0:T(8,128)(2,1)S(1)}, bf16[256,256]{1,0:T(8,128)(2,1)S(1)}, u32[]{:S(2)}, u32[]{:S(2)}) collective-permute-start(bf16[256,256]{1,0:T(8,128)(2,1)S(1)} %convert_element_type.182), channel_id=1, source_target_pairs={{0,32},{16,48},{32,0},{48,16},{1,33},{17,49},{33,1},{49,17},{2,34}... | collective-permute-start | bytes 393224 | tf_op jit(solution)/shard_map/ppermute | solution.py:31
  392.7 27.4 %copy-start.5 = (bf16[2,288,512]{2,1,0:T(8,128)(2,1)}, bf16[2,288,512]{2,1,0:T(8,128)(2,1)S(1)}, u32[]{:S(2)}) copy-start(bf16[2,288,512]{2,1,0:T(8,128)(2,1)S(1)} %broadcast_select_fusion.refs_8_) | copy-start | bytes 1769476
  396.1 14.7 %collective-permute-start.19 = (bf16[2,288,512]{2,1,0:T(8,128)(2,1)S(1)}, bf16[2,288,512]{2,1,0:T(8,128)(2,1)S(1)}, u32[]{:S(2)}, u32[]{:S(2)}) collective-permute-start(bf16[2,288,512]{2,1,0:T(8,128)(2,1)S(1)} %broadcast_select_fusion.refs_8_), channel_id=1, source_target_pairs={{0,64},{64,0},{128,192},{192,128},{1,65},{65,1},{129,193},{193,129... | collective-permute-start | bytes 1769480 | tf_op jit(solution)/shard_map/ppermute | solution.py:31
  396.1 16.0 %collective-permute-start.20 = (bf16[2,288,512]{2,1,0:T(8,128)(2,1)S(1)}, bf16[2,288,512]{2,1,0:T(8,128)(2,1)S(1)}, u32[]{:S(2)}, u32[]{:S(2)}) collective-permute-start(bf16[2,288,512]{2,1,0:T(8,128)(2,1)S(1)} %broadcast_select_fusion.refs_8_), channel_id=1, source_target_pairs={{0,16},{16,32},{32,48},{48,0},{1,17},{17,33},{33,49},{49,1},{2,18}... | collective-permute-start | bytes 1769480 | tf_op jit(solution)/shard_map/ppermute | solution.py:27
  396.7 15.5 %collective-permute-start.21 = (bf16[2,288,512]{2,1,0:T(8,128)(2,1)S(1)}, bf16[2,288,512]{2,1,0:T(8,128)(2,1)S(1)}, u32[]{:S(2)}, u32[]{:S(2)}) collective-permute-start(bf16[2,288,512]{2,1,0:T(8,128)(2,1)S(1)} %broadcast_select_fusion.refs_8_), channel_id=1, source_target_pairs={{0,48},{16,0},{32,16},{48,32},{1,49},{17,1},{33,17},{49,33},{2,50}... | collective-permute-start | bytes 1769480 | tf_op jit(solution)/shard_map/ppermute | solution.py:27
  410.9 9.2 %copy-start.12 = (bf16[2,288,512]{2,1,0:T(8,128)(2,1)}, bf16[2,288,512]{2,1,0:T(8,128)(2,1)S(1)}, u32[]{:S(2)}) copy-start(bf16[2,288,512]{2,1,0:T(8,128)(2,1)S(1)} %collective-permute-done.19.refs_9_) | copy-start | bytes 1769476
  412.1 17.2 %copy-start.15 = (bf16[2,288,512]{2,1,0:T(8,128)(2,1)}, bf16[2,288,512]{2,1,0:T(8,128)(2,1)S(1)}, u32[]{:S(2)}) copy-start(bf16[2,288,512]{2,1,0:T(8,128)(2,1)S(1)} %collective-permute-done.20.refs_16_) | copy-start | bytes 1769476
  413.0 16.4 %collective-permute-start.22 = (bf16[2,288,512]{2,1,0:T(8,128)(2,1)S(1)}, bf16[2,288,512]{2,1,0:T(8,128)(2,1)}, u32[]{:S(2)}, u32[]{:S(2)}) collective-permute-start(bf16[2,288,512]{2,1,0:T(8,128)(2,1)S(1)} %collective-permute-done.19.refs_9_), channel_id=1, source_target_pairs={{0,16},{16,32},{32,48},{48,0},{1,17},{17,33},{33,49},{49,1},{2,18}... | collective-permute-start | bytes 1769480 | tf_op jit(solution)/shard_map/ppermute | solution.py:27
  413.0 16.4 %collective-permute-start.23 = (bf16[2,288,512]{2,1,0:T(8,128)(2,1)S(1)}, bf16[2,288,512]{2,1,0:T(8,128)(2,1)}, u32[]{:S(2)}, u32[]{:S(2)}) collective-permute-start(bf16[2,288,512]{2,1,0:T(8,128)(2,1)S(1)} %collective-permute-done.19.refs_9_), channel_id=1, source_target_pairs={{0,48},{16,0},{32,16},{48,32},{1,49},{17,1},{33,17},{49,33},{2,50}... | collective-permute-start | bytes 1769480 | tf_op jit(solution)/shard_map/ppermute | solution.py:27
  416.3 13.0 %collective-permute-start.24 = (bf16[512,256]{1,0:T(8,128)(2,1)S(1)}, bf16[512,256]{1,0:T(8,128)(2,1)S(1)}, u32[]{:S(2)}, u32[]{:S(2)}) collective-permute-start(bf16[512,256]{1,0:T(8,128)(2,1)S(1)} %get-tuple-element.96), channel_id=1, source_target_pairs={{0,128},{64,192},{128,0},{192,64},{1,129},{65,193},{129,1},{193,65... | collective-permute-start | bytes 786440 | tf_op jit(solution)/shard_map/ppermute | solution.py:27
  429.3 14.1 %copy-start.17 = (bf16[512,256]{1,0:T(8,128)(2,1)}, bf16[512,256]{1,0:T(8,128)(2,1)S(1)}, u32[]{:S(2)}) copy-start(bf16[512,256]{1,0:T(8,128)(2,1)S(1)} %collective-permute-done.24) | copy-start | bytes 786436
  429.4 16.3 %collective-permute-start.25 = (bf16[2,288,512]{2,1,0:T(8,128)(2,1)S(1)}, bf16[2,288,512]{2,1,0:T(8,128)(2,1)S(1)}, u32[]{:S(2)}, u32[]{:S(2)}) collective-permute-start(bf16[2,288,512]{2,1,0:T(8,128)(2,1)S(1)} %collective-permute-done.20.refs_16_), channel_id=1, source_target_pairs={{0,16},{16,32},{32,48},{48,0},{1,17},{17,33},{33,49},{49,1},{2,18}... | collective-permute-start | bytes 1769480 | tf_op jit(solution)/shard_map/ppermute | solution.py:27
  429.5 16.2 %collective-permute-start.26 = (bf16[2,288,512]{2,1,0:T(8,128)(2,1)}, bf16[2,288,512]{2,1,0:T(8,128)(2,1)S(1)}, u32[]{:S(2)}, u32[]{:S(2)}) collective-permute-start(bf16[2,288,512]{2,1,0:T(8,128)(2,1)} %collective-permute-done.23.refs_19_), channel_id=1, source_target_pairs={{0,48},{16,0},{32,16},{48,32},{1,49},{17,1},{33,17},{49,33},{2,50}... | collective-permute-start | bytes 1769480 | tf_op jit(solution)/shard_map/ppermute | solution.py:27
  432.7 11.3 %collective-permute-start.27 = (bf16[512,256]{1,0:T(8,128)(2,1)}, bf16[512,256]{1,0:T(8,128)(2,1)S(1)}, u32[]{:S(2)}, u32[]{:S(2)}) collective-permute-start(bf16[512,256]{1,0:T(8,128)(2,1)} %get-tuple-element.102), channel_id=1, source_target_pairs={{0,64},{64,128},{128,192},{192,0},{1,65},{65,129},{129,193},{193,1... | collective-permute-start | bytes 786440 | tf_op jit(solution)/shard_map/ppermute | solution.py:27
  432.8 12.9 %collective-permute-start.28 = (bf16[512,256]{1,0:T(8,128)(2,1)}, bf16[512,256]{1,0:T(8,128)(2,1)}, u32[]{:S(2)}, u32[]{:S(2)}) collective-permute-start(bf16[512,256]{1,0:T(8,128)(2,1)} %get-tuple-element.103), channel_id=1, source_target_pairs={{0,192},{64,0},{128,64},{192,128},{1,193},{65,1},{129,65},{193,129... | collective-permute-start | bytes 786440 | tf_op jit(solution)/shard_map/ppermute | solution.py:27
  443.9 1.7 copy-start.18
  445.6 1.7 copy-start.13
  445.7 1.7 copy-start.14
  452.2 35.8 %copy-start = (f32[2,256,640]{2,1,0:T(8,128)S(1)}, f32[2,256,640]{2,1,0:T(8,128)}, u32[]{:S(2)}) copy-start(f32[2,256,640]{2,1,0:T(8,128)} %project.5.a) | copy-start | bytes 3932164
  454.3 33.7 %collective-permute-start.29 = (f32[256,640]{1,0:T(8,128)}, f32[256,640]{1,0:T(8,128)S(1)}, u32[]{:S(2)}, u32[]{:S(2)}) collective-permute-start(f32[256,640]{1,0:T(8,128)} %slice_bitcast_fusion), channel_id=1, source_target_pairs={{0,8},{8,0},{1,9},{9,1},{2,10},{10,2},{3,11},{11,3},{4,12},{12,4},... | collective-permute-start | bytes 1966088 | tf_op jit(solution)/shard_map/ppermute | solution.py:27
  454.5 27.7 %collective-permute-start.30 = (bf16[256,256]{1,0:T(8,128)(2,1)S(1)}, bf16[256,256]{1,0:T(8,128)(2,1)S(1)}, u32[]{:S(2)}, u32[]{:S(2)}) collective-permute-start(bf16[256,256]{1,0:T(8,128)(2,1)S(1)} %get-tuple-element.135), channel_id=1, source_target_pairs={{0,8},{1,40},{2,72},{3,104},{4,136},{5,168},{6,200},{7,232},{8,16}... | collective-permute-start | bytes 393224 | tf_op jit(solution)/shard_map/ppermute | solution.py:481
  456.0 30.3 %collective-permute-start.31 = (bf16[256,256]{1,0:T(8,128)(2,1)S(1)}, bf16[256,256]{1,0:T(8,128)(2,1)S(1)}, u32[]{:S(2)}, u32[]{:S(2)}) collective-permute-start(bf16[256,256]{1,0:T(8,128)(2,1)S(1)} %get-tuple-element.134), channel_id=1, source_target_pairs={{0,0},{1,56},{2,88},{3,120},{4,152},{5,184},{6,216},{7,248},{8,8},... | collective-permute-start | bytes 393224 | tf_op jit(solution)/shard_map/ppermute | solution.py:481
  (6 other events, 6.8 us)

commit v3 on v2

--- a/solution.py
+++ b/solution.py
@@ -62,114 +62,32 @@
     return (wide * lax.rsqrt(meansq + 1e-05) * norm_gain[None, :]).astype(bf16)
 
 
-def block_body(role, table, q, kt, *refs):
-    side = kt.shape[0]
-    width = q.shape[1]
+def pack_body(table, q, kt, out):
+    n = q.shape[0]
+    out[0, :n] = q[...]
+    out[0, n:] = kt[...]
+
+
+def pack(at, q, kt):
+    width, side = q.shape[1], kt.shape[0]
     n = q.shape[0] // (4 * NY)
-    piece, high = n // 2, side // 2
-    if role == "quarter":
-        there, c, d, out, found, turned, sems = refs
-    elif role == "far":
-        there, *outs, sems = refs
-    elif role == "relay":
-        there, relay, out, sems = refs
-    else:
-        out, sems = refs
-    if role in ("pack", "relay"):
-        outs = [out.at[0], out.at[1]]
-
-    def home(p):
-        at = 2 * table[0] + p
-        rows = q.at[pl.ds(pl.multiple_of(at * n, n), n), :]
-        return rows, kt.at[:, pl.ds(pl.multiple_of(at * width, width), width)]
-
-    def received(x, p):
-        return x.at[p, pl.ds(0, n), :], x.at[p, pl.ds(n, side), :]
-
-    def run(pairs):
-        copies = [pltpu.make_async_copy(a, b, sems.at[i]) for i, (a, b) in enumerate(pairs)]
-        for copy in copies:
-            copy.start()
-        for copy in copies:
-            copy.wait()
-
-    def put(p, source):
-        rows, keys = source
-        if role == "quarter":
-            pairs = [
-                (rows.at[pl.ds(i * piece, piece), :], out.at[2 * p + i, pl.ds(0, piece), :])
-                for i in range(2)
-            ]
-            return pairs + [(keys, found.at[p])]
-        to = outs[p]
-        return [(rows, to.at[pl.ds(0, n), :]), (keys, to.at[pl.ds(n, side), :])]
-
-    def choose(cases):
-        left = True
-        for when, pairs in cases:
-            pl.when(when & left)(functools.partial(run, pairs))
-            left = left & ~when
-
-    yes = table[0] >= 0
-    if role == "pack":
-        run(put(0, home(0)) + put(1, home(1)))
-    elif role in ("far", "relay"):
-        cases = [
-            (table[1] == 1, put(0, home(0)) + put(1, home(1))),
-            (yes, [(there.at[p], outs[p]) for p in range(2)]),
-        ]
-        if role == "relay":
-            cases = [(table[2] == 1, [(relay, outs[p]) for p in range(2)])] + cases
-        choose(cases)
-    else:
-        for p in range(2):
-            mine = table[2] == 1
-            choose(
-                [
-                    (mine & (table[1] == 1), put(p, home(p))),
-                    (mine, put(p, received(there, p))),
-                    (table[3 + p] == 1, put(p, received(c, p))),
-                    (yes, put(p, received(d, p))),
-                ]
-            )
-        for p in range(2):
-            for i in range(2):
-                span = slice(i * piece, (i + 1) * piece)
-                turned[2 * p + i] = jnp.concatenate(
-                    [found[p, :high, span], found[p, high:, span]], axis=1
-                )
-        run([(turned.at[i], out.at[i, pl.ds(piece, high), :]) for i in range(4)])
-
-
-def weight_block(role, table, q, kt, *more):
-    width, side = q.shape[1], kt.shape[0]
-    rows = q.shape[0] // (4 * NY) + side
-    shape = lambda *dims: jax.ShapeDtypeStruct(dims, bf16)
-    shapes = {"far": [shape(rows, width)] * 2, "quarter": [shape(4, rows // 2, width)]}
-    shapes = shapes.get(role, [shape(2, rows, width)])
-    scratch = [pltpu.SemaphoreType.DMA((4,))]
-    if role == "quarter":
-        scratch = [
-            pltpu.VMEM((2, side, width), bf16),
-            pltpu.VMEM((4, side // 2, width), bf16),
-        ] + scratch
-    anywhere = pl.BlockSpec(memory_space=pl.ANY)
-    out = pl.pallas_call(
-        functools.partial(block_body, role),
+    return pl.pallas_call(
+        pack_body,
         grid_spec=pltpu.PrefetchScalarGridSpec(
             num_scalar_prefetch=1,
-            grid=(1,),
-            in_specs=[anywhere] * (2 + len(more)),
-            out_specs=[anywhere] * len(shapes),
-            scratch_shapes=scratch,
-        ),
-        out_shape=shapes,
+            grid=(2,),
+            in_specs=[
+                pl.BlockSpec((n, width), lambda p, tab: (2 * tab[0] + p, 0)),
+                pl.BlockSpec((side, width), lambda p, tab: (0, 2 * tab[0] + p)),
+            ],
+            out_specs=pl.BlockSpec((1, n + side, width), lambda p, tab: (p, 0, 0)),
+        ),
+        out_shape=jax.ShapeDtypeStruct((2, n + side, width), bf16),
         cost_estimate=pl.CostEstimate(
-            flops=0, bytes_accessed=8 * rows * width, transcendentals=0
-        ),
-        name="block_" + role,
-    )(table.astype(jnp.int32), q, kt, *more)
-    return out if role == "far" else out[0]
+            flops=0, bytes_accessed=8 * (n + side) * width, transcendentals=0
+        ),
+        name="pack",
+    )(at.reshape(1).astype(jnp.int32), q, kt)
 
 
 def across(left, right):
@@ -377,29 +295,31 @@
 
     q = query_store[0]
     kt = key_store[0].T
-    one = jnp.int32(1)
 
     def chip(rel):
         return (y + rel) % NY
 
-    def told(rel, *flags):
-        return jnp.stack([k * NY + chip(rel), *[x * one for x in flags]])
-
-    def pack(k, rel):
-        return weight_block("pack", jnp.stack([(1 - k) * NY + chip(rel)]), q, kt)
+    def block(core, rel):
+        return pack(core * NY + chip(rel), q, kt)
 
     step_y = (y - root_y) % NY
-    far0, far1 = weight_block("far", told(2, here), q, kt, send(pack(k, 2), "k", 1))
-    far0, far1, later_k = together((far0, far1, k))
+    away, k1 = together((block(1 - k, 2), k))
+    there, home = send(away, "k", 1), block(k1, 2)
+    far0, far1, k2, here = together(
+        (jnp.where(here, home[0], there[0]), jnp.where(here, home[1], there[1]), k, here)
+    )
     a = send(far0, "y", 1)
     b = send(far1, "y", -1)
-    others = [pack(later_k, rel) for rel in (1, 3)]
-    others, later_hidden, last_k = together((others, hidden, later_k))
+    others = [block(1 - k2, rel) for rel in (1, 3)]
+    others, later_hidden, k3 = together((others, hidden, k2))
     others = [send(x, "k", 1) for x in others]
     theirs = send(later_hidden, "k", 1)
-    others.append(send(pack(last_k, 0), "k", 1))
-    up = weight_block("relay", told(1, here, step_y == 1), q, kt, others[0], a)
-    down = weight_block("relay", told(3, here, step_y == 3), q, kt, others[1], b)
+    others.append(send(block(1 - k3, 0), "k", 1))
+    up, down, own = (
+        jnp.where(here, block(k3, rel), x) for rel, x in zip((1, 3, 0), others)
+    )
+    up = jnp.where(step_y == 1, a[None], up)
+    down = jnp.where(step_y == 3, b[None], down)
     up, down, gain, ours = together((up, down, norm_gain, hidden))
     c = send(up, "y", 1)
     d = send(down, "y", -1)
@@ -420,10 +340,15 @@
     def butterfly(extra, axis, bit):
         return extra + swap(extra.astype(bf16), axis, bit).astype(f32)
 
-    extra = butterfly(butterfly(extra, "zl", 1), "zl", 2)
-    p_low, p_high, base, extra, step_y = together((p_low, p_high, base, extra, step_y))
-    flags = told(0, here, step_y == 0, (step_y == 1) | (step_y == 2), step_y == 1)
-    quarter = weight_block("quarter", flags, q, kt, others[2], c, d)
+    extra = butterfly(extra, "zl", 1)
+    p_low, p_high, base, extra, own, step_y = together((p_low, p_high, base, extra, own, step_y))
+    low = lax.broadcasted_iota(jnp.int32, (2, 1, 1), 0) == 0
+    from_c = (step_y == 1) | ((step_y == 2) & low)
+    quarter = jnp.where(step_y == 0, own, jnp.where(from_c, c, d))
+    side = quarter[:, h * piece :].reshape(2, 2, kwidth // 2, 2, piece)
+    side = side.transpose(0, 3, 2, 1, 4).reshape(NZ, kwidth // 2, 2 * piece)
+    quarter = quarter[:, : h * piece].reshape(NZ, piece, qwidth)
+    quarter = jnp.concatenate([quarter, side], axis=1)
     p_low, p_high, quarter = together((p_low, p_high, quarter))
 
     ga = send(p_low, "y", 1)
@@ -435,12 +360,12 @@
     up = base[:NZ].reshape(shape) + jnp.where(first, ga.astype(f32)[None], 0.0)
     down = base[NZ : 2 * NZ].reshape(shape) + jnp.where(first, 0.0, gb.astype(f32)[None])
     kept = jnp.where(z == root_z, pick(quarter, z % 2), kept)
-    extra = butterfly(extra, "y", 1)
+    extra = butterfly(extra, "zl", 2)
     up, down, kept, extra = together((up.astype(bf16), down.astype(bf16), kept, extra))
     gc = send(up, "y", 1).reshape(NZ, 2 * tile, tile)
     gd = send(down, "y", -1).reshape(NZ, 2 * tile, tile)
     kept = jnp.where(z // 2 == root_z // 2, kept, swap(kept, "zl", 2))
-    extra = butterfly(extra, "y", 2)
+    extra = butterfly(extra, "y", 1)
     total = [base[2 * NZ + s] + gc[s].astype(f32) + gd[s].astype(f32) for s in range(NZ)]
     hess, rest = total[0], [x.astype(bf16) for x in total[1:]]
     kept, hess, rest, extra = together((kept, hess, rest, extra))
@@ -454,8 +379,9 @@
     crossed = swap(kept, "zl", 1)
     left0, right0 = send(kept, "y", 1), send(kept, "y", -1)
     cosine, sine = turns(positions(token_ids))
-    crossed, left0, right0, rest, cosine, sine = together(
-        (crossed, left0, right0, rest, cosine, sine)
+    extra = butterfly(extra, "y", 2)
+    crossed, left0, right0, rest, extra, cosine, sine = together(
+        (crossed, left0, right0, rest, extra, cosine, sine)
     )
     left1, right1 = send(crossed, "y", 1), send(crossed, "y", -1)
     parts = [send(rest[1], "zl", 2)]

time: 492 us -> 216 us (0.44)
  Pallas kernels: 325 us -> 46.4 us
  other arithmetic: 21.4 us -> 28.5 us
  local copies, waits for them, and re-layouts: 14.6 us -> 8.11 us
  waiting for transfers between devices: 79.6 us -> 85.1 us
    pallas_call x8, Pallas kernels: 296 us -> 17.3 us  [pack(): pl.pallas_call(pack_body, grid_spec=pltpu.PrefetchScalarGridSpec(num_scal...]
    select_n x0 -> x5, other arithmetic: none -> 8.74 us  [the longest x1 2.39 us: shards(): down = jnp.where(step_y == 3, b[None], down)]
    ppermute x23, waiting for transfers between devices: 19 us -> 24.1 us  [send(): return lax.ppermute(array, axis, [(i, (i + shift) % n) for i in range(n)])]
    unnamed x44 -> x40, local copies, waits for them, and re-layouts: 8 us -> 2.92 us
  transfers between devices with their start and end apart: 32 -> 32, of which waited for: 13 -> 16; matrix products, arithmetic and copies ran while one was open for 4% -> 11% of each run, Pallas kernels for 35% -> 16%
where the time goes in v3:
time: 216 us; the launch traced here: 215 us
  waiting for transfers between devices  85.1 us (39%)
  Pallas kernels  46.4 us (21%)
  starting transfers between devices  44.7 us (21%)
  other arithmetic  28.5 us (13%)
  local copies, waits for them, and re-layouts  8.11 us (4%)
    ppermute x7, waiting for transfers between devices, swap(): return lax.ppermute(array, axis, [(i, i ^ bit) for i in range(SIZES[axis])])  37.2 us
    ppermute x23, starting transfers between devices, send(): return lax.ppermute(array, axis, [(i, (i + shift) % n) for i in range(n)])  29.9 us
    ppermute x23, waiting for transfers between devices, send(): return lax.ppermute(array, axis, [(i, (i + shift) % n) for i in range(n)])  24.1 us
    ppermute x2, waiting for transfers between devices, shards(): lax.ppermute(jnp.where(second, tiles[1], tiles[0]), ALL, partner_moves(n))  23.8 us
    pallas_call x8, Pallas kernels, pack(): pl.pallas_call(pack_body, grid_spec=pltpu.PrefetchScalarGridSpec(num_scal...  17.3 us
    pallas_call x3, Pallas kernels, project(): pl.pallas_call(functools.partial(project_body, slots, piece, fresh), grid...  15.5 us
    pallas_call x1, Pallas kernels, gram(): pl.pallas_call(gram_body, grid_spec=pltpu.PrefetchScalarGridSpec(num_scal...  10.8 us
    ppermute x2, starting transfers between devices, shards(): lax.ppermute(jnp.where(second, tiles[1], tiles[0]), ALL, partner_moves(n))  9.03 us
  transfers between devices with their start and end apart: 32, of which 16 were waited for; matrix products, arithmetic and copies ran while one was open for 11% of the time, Pallas kernels for 16%

profile of v3, /device:TPU:132, one launch (start us, length us, event | category | flops | bytes accessed | tf_op | source)
XLA Modules:
  0.0 215.2 jit_solution(8372508521710988774)
XLA Ops:
  0.6 2.1 pack.8
  3.5 2.2 %pack.9 = bf16[2,576,512]{2,1,0:T(8,128)(2,1)} custom-call(s32[1]{0:T(128)} %bitcast.6.table, bf16[8192,512]{1,0:T(8,128)(2,1)} %bitcast.57, bf16[64,8192]{1,0:T(8,128)(2,1)} %bitcast.65), custom_call_target="tpu_custom_call" | custom-call | bytes 2359296 | tf_op jit(solution)/shard_map/pack/pallas_call | solution.py:74
  5.8 2.4 %fusion.6 = (bf16[576,512]{1,0:T(8,128)(2,1)}, bf16[576,512]{1,0:T(8,128)(2,1)}) fusion(bf16[2,576,512]{2,1,0:T(8,128)(2,1)S(1)} %collective-permute-done, bf16[2,576,512]{2,1,0:T(8,128)(2,1)} %pack.9, pred[]{:T(512)S(6)} %eq.136), kind=kLoop, calls=%fused_computation.20 | loop fusion | flops 589824 | bytes 3538945 | tf_op jit(solution)/shard_map/jit(_where)/select_n | solution.py:309
  8.2 2.2 %pack.11 = bf16[2,576,512]{2,1,0:T(8,128)(2,1)} custom-call(s32[1]{0:T(128)} %bitcast.11.table, bf16[8192,512]{1,0:T(8,128)(2,1)} %bitcast.58, bf16[64,8192]{1,0:T(8,128)(2,1)} %bitcast.66), custom_call_target="tpu_custom_call" | custom-call | bytes 2359296 | tf_op jit(solution)/shard_map/pack/pallas_call | solution.py:74
  10.4 2.1 pack.10
  13.6 3.0 %collective-permute-start.3 = (bf16[576,512]{1,0:T(8,128)(2,1)}, bf16[576,512]{1,0:T(8,128)(2,1)}, u32[]{:S(2)}, u32[]{:S(2)}) collective-permute-start(bf16[576,512]{1,0:T(8,128)(2,1)} %get-tuple-element.72), channel_id=1, source_target_pairs={{0,48},{16,0},{32,16},{48,32},{1,49},{17,1},{33,17},{49,33},{2,50}... | collective-permute-start | bytes 1769480 | tf_op jit(solution)/shard_map/ppermute | solution.py:27
  17.5 2.1 pack.13
  19.6 2.1 pack.12
  21.7 2.1 pack.15
  23.8 2.3 %pack.14 = bf16[2,576,512]{2,1,0:T(8,128)(2,1)} custom-call(s32[1]{0:T(128)} %bitcast.14.table, bf16[8192,512]{1,0:T(8,128)(2,1)} %bitcast.63, bf16[64,8192]{1,0:T(8,128)(2,1)} %bitcast.71), custom_call_target="tpu_custom_call" | custom-call | bytes 2359296 | tf_op jit(solution)/shard_map/pack/pallas_call | solution.py:74
  26.2 3.8 %collective-permute-done.3 = bf16[576,512]{1,0:T(8,128)(2,1)} collective-permute-done((bf16[576,512]{1,0:T(8,128)(2,1)}, bf16[576,512]{1,0:T(8,128)(2,1)}, u32[]{:S(2)}, u32[]{:S(2)}) %collective-permute-start.3) | collective-permute-done | bytes 589856 | tf_op jit(solution)/shard_map/ppermute | solution.py:27
  29.9 2.4 %select_select_fusion.1 = bf16[2,576,512]{2,1,0:T(8,128)(2,1)} fusion(bf16[2,576,512]{2,1,0:T(8,128)(2,1)S(1)} %copy-done.5, bf16[2,576,512]{2,1,0:T(8,128)(2,1)S(1)} %collective-permute-done.4, pred[]{:T(512)S(6)} %eq.137, pred[]{:T(512)S(6)} %eq.136, bf16[576,512]{1,0:T(8,128)(2,1)} %collective-permute-done.3), kind=kLoop, calls=%fused_computation.14 | loop fusion | flops 1179648 | bytes 4128770 | tf_op jit(solution)/shard_map/jit(_where)/select_n | solution.py:322
  33.4 2.4 %select_select_fusion.2 = bf16[2,576,512]{2,1,0:T(8,128)(2,1)} fusion(bf16[2,576,512]{2,1,0:T(8,128)(2,1)S(1)} %copy-done.4, bf16[2,576,512]{2,1,0:T(8,128)(2,1)S(1)} %collective-permute-done.2, pred[]{:T(512)S(6)} %eq.136, pred[]{:T(512)S(6)} %eq.135, bf16[576,512]{1,0:T(8,128)(2,1)} %collective-permute-done.1), kind=kLoop, calls=%fused_computation.15 | loop fusion | flops 1179648 | bytes 4128770 | tf_op jit(solution)/shard_map/jit(_where)/select_n | solution.py:321
  35.8 3.2 %collective-permute-start.9 = (bf16[2,576,512]{2,1,0:T(8,128)(2,1)}, bf16[2,576,512]{2,1,0:T(8,128)(2,1)}, u32[]{:S(2)}, u32[]{:S(2)}) collective-permute-start(bf16[2,576,512]{2,1,0:T(8,128)(2,1)} %select_select_fusion.1), channel_id=1, source_target_pairs={{0,48},{16,0},{32,16},{48,32},{1,49},{17,1},{33,17},{49,33},{2,50}... | collective-permute-start | bytes 3538952 | tf_op jit(solution)/shard_map/ppermute | solution.py:27
  40.1 3.1 %fusion.3 = f32[256]{0:T(256)S(1)} fusion(bf16[256,8192]{1,0:T(8,128)(2,1)} %collective-permute-done.5), kind=kLoop, calls=%fused_computation.7 | loop fusion | flops 6291200 | bytes 4195328 | tf_op jit(solution)/shard_map/reduce_sum | solution.py:61
  43.2 4.0 %fusion.5 = (bf16[256,8192]{1,0:T(8,128)(2,1)S(1)}, bf16[256,8192]{1,0:T(8,128)(2,1)S(1)}) fusion(bf16[256,8192]{1,0:T(8,128)(2,1)} %collective-permute-done.5, f32[256]{0:T(256)S(1)} %add_rsqrt_fusion, f32[8192]{0:T(1024)S(1)} %copy-done.15, f32[256]{0:T(256)S(1)} %add_rsqrt_fusion.1, bf16[256,8192]{1,0:T(8,128)(2,1)S(1)} %copy-done.3), kind=kLoop, calls=%fused_computation.9 | loop fusion | flops 16777216 | bytes 16812032 | tf_op jit(solution)/shard_map/convert_element_type | solution.py:62
  47.5 1.8 copy-done.1
  51.6 10.8 %gram.1 = (bf16[2,512,256]{2,1,0:T(8,128)(2,1)}, bf16[2,512,256]{2,1,0:T(8,128)(2,1)}, f32[12,512,256]{2,1,0:T(8,128)}) custom-call(s32[4,16]{1,0:T(4,128)} %pad_add_fusion.table, bf16[256,8192]{1,0:T(8,128)(2,1)} %copy-done.2, bf16[256,8192]{1,0:T(8,128)(2,1)} %copy-done.2, bf16[256,8192]{1,0:T(8,128)(2,1)} %copy-done.2, bf16[256,8192]{1,0:T(8,128)(2,1)} %copy-done.2, ...), custom_call_target="tpu_custom_call" | custom-call | flops 4294967296 | bytes 16777216 | tf_op jit(solution)/shard_map/gram/pallas_call | solution.py:138
  62.5 2.8 %collective-permute-done.8 = bf16[2,576,512]{2,1,0:T(8,128)(2,1)S(1)} collective-permute-done((bf16[2,576,512]{2,1,0:T(8,128)(2,1)}, bf16[2,576,512]{2,1,0:T(8,128)(2,1)S(1)}, u32[]{:S(2)}, u32[]{:S(2)}) %collective-permute-start.8) | collective-permute-done | bytes 1179680 | tf_op jit(solution)/shard_map/ppermute | solution.py:27
  65.2 1.5 select_select_fusion
  66.8 1.6 collective-permute-start.13
  69.9 1.2 collective-permute-start.10
  71.2 2.0 collective-permute-start.11
  73.2 2.5 %fusion.30 = (f32[4,512,256]{2,1,0:T(8,128)S(1)}, f32[4,512,256]{2,1,0:T(8,128)S(1)}) fusion(f32[12,512,256]{2,1,0:T(8,128)} %get-tuple-element.80), kind=kLoop, calls=%fused_computation.107 | loop fusion | bytes 8388608 | tf_op jit(solution)/shard_map/slice | solution.py:361
  75.8 8.0 %collective-permute-done.10 = bf16[2,512,256]{2,1,0:T(8,128)(2,1)S(1)} collective-permute-done((bf16[2,512,256]{2,1,0:T(8,128)(2,1)S(1)}, bf16[2,512,256]{2,1,0:T(8,128)(2,1)S(1)}, u32[]{:S(2)}, u32[]{:S(2)}) %collective-permute-start.10) | collective-permute-done | bytes 524320 | tf_op jit(solution)/shard_map/ppermute | solution.py:27
  85.5 1.7 collective-permute-start.15
  87.2 1.6 collective-permute-start.16
  92.1 21.4 %collective-permute-done.17 = bf16[256,256]{1,0:T(8,128)(2,1)} collective-permute-done((bf16[256,256]{1,0:T(8,128)(2,1)}, bf16[256,256]{1,0:T(8,128)(2,1)}, u32[]{:S(2)}, u32[]{:S(2)}) %collective-permute-start.17) | collective-permute-done | bytes 131104 | tf_op jit(solution)/shard_map/ppermute | solution.py:31
  115.4 3.5 %fusion.10 = (bf16[512,256]{1,0:T(8,128)(2,1)}, bf16[512,256]{1,0:T(8,128)(2,1)S(1)}, bf16[512,256]{1,0:T(8,128)(2,1)}, f32[512,256]{1,0:T(8,128)S(1)}) fusion(f32[12,512,256]{2,1,0:T(8,128)} %get-tuple-element.80, bf16[4,512,256]{2,1,0:T(8,128)(2,1)} %bitcast.24, bf16[4,512,256]{2,1,0:T(8,128)(2,1)} %bitcast.23), kind=kLoop, calls=%fused_computation.33 | loop fusion | flops 2490368 | bytes 5505024 | tf_op jit(solution)/shard_map/convert_element_type | solution.py:370
  119.7 2.4 %collective-permute-start.20 = (bf16[2,288,512]{2,1,0:T(8,128)(2,1)S(1)}, bf16[2,288,512]{2,1,0:T(8,128)(2,1)S(1)}, u32[]{:S(2)}, u32[]{:S(2)}) collective-permute-start(bf16[2,288,512]{2,1,0:T(8,128)(2,1)S(1)} %broadcast_select_fusion.1.refs_8_), channel_id=1, source_target_pairs={{0,48},{16,0},{32,16},{48,32},{1,49},{17,1},{33,17},{49,33},{2,50}... | collective-permute-start | bytes 1769480 | tf_op jit(solution)/shard_map/ppermute | solution.py:27
  123.5 14.2 %collective-permute-done.21 = bf16[256,256]{1,0:T(8,128)(2,1)S(1)} collective-permute-done((bf16[256,256]{1,0:T(8,128)(2,1)S(1)}, bf16[256,256]{1,0:T(8,128)(2,1)S(1)}, u32[]{:S(2)}, u32[]{:S(2)}) %collective-permute-start.21) | collective-permute-done | bytes 131104 | tf_op jit(solution)/shard_map/ppermute | solution.py:31
  138.2 1.3 collective-permute-start.22
  139.4 2.3 %collective-permute-start.23 = (bf16[2,288,512]{2,1,0:T(8,128)(2,1)S(1)}, bf16[2,288,512]{2,1,0:T(8,128)(2,1)}, u32[]{:S(2)}, u32[]{:S(2)}) collective-permute-start(bf16[2,288,512]{2,1,0:T(8,128)(2,1)S(1)} %collective-permute-done.18.refs_9_), channel_id=1, source_target_pairs={{0,48},{16,0},{32,16},{48,32},{1,49},{17,1},{33,17},{49,33},{2,50}... | collective-permute-start | bytes 1769480 | tf_op jit(solution)/shard_map/ppermute | solution.py:27
  141.8 2.2 %collective-permute-start.24 = (bf16[512,256]{1,0:T(8,128)(2,1)S(1)}, bf16[512,256]{1,0:T(8,128)(2,1)S(1)}, u32[]{:S(2)}, u32[]{:S(2)}) collective-permute-start(bf16[512,256]{1,0:T(8,128)(2,1)S(1)} %get-tuple-element.102), channel_id=1, source_target_pairs={{0,128},{64,192},{128,0},{192,64},{1,129},{65,193},{129,1},{193,65... | collective-permute-start | bytes 786440 | tf_op jit(solution)/shard_map/ppermute | solution.py:27
  144.5 4.4 %project.3.refs_20_ = f32[2,256,640]{2,1,0:T(8,128)} custom-call(s32[4]{0:T(128)} %get-tuple-element.149.table, bf16[256,8192]{1,0:T(8,128)(2,1)} %copy-done.2, bf16[256,8192]{1,0:T(8,128)(2,1)} %copy-done.2, bf16[256,8192]{1,0:T(8,128)(2,1)} %copy-done.2, bf16[256,8192]{1,0:T(8,128)(2,1)} %copy-done.2, bf16[256,8192]{1,0:T(8,128)(2,1)} %copy-done.1, ...), custom_call_target="tpu_custom_call" | custom-call | flops 536870912 | bytes 2621440 | tf_op jit(solution)/shard_map/project/pallas_call | solution.py:189
  148.9 5.8 %collective-permute-done.24 = bf16[512,256]{1,0:T(8,128)(2,1)S(1)} collective-permute-done((bf16[512,256]{1,0:T(8,128)(2,1)S(1)}, bf16[512,256]{1,0:T(8,128)(2,1)S(1)}, u32[]{:S(2)}, u32[]{:S(2)}) %collective-permute-start.24) | collective-permute-done | bytes 262176 | tf_op jit(solution)/shard_map/ppermute | solution.py:27
  155.0 3.0 %collective-permute-start.26 = (bf16[2,288,512]{2,1,0:T(8,128)(2,1)}, bf16[2,288,512]{2,1,0:T(8,128)(2,1)S(1)}, u32[]{:S(2)}, u32[]{:S(2)}) collective-permute-start(bf16[2,288,512]{2,1,0:T(8,128)(2,1)} %collective-permute-done.23.refs_19_), channel_id=1, source_target_pairs={{0,48},{16,0},{32,16},{48,32},{1,49},{17,1},{33,17},{49,33},{2,50}... | collective-permute-start | bytes 1769480 | tf_op jit(solution)/shard_map/ppermute | solution.py:27
  158.3 3.5 %collective-permute-start.28 = (bf16[512,256]{1,0:T(8,128)(2,1)}, bf16[512,256]{1,0:T(8,128)(2,1)}, u32[]{:S(2)}, u32[]{:S(2)}) collective-permute-start(bf16[512,256]{1,0:T(8,128)(2,1)} %get-tuple-element.109), channel_id=1, source_target_pairs={{0,192},{64,0},{128,64},{192,128},{1,193},{65,1},{129,65},{193,129... | collective-permute-start | bytes 786440 | tf_op jit(solution)/shard_map/ppermute | solution.py:27
  162.4 6.3 %project.4.refs_10_ = f32[2,256,640]{2,1,0:T(8,128)} custom-call(s32[8]{0:T(128)} %pad_add_fusion.2.table, bf16[256,8192]{1,0:T(8,128)(2,1)} %copy-done.2, bf16[256,8192]{1,0:T(8,128)(2,1)} %copy-done.2, bf16[256,8192]{1,0:T(8,128)(2,1)} %copy-done.2, bf16[256,8192]{1,0:T(8,128)(2,1)} %copy-done.2, bf16[256,8192]{1,0:T(8,128)(2,1)} %copy-done.2, ...), custom_call_target="tpu_custom_call" | custom-call | flops 1073741824 | bytes 4718592 | tf_op jit(solution)/shard_map/project/pallas_call | solution.py:189
  169.2 1.5 collective-permute-done.28
  170.8 1.6 fusion.29
  172.4 4.8 %project.5.a = f32[2,256,640]{2,1,0:T(8,128)} custom-call(s32[4]{0:T(128)} %get-tuple-element.150.table, bf16[256,8192]{1,0:T(8,128)(2,1)} %copy-done.2, bf16[256,8192]{1,0:T(8,128)(2,1)} %copy-done.2, bf16[256,8192]{1,0:T(8,128)(2,1)} %copy-done.2, bf16[256,8192]{1,0:T(8,128)(2,1)} %copy-done.2, bf16[256,8192]{1,0:T(8,128)(2,1)} %copy-done.1, ...), custom_call_target="tpu_custom_call" | custom-call | flops 536870912 | bytes 2621440 | tf_op jit(solution)/shard_map/project/pallas_call | solution.py:189
  177.3 2.0 slice_bitcast_fusion
  179.6 8.9 %collective-permute-start.31 = (bf16[256,256]{1,0:T(8,128)(2,1)S(1)}, bf16[256,256]{1,0:T(8,128)(2,1)S(1)}, u32[]{:S(2)}, u32[]{:S(2)}) collective-permute-start(bf16[256,256]{1,0:T(8,128)(2,1)S(1)} %get-tuple-element.142), channel_id=1, source_target_pairs={{0,0},{1,56},{2,88},{3,120},{4,152},{5,184},{6,216},{7,248},{8,8},... | collective-permute-start | bytes 393224 | tf_op jit(solution)/shard_map/ppermute | solution.py:407
  188.6 19.6 %collective-permute-done.30.r0 = bf16[256,256]{1,0:T(8,128)(2,1)S(1)} collective-permute-done((bf16[256,256]{1,0:T(8,128)(2,1)S(1)}, bf16[256,256]{1,0:T(8,128)(2,1)S(1)}, u32[]{:S(2)}, u32[]{:S(2)}) %collective-permute-start.30) | collective-permute-done | bytes 131104 | tf_op jit(solution)/shard_map/ppermute | solution.py:407
  208.3 4.2 %collective-permute-done.31.r1 = bf16[256,256]{1,0:T(8,128)(2,1)S(1)} collective-permute-done((bf16[256,256]{1,0:T(8,128)(2,1)S(1)}, bf16[256,256]{1,0:T(8,128)(2,1)S(1)}, u32[]{:S(2)}, u32[]{:S(2)}) %collective-permute-start.31) | collective-permute-done | bytes 131104 | tf_op jit(solution)/shard_map/ppermute | solution.py:407
  212.4 1.7 assemble.1
  214.1 1.1 rope.1
  (128 shorter events, 20.6 us)
Async XLA Ops:
  2.8 3.1 %collective-permute-start = (bf16[2,576,512]{2,1,0:T(8,128)(2,1)}, bf16[2,576,512]{2,1,0:T(8,128)(2,1)S(1)}, u32[]{:S(2)}, u32[]{:S(2)}) collective-permute-start(bf16[2,576,512]{2,1,0:T(8,128)(2,1)} %pack.8), channel_id=1, source_target_pairs={{0,8},{8,0},{1,9},{9,1},{2,10},{10,2},{3,11},{11,3},{4,12},{12,4},... | collective-permute-start | bytes 3538952 | tf_op jit(solution)/shard_map/ppermute | solution.py:27
  10.4 2.7 %copy-start.17 = (s32[4]{0:T(128)S(1)}, s32[4]{0:T(128)}, u32[]{:S(2)}) copy-start(s32[4]{0:T(128)} %constant.318.clone) | copy-start | bytes 52
  12.5 27.6 %collective-permute-start.5 = (bf16[256,8192]{1,0:T(8,128)(2,1)}, bf16[256,8192]{1,0:T(8,128)(2,1)}, u32[]{:S(2)}, u32[]{:S(2)}) collective-permute-start(bf16[256,8192]{1,0:T(8,128)(2,1)} %param.7), channel_id=1, source_target_pairs={{0,8},{8,0},{1,9},{9,1},{2,10},{10,2},{3,11},{11,3},{4,12},{12,4},... | collective-permute-start | bytes 12582920 | tf_op jit(solution)/shard_map/ppermute | solution.py:27
  12.8 17.1 %collective-permute-start.4 = (bf16[2,576,512]{2,1,0:T(8,128)(2,1)}, bf16[2,576,512]{2,1,0:T(8,128)(2,1)S(1)}, u32[]{:S(2)}, u32[]{:S(2)}) collective-permute-start(bf16[2,576,512]{2,1,0:T(8,128)(2,1)} %pack.11), channel_id=1, source_target_pairs={{0,8},{8,0},{1,9},{9,1},{2,10},{10,2},{3,11},{11,3},{4,12},{12,4},... | collective-permute-start | bytes 3538952 | tf_op jit(solution)/shard_map/ppermute | solution.py:27
  13.1 20.4 %collective-permute-start.2 = (bf16[2,576,512]{2,1,0:T(8,128)(2,1)}, bf16[2,576,512]{2,1,0:T(8,128)(2,1)S(1)}, u32[]{:S(2)}, u32[]{:S(2)}) collective-permute-start(bf16[2,576,512]{2,1,0:T(8,128)(2,1)} %pack.10), channel_id=1, source_target_pairs={{0,8},{8,0},{1,9},{9,1},{2,10},{10,2},{3,11},{11,3},{4,12},{12,4},... | collective-permute-start | bytes 3538952 | tf_op jit(solution)/shard_map/ppermute | solution.py:27
  13.6 16.3 %collective-permute-start.3 = (bf16[576,512]{1,0:T(8,128)(2,1)}, bf16[576,512]{1,0:T(8,128)(2,1)}, u32[]{:S(2)}, u32[]{:S(2)}) collective-permute-start(bf16[576,512]{1,0:T(8,128)(2,1)} %get-tuple-element.72), channel_id=1, source_target_pairs={{0,48},{16,0},{32,16},{48,32},{1,49},{17,1},{33,17},{49,33},{2,50}... | collective-permute-start | bytes 1769480 | tf_op jit(solution)/shard_map/ppermute | solution.py:27
  16.6 16.8 %collective-permute-start.1 = (bf16[576,512]{1,0:T(8,128)(2,1)}, bf16[576,512]{1,0:T(8,128)(2,1)}, u32[]{:S(2)}, u32[]{:S(2)}) collective-permute-start(bf16[576,512]{1,0:T(8,128)(2,1)} %get-tuple-element.67), channel_id=1, source_target_pairs={{0,16},{16,32},{32,48},{48,0},{1,17},{17,33},{33,49},{49,1},{2,18}... | collective-permute-start | bytes 1769480 | tf_op jit(solution)/shard_map/ppermute | solution.py:27
  23.8 6.1 %copy-start.5 = (bf16[2,576,512]{2,1,0:T(8,128)(2,1)S(1)}, bf16[2,576,512]{2,1,0:T(8,128)(2,1)}, u32[]{:S(2)}) copy-start(bf16[2,576,512]{2,1,0:T(8,128)(2,1)} %pack.13) | copy-start | bytes 3538948
  26.1 7.3 %copy-start.4 = (bf16[2,576,512]{2,1,0:T(8,128)(2,1)S(1)}, bf16[2,576,512]{2,1,0:T(8,128)(2,1)}, u32[]{:S(2)}) copy-start(bf16[2,576,512]{2,1,0:T(8,128)(2,1)} %pack.12) | copy-start | bytes 3538948
  29.9 10.0 %collective-permute-start.7 = (bf16[2,576,512]{2,1,0:T(8,128)(2,1)}, bf16[2,576,512]{2,1,0:T(8,128)(2,1)S(1)}, u32[]{:S(2)}, u32[]{:S(2)}) collective-permute-start(bf16[2,576,512]{2,1,0:T(8,128)(2,1)} %pack.15), channel_id=1, source_target_pairs={{0,8},{8,0},{1,9},{9,1},{2,10},{10,2},{3,11},{11,3},{4,12},{12,4},... | collective-permute-start | bytes 3538952 | tf_op jit(solution)/shard_map/ppermute | solution.py:27
  29.9 9.1 %copy-start.3 = (bf16[256,8192]{1,0:T(8,128)(2,1)S(1)}, bf16[256,8192]{1,0:T(8,128)(2,1)}, u32[]{:S(2)}) copy-start(bf16[256,8192]{1,0:T(8,128)(2,1)} %param.7) | copy-start | bytes 12582916
  35.8 4.2 %copy-start.6 = (bf16[2,576,512]{2,1,0:T(8,128)(2,1)S(1)}, bf16[2,576,512]{2,1,0:T(8,128)(2,1)}, u32[]{:S(2)}) copy-start(bf16[2,576,512]{2,1,0:T(8,128)(2,1)} %pack.14) | copy-start | bytes 3538948
  35.8 29.4 %collective-permute-start.8 = (bf16[2,576,512]{2,1,0:T(8,128)(2,1)}, bf16[2,576,512]{2,1,0:T(8,128)(2,1)S(1)}, u32[]{:S(2)}, u32[]{:S(2)}) collective-permute-start(bf16[2,576,512]{2,1,0:T(8,128)(2,1)} %select_select_fusion.2), channel_id=1, source_target_pairs={{0,16},{16,32},{32,48},{48,0},{1,17},{17,33},{33,49},{49,1},{2,18}... | collective-permute-start | bytes 3538952 | tf_op jit(solution)/shard_map/ppermute | solution.py:27
  35.8 29.4 %collective-permute-start.9 = (bf16[2,576,512]{2,1,0:T(8,128)(2,1)}, bf16[2,576,512]{2,1,0:T(8,128)(2,1)}, u32[]{:S(2)}, u32[]{:S(2)}) collective-permute-start(bf16[2,576,512]{2,1,0:T(8,128)(2,1)} %select_select_fusion.1), channel_id=1, source_target_pairs={{0,48},{16,0},{32,16},{48,32},{1,49},{17,1},{33,17},{49,33},{2,50}... | collective-permute-start | bytes 3538952 | tf_op jit(solution)/shard_map/ppermute | solution.py:27
  40.1 3.1 %copy-start.15 = (f32[8192]{0:T(1024)S(1)}, f32[8192]{0:T(1024)}, u32[]{:S(2)}) copy-start(f32[8192]{0:T(1024)} %param.8) | copy-start | bytes 98308
  47.3 2.0 copy-start.1
  47.3 3.3 %copy-start.2 = (bf16[256,8192]{1,0:T(8,128)(2,1)}, bf16[256,8192]{1,0:T(8,128)(2,1)S(1)}, u32[]{:S(2)}) copy-start(bf16[256,8192]{1,0:T(8,128)(2,1)S(1)} %get-tuple-element.145.refs_0_.refs_1_.refs_2_.refs_3_.refs_8_.refs_4_.refs_5_.refs_6_.refs_7_) | copy-start | bytes 12582916
  50.6 11.8 %collective-permute-start.6 = (bf16[256,256]{1,0:T(8,128)(2,1)S(1)}, bf16[256,256]{1,0:T(8,128)(2,1)S(1)}, u32[]{:S(2)}, u32[]{:S(2)}) collective-permute-start(bf16[256,256]{1,0:T(8,128)(2,1)S(1)} %get-tuple-element.153), channel_id=1, source_target_pairs={{0,64},{64,0},{128,192},{192,128},{1,65},{65,1},{129,193},{193,129... | collective-permute-start | bytes 393224 | tf_op jit(solution)/shard_map/ppermute | solution.py:31
  66.8 8.9 %collective-permute-start.13 = (bf16[256,256]{1,0:T(8,128)(2,1)S(1)}, bf16[256,256]{1,0:T(8,128)(2,1)S(1)}, u32[]{:S(2)}, u32[]{:S(2)}) collective-permute-start(bf16[256,256]{1,0:T(8,128)(2,1)S(1)} %convert_element_type.155), channel_id=1, source_target_pairs={{0,128},{64,192},{128,0},{192,64},{1,129},{65,193},{129,1},{193,65... | collective-permute-start | bytes 393224 | tf_op jit(solution)/shard_map/ppermute | solution.py:31
  68.4 2.7 %copy-start.18 = (bf16[2,512,256]{2,1,0:T(8,128)(2,1)S(1)}, bf16[2,512,256]{2,1,0:T(8,128)(2,1)}, u32[]{:S(2)}) copy-start(bf16[2,512,256]{2,1,0:T(8,128)(2,1)} %get-tuple-element.88) | copy-start | bytes 1572868
  68.8 16.6 %collective-permute-start.12 = (bf16[2,288,512]{2,1,0:T(8,128)(2,1)S(1)}, bf16[2,288,512]{2,1,0:T(8,128)(2,1)S(1)}, u32[]{:S(2)}, u32[]{:S(2)}) collective-permute-start(bf16[2,288,512]{2,1,0:T(8,128)(2,1)S(1)} %dynamic-slice_bitcast_fusion), channel_id=1, source_target_pairs={{0,64},{64,0},{128,192},{192,128},{1,65},{65,1},{129,193},{193,129... | collective-permute-start | bytes 1769480 | tf_op jit(solution)/shard_map/ppermute | solution.py:31
  69.9 13.8 %collective-permute-start.10 = (bf16[2,512,256]{2,1,0:T(8,128)(2,1)S(1)}, bf16[2,512,256]{2,1,0:T(8,128)(2,1)S(1)}, u32[]{:S(2)}, u32[]{:S(2)}) collective-permute-start(bf16[2,512,256]{2,1,0:T(8,128)(2,1)S(1)} %copy-done.19), channel_id=1, source_target_pairs={{0,16},{16,32},{32,48},{48,0},{1,17},{17,33},{33,49},{49,1},{2,18}... | collective-permute-start | bytes 1572872 | tf_op jit(solution)/shard_map/ppermute | solution.py:27
  71.2 12.7 %collective-permute-start.11 = (bf16[2,512,256]{2,1,0:T(8,128)(2,1)S(1)}, bf16[2,512,256]{2,1,0:T(8,128)(2,1)S(1)}, u32[]{:S(2)}, u32[]{:S(2)}) collective-permute-start(bf16[2,512,256]{2,1,0:T(8,128)(2,1)S(1)} %copy-done.18), channel_id=1, source_target_pairs={{0,48},{16,0},{32,16},{48,32},{1,49},{17,1},{33,17},{49,33},{2,50}... | collective-permute-start | bytes 1572872 | tf_op jit(solution)/shard_map/ppermute | solution.py:27
  84.0 5.7 %copy-start.16 = (s32[256]{0:T(256)S(1)}, s32[256]{0:T(256)}, u32[]{:S(2)}) copy-start(s32[256]{0:T(256)} %param.9) | copy-start | bytes 3076
  85.5 29.8 %collective-permute-start.15 = (bf16[2,2,512,256]{3,2,1,0:T(8,128)(2,1)S(1)}, bf16[2,2,512,256]{3,2,1,0:T(8,128)(2,1)}, u32[]{:S(2)}, u32[]{:S(2)}) collective-permute-start(bf16[2,2,512,256]{3,2,1,0:T(8,128)(2,1)S(1)} %get-tuple-element.92), channel_id=1, source_target_pairs={{0,16},{16,32},{32,48},{48,0},{1,17},{17,33},{33,49},{49,1},{2,18}... | collective-permute-start | bytes 3145736 | tf_op jit(solution)/shard_map/ppermute | solution.py:27
  87.2 28.1 %collective-permute-start.16 = (bf16[2,2,512,256]{3,2,1,0:T(8,128)(2,1)S(1)}, bf16[2,2,512,256]{3,2,1,0:T(8,128)(2,1)}, u32[]{:S(2)}, u32[]{:S(2)}) collective-permute-start(bf16[2,2,512,256]{3,2,1,0:T(8,128)(2,1)S(1)} %get-tuple-element.93), channel_id=1, source_target_pairs={{0,48},{16,0},{32,16},{48,32},{1,49},{17,1},{33,17},{49,33},{2,50}... | collective-permute-start | bytes 3145736 | tf_op jit(solution)/shard_map/ppermute | solution.py:27
  88.8 26.4 %collective-permute-start.14 = (bf16[2,288,512]{2,1,0:T(8,128)(2,1)S(1)}, bf16[2,288,512]{2,1,0:T(8,128)(2,1)S(1)}, u32[]{:S(2)}, u32[]{:S(2)}) collective-permute-start(bf16[2,288,512]{2,1,0:T(8,128)(2,1)S(1)} %bitcast_select_fusion), channel_id=1, source_target_pairs={{0,128},{64,192},{128,0},{192,64},{1,129},{65,193},{129,1},{193,65... | collective-permute-start | bytes 1769480 | tf_op jit(solution)/shard_map/ppermute | solution.py:31
  90.9 22.7 %collective-permute-start.17 = (bf16[256,256]{1,0:T(8,128)(2,1)}, bf16[256,256]{1,0:T(8,128)(2,1)}, u32[]{:S(2)}, u32[]{:S(2)}) collective-permute-start(bf16[256,256]{1,0:T(8,128)(2,1)} %convert_element_type.171), channel_id=1, source_target_pairs={{0,16},{16,0},{32,48},{48,32},{1,17},{17,1},{33,49},{49,33},{2,18}... | collective-permute-start | bytes 393224 | tf_op jit(solution)/shard_map/ppermute | solution.py:31
  115.3 4.4 %copy-start.7 = (bf16[2,288,512]{2,1,0:T(8,128)(2,1)}, bf16[2,288,512]{2,1,0:T(8,128)(2,1)S(1)}, u32[]{:S(2)}) copy-start(bf16[2,288,512]{2,1,0:T(8,128)(2,1)S(1)} %broadcast_select_fusion.1.refs_8_) | copy-start | bytes 1769476
  118.8 18.9 %collective-permute-start.18 = (bf16[2,288,512]{2,1,0:T(8,128)(2,1)S(1)}, bf16[2,288,512]{2,1,0:T(8,128)(2,1)S(1)}, u32[]{:S(2)}, u32[]{:S(2)}) collective-permute-start(bf16[2,288,512]{2,1,0:T(8,128)(2,1)S(1)} %broadcast_select_fusion.1.refs_8_), channel_id=1, source_target_pairs={{0,64},{64,0},{128,192},{192,128},{1,65},{65,1},{129,193},{193,129... | collective-permute-start | bytes 1769480 | tf_op jit(solution)/shard_map/ppermute | solution.py:31
  118.8 19.3 %collective-permute-start.19 = (bf16[2,288,512]{2,1,0:T(8,128)(2,1)S(1)}, bf16[2,288,512]{2,1,0:T(8,128)(2,1)S(1)}, u32[]{:S(2)}, u32[]{:S(2)}) collective-permute-start(bf16[2,288,512]{2,1,0:T(8,128)(2,1)S(1)} %broadcast_select_fusion.1.refs_8_), channel_id=1, source_target_pairs={{0,16},{16,32},{32,48},{48,0},{1,17},{17,33},{33,49},{49,1},{2,18}... | collective-permute-start | bytes 1769480 | tf_op jit(solution)/shard_map/ppermute | solution.py:27
  119.7 18.5 %collective-permute-start.20 = (bf16[2,288,512]{2,1,0:T(8,128)(2,1)S(1)}, bf16[2,288,512]{2,1,0:T(8,128)(2,1)S(1)}, u32[]{:S(2)}, u32[]{:S(2)}) collective-permute-start(bf16[2,288,512]{2,1,0:T(8,128)(2,1)S(1)} %broadcast_select_fusion.1.refs_8_), channel_id=1, source_target_pairs={{0,48},{16,0},{32,16},{48,32},{1,49},{17,1},{33,17},{49,33},{2,50}... | collective-permute-start | bytes 1769480 | tf_op jit(solution)/shard_map/ppermute | solution.py:27
  122.2 15.5 %collective-permute-start.21 = (bf16[256,256]{1,0:T(8,128)(2,1)S(1)}, bf16[256,256]{1,0:T(8,128)(2,1)S(1)}, u32[]{:S(2)}, u32[]{:S(2)}) collective-permute-start(bf16[256,256]{1,0:T(8,128)(2,1)S(1)} %convert_element_type.173), channel_id=1, source_target_pairs={{0,32},{16,48},{32,0},{48,16},{1,33},{17,49},{33,1},{49,17},{2,34}... | collective-permute-start | bytes 393224 | tf_op jit(solution)/shard_map/ppermute | solution.py:31
  137.7 6.7 %copy-start.8 = (bf16[2,288,512]{2,1,0:T(8,128)(2,1)}, bf16[2,288,512]{2,1,0:T(8,128)(2,1)S(1)}, u32[]{:S(2)}) copy-start(bf16[2,288,512]{2,1,0:T(8,128)(2,1)S(1)} %collective-permute-done.18.refs_9_) | copy-start | bytes 1769476
  138.1 16.5 %copy-start.11 = (bf16[2,288,512]{2,1,0:T(8,128)(2,1)}, bf16[2,288,512]{2,1,0:T(8,128)(2,1)S(1)}, u32[]{:S(2)}) copy-start(bf16[2,288,512]{2,1,0:T(8,128)(2,1)S(1)} %collective-permute-done.19.refs_16_) | copy-start | bytes 1769476
  138.2 10.7 %copy-start.12 = (bf16[2,288,512]{2,1,0:T(8,128)(2,1)}, bf16[2,288,512]{2,1,0:T(8,128)(2,1)S(1)}, u32[]{:S(2)}) copy-start(bf16[2,288,512]{2,1,0:T(8,128)(2,1)S(1)} %collective-permute-done.20.refs_18_) | copy-start | bytes 1769476
  138.2 16.5 %collective-permute-start.22 = (bf16[2,288,512]{2,1,0:T(8,128)(2,1)S(1)}, bf16[2,288,512]{2,1,0:T(8,128)(2,1)}, u32[]{:S(2)}, u32[]{:S(2)}) collective-permute-start(bf16[2,288,512]{2,1,0:T(8,128)(2,1)S(1)} %collective-permute-done.18.refs_9_), channel_id=1, source_target_pairs={{0,16},{16,32},{32,48},{48,0},{1,17},{17,33},{33,49},{49,1},{2,18}... | collective-permute-start | bytes 1769480 | tf_op jit(solution)/shard_map/ppermute | solution.py:27
  139.4 15.3 %collective-permute-start.23 = (bf16[2,288,512]{2,1,0:T(8,128)(2,1)S(1)}, bf16[2,288,512]{2,1,0:T(8,128)(2,1)}, u32[]{:S(2)}, u32[]{:S(2)}) collective-permute-start(bf16[2,288,512]{2,1,0:T(8,128)(2,1)S(1)} %collective-permute-done.18.refs_9_), channel_id=1, source_target_pairs={{0,48},{16,0},{32,16},{48,32},{1,49},{17,1},{33,17},{49,33},{2,50}... | collective-permute-start | bytes 1769480 | tf_op jit(solution)/shard_map/ppermute | solution.py:27
  141.8 12.9 %collective-permute-start.24 = (bf16[512,256]{1,0:T(8,128)(2,1)S(1)}, bf16[512,256]{1,0:T(8,128)(2,1)S(1)}, u32[]{:S(2)}, u32[]{:S(2)}) collective-permute-start(bf16[512,256]{1,0:T(8,128)(2,1)S(1)} %get-tuple-element.102), channel_id=1, source_target_pairs={{0,128},{64,192},{128,0},{192,64},{1,129},{65,193},{129,1},{193,65... | collective-permute-start | bytes 786440 | tf_op jit(solution)/shard_map/ppermute | solution.py:27
  154.7 14.1 %copy-start.13 = (bf16[512,256]{1,0:T(8,128)(2,1)}, bf16[512,256]{1,0:T(8,128)(2,1)S(1)}, u32[]{:S(2)}) copy-start(bf16[512,256]{1,0:T(8,128)(2,1)S(1)} %collective-permute-done.24) | copy-start | bytes 786436
  154.7 16.1 %collective-permute-start.25 = (bf16[2,288,512]{2,1,0:T(8,128)(2,1)S(1)}, bf16[2,288,512]{2,1,0:T(8,128)(2,1)S(1)}, u32[]{:S(2)}, u32[]{:S(2)}) collective-permute-start(bf16[2,288,512]{2,1,0:T(8,128)(2,1)S(1)} %collective-permute-done.19.refs_16_), channel_id=1, source_target_pairs={{0,16},{16,32},{32,48},{48,0},{1,17},{17,33},{33,49},{49,1},{2,18}... | collective-permute-start | bytes 1769480 | tf_op jit(solution)/shard_map/ppermute | solution.py:27
  155.0 15.8 %collective-permute-start.26 = (bf16[2,288,512]{2,1,0:T(8,128)(2,1)}, bf16[2,288,512]{2,1,0:T(8,128)(2,1)S(1)}, u32[]{:S(2)}, u32[]{:S(2)}) collective-permute-start(bf16[2,288,512]{2,1,0:T(8,128)(2,1)} %collective-permute-done.23.refs_19_), channel_id=1, source_target_pairs={{0,48},{16,0},{32,16},{48,32},{1,49},{17,1},{33,17},{49,33},{2,50}... | collective-permute-start | bytes 1769480 | tf_op jit(solution)/shard_map/ppermute | solution.py:27
  158.0 11.3 %collective-permute-start.27 = (bf16[512,256]{1,0:T(8,128)(2,1)}, bf16[512,256]{1,0:T(8,128)(2,1)S(1)}, u32[]{:S(2)}, u32[]{:S(2)}) collective-permute-start(bf16[512,256]{1,0:T(8,128)(2,1)} %get-tuple-element.108), channel_id=1, source_target_pairs={{0,64},{64,128},{128,192},{192,0},{1,65},{65,129},{129,193},{193,1... | collective-permute-start | bytes 786440 | tf_op jit(solution)/shard_map/ppermute | solution.py:27
  158.3 12.4 %collective-permute-start.28 = (bf16[512,256]{1,0:T(8,128)(2,1)}, bf16[512,256]{1,0:T(8,128)(2,1)}, u32[]{:S(2)}, u32[]{:S(2)}) collective-permute-start(bf16[512,256]{1,0:T(8,128)(2,1)} %get-tuple-element.109), channel_id=1, source_target_pairs={{0,192},{64,0},{128,64},{192,128},{1,193},{65,1},{129,65},{193,129... | collective-permute-start | bytes 786440 | tf_op jit(solution)/shard_map/ppermute | solution.py:27
  179.3 34.9 %collective-permute-start.29 = (f32[256,640]{1,0:T(8,128)}, f32[256,640]{1,0:T(8,128)S(1)}, u32[]{:S(2)}, u32[]{:S(2)}) collective-permute-start(f32[256,640]{1,0:T(8,128)} %slice_bitcast_fusion), channel_id=1, source_target_pairs={{0,8},{8,0},{1,9},{9,1},{2,10},{10,2},{3,11},{11,3},{4,12},{12,4},... | collective-permute-start | bytes 1966088 | tf_op jit(solution)/shard_map/ppermute | solution.py:27
  179.3 34.9 %copy-start = (f32[2,256,640]{2,1,0:T(8,128)S(1)}, f32[2,256,640]{2,1,0:T(8,128)}, u32[]{:S(2)}) copy-start(f32[2,256,640]{2,1,0:T(8,128)} %project.5.a) | copy-start | bytes 3932164
  179.5 28.7 %collective-permute-start.30 = (bf16[256,256]{1,0:T(8,128)(2,1)S(1)}, bf16[256,256]{1,0:T(8,128)(2,1)S(1)}, u32[]{:S(2)}, u32[]{:S(2)}) collective-permute-start(bf16[256,256]{1,0:T(8,128)(2,1)S(1)} %get-tuple-element.143), channel_id=1, source_target_pairs={{0,8},{1,40},{2,72},{3,104},{4,136},{5,168},{6,200},{7,232},{8,16}... | collective-permute-start | bytes 393224 | tf_op jit(solution)/shard_map/ppermute | solution.py:407
  179.6 32.8 %collective-permute-start.31 = (bf16[256,256]{1,0:T(8,128)(2,1)S(1)}, bf16[256,256]{1,0:T(8,128)(2,1)S(1)}, u32[]{:S(2)}, u32[]{:S(2)}) collective-permute-start(bf16[256,256]{1,0:T(8,128)(2,1)S(1)} %get-tuple-element.142), channel_id=1, source_target_pairs={{0,0},{1,56},{2,88},{3,120},{4,152},{5,184},{6,216},{7,248},{8,8},... | collective-permute-start | bytes 393224 | tf_op jit(solution)/shard_map/ppermute | solution.py:407
  (4 other events, 6.4 us)

commit v4 on v3

--- a/solution.py
+++ b/solution.py
@@ -155,10 +155,10 @@
 
 
 def project_body(slots, piece, fresh, table, *refs):
-    out = refs[-1]
+    outs = refs[-2:]
     ma, mb = refs[:slots], refs[slots : 2 * slots]
     left, right = [], []
-    for w in refs[2 * slots : -1 if fresh else -2]:
+    for w in refs[2 * slots : -2 if fresh else -4]:
         if w.shape[2] == piece:
             side = left if len(left) == len(right) else right
             side += [w[i] for i in range(w.shape[0])]
@@ -167,7 +167,7 @@
             right += [w[i, :, piece:] for i in range(w.shape[0])]
     spans = [slice(0, piece), slice(piece, 2 * piece), slice(2 * piece, 2 * piece + HEAD)]
     for core, tokens in ((0, ma), (1, mb)):
-        sums = [0.0 if fresh else refs[-2][core, :, span] for span in spans]
+        sums = [0.0 if fresh else refs[-4 + core][:, span] for span in spans]
         for x, w0, w1 in zip(tokens, left, right):
             x = x[...]
             kt = [w0[piece:], w1[piece:]]
@@ -176,7 +176,7 @@
             sums[1] += jnp.dot(x, w1[:piece], preferred_element_type=f32)
             sums[2] += lax.dot_general(x, kt, (((1,), (1,)), ((), ())), preferred_element_type=f32)
         for span, value in zip(spans, sums):
-            out[core, :, span] = value
+            outs[core][:, span] = value
 
 
 def project(piece, table, mine, other, weights, sofar=None):
@@ -184,31 +184,32 @@
     slots = table.shape[0]
     at = [pl.BlockSpec((tokens, piece), lambda s, tab, n=n: (0, tab[n])) for n in range(slots)]
     full = lambda shape: pl.BlockSpec(shape, lambda s, tab: (0, 0, 0))
-    whole = (2, tokens, 2 * piece + HEAD)
+    whole = (tokens, 2 * piece + HEAD)
+    both = pl.BlockSpec(whole, lambda s, tab: (0, 0))
     fresh = sofar is None
     return pl.pallas_call(
         functools.partial(project_body, slots, piece, fresh),
         grid_spec=pltpu.PrefetchScalarGridSpec(
             num_scalar_prefetch=1,
             grid=(1,),
-            in_specs=at + at + [full(w.shape) for w in weights] + ([] if fresh else [full(whole)]),
-            out_specs=full(whole),
-        ),
-        out_shape=jax.ShapeDtypeStruct(whole, f32),
+            in_specs=at + at + [full(w.shape) for w in weights] + ([] if fresh else [both] * 2),
+            out_specs=[both] * 2,
+        ),
+        out_shape=[jax.ShapeDtypeStruct(whole, f32)] * 2,
         cost_estimate=pl.CostEstimate(
             flops=8 * tokens * piece * piece * slots,
             bytes_accessed=slots * 8 * tokens * piece + 8 * tokens * piece,
             transcendentals=0,
         ),
         name="project",
-    )(table, *[mine] * slots, *[other] * slots, *weights, *([] if fresh else [sofar]))
+    )(table, *[mine] * slots, *[other] * slots, *weights, *([] if fresh else sofar))
 
 
 def rope_body(at, a, b, cosine, sine, queries, keys):
     even = lax.broadcasted_iota(jnp.int32, cosine.shape, 1) % 2 == 0
     width, part = queries.shape[1], keys.shape[0]
     for start in range(0, width + HEAD, HEAD):
-        x = a[0, :, start : start + HEAD] + b[:, start : start + HEAD]
+        x = a[:, start : start + HEAD] + b[:, start : start + HEAD]
         swapped = jnp.where(even, pltpu.roll(x, HEAD - 1, 1), pltpu.roll(x, 1, 1))
         x = x * cosine[...] + swapped * sine[...]
         if start < width:
@@ -228,7 +229,7 @@
     return pl.pallas_call(
         rope_body,
         grid=(1,),
-        in_specs=[pl.BlockSpec(memory_space=pltpu.SMEM), full((1, tokens, width))]
+        in_specs=[pl.BlockSpec(memory_space=pltpu.SMEM), full((tokens, width))]
         + [full(x.shape) for x in (b, cosine, sine)],
         out_specs=[full(shape) for shape in shapes],
         out_shape=[jax.ShapeDtypeStruct(shape, bf16) for shape in shapes],
@@ -415,7 +416,7 @@
     all_tokens = tokens * NY * NZ * 2
     hessian = assemble(2.0 / all_tokens, slots, hess, mirrored[0], mirrored[1], extra)
     at = ((column * kwidth) % HEAD) // kwidth
-    queries, keys = rope(at.reshape(1), kwidth, raw, send(raw[1], "k", 1), cosine, sine)
+    queries, keys = rope(at.reshape(1), kwidth, raw[0], send(raw[1], "k", 1), cosine, sine)
     return (queries, keys.T, hessian)
 
 

time: 216 us -> 215 us (level)
    unnamed x40 -> x42, local copies, waits for them, and re-layouts: 2.92 us -> 4.64 us
where the time goes in v4:
time: 215 us; the launch traced here: 214 us
  waiting for transfers between devices  85.2 us (40%)
  Pallas kernels  46.1 us (21%)
  starting transfers between devices  44.1 us (21%)
  other arithmetic  28.5 us (13%)
  local copies, waits for them, and re-layouts  7.85 us (4%)
    ppermute x7, waiting for transfers between devices, swap(): return lax.ppermute(array, axis, [(i, i ^ bit) for i in range(SIZES[axis])])  37.2 us
    ppermute x23, starting transfers between devices, send(): return lax.ppermute(array, axis, [(i, (i + shift) % n) for i in range(n)])  29.6 us
    ppermute x23, waiting for transfers between devices, send(): return lax.ppermute(array, axis, [(i, (i + shift) % n) for i in range(n)])  24.3 us
    ppermute x2, waiting for transfers between devices, shards(): lax.ppermute(jnp.where(second, tiles[1], tiles[0]), ALL, partner_moves(n))  23.7 us
    pallas_call x8, Pallas kernels, pack(): pl.pallas_call(pack_body, grid_spec=pltpu.PrefetchScalarGridSpec(num_scal...  17.2 us
    pallas_call x3, Pallas kernels, project(): pl.pallas_call(functools.partial(project_body, slots, piece, fresh), grid...  15.3 us
    pallas_call x1, Pallas kernels, gram(): pl.pallas_call(gram_body, grid_spec=pltpu.PrefetchScalarGridSpec(num_scal...  10.8 us
    ppermute x2, starting transfers between devices, shards(): lax.ppermute(jnp.where(second, tiles[1], tiles[0]), ALL, partner_moves(n))  8.81 us
  transfers between devices with their start and end apart: 32, of which 16 were waited for; matrix products, arithmetic and copies ran while one was open for 11% of the time, Pallas kernels for 16%

profile of v4, /device:TPU:132, one launch (start us, length us, event | category | flops | bytes accessed | tf_op | source)
XLA Modules:
  0.0 214.4 jit_solution(5807224046026028605)
XLA Ops:
  0.6 2.1 pack.8
  3.5 2.2 %pack.9 = bf16[2,576,512]{2,1,0:T(8,128)(2,1)} custom-call(s32[1]{0:T(128)} %bitcast.6.table, bf16[8192,512]{1,0:T(8,128)(2,1)} %bitcast.55, bf16[64,8192]{1,0:T(8,128)(2,1)} %bitcast.63), custom_call_target="tpu_custom_call" | custom-call | bytes 2359296 | tf_op jit(solution)/shard_map/pack/pallas_call | solution.py:74
  5.8 2.4 %fusion.6 = (bf16[576,512]{1,0:T(8,128)(2,1)}, bf16[576,512]{1,0:T(8,128)(2,1)}) fusion(bf16[2,576,512]{2,1,0:T(8,128)(2,1)S(1)} %collective-permute-done, bf16[2,576,512]{2,1,0:T(8,128)(2,1)} %pack.9, pred[]{:T(512)S(6)} %eq.136), kind=kLoop, calls=%fused_computation.19 | loop fusion | flops 589824 | bytes 3538945 | tf_op jit(solution)/shard_map/jit(_where)/select_n | solution.py:310
  8.2 2.2 %pack.11 = bf16[2,576,512]{2,1,0:T(8,128)(2,1)} custom-call(s32[1]{0:T(128)} %bitcast.11.table, bf16[8192,512]{1,0:T(8,128)(2,1)} %bitcast.56, bf16[64,8192]{1,0:T(8,128)(2,1)} %bitcast.64), custom_call_target="tpu_custom_call" | custom-call | bytes 2359296 | tf_op jit(solution)/shard_map/pack/pallas_call | solution.py:74
  10.4 2.1 pack.10
  13.6 3.0 %collective-permute-start.3 = (bf16[576,512]{1,0:T(8,128)(2,1)}, bf16[576,512]{1,0:T(8,128)(2,1)}, u32[]{:S(2)}, u32[]{:S(2)}) collective-permute-start(bf16[576,512]{1,0:T(8,128)(2,1)} %get-tuple-element.81), channel_id=1, source_target_pairs={{0,48},{16,0},{32,16},{48,32},{1,49},{17,1},{33,17},{49,33},{2,50}... | collective-permute-start | bytes 1769480 | tf_op jit(solution)/shard_map/ppermute | solution.py:27
  17.5 2.1 pack.13
  19.6 2.1 pack.12
  21.7 2.1 pack.15
  23.9 2.3 %pack.14 = bf16[2,576,512]{2,1,0:T(8,128)(2,1)} custom-call(s32[1]{0:T(128)} %bitcast.14.table, bf16[8192,512]{1,0:T(8,128)(2,1)} %bitcast.61, bf16[64,8192]{1,0:T(8,128)(2,1)} %bitcast.69), custom_call_target="tpu_custom_call" | custom-call | bytes 2359296 | tf_op jit(solution)/shard_map/pack/pallas_call | solution.py:74
  26.2 3.8 %collective-permute-done.3 = bf16[576,512]{1,0:T(8,128)(2,1)} collective-permute-done((bf16[576,512]{1,0:T(8,128)(2,1)}, bf16[576,512]{1,0:T(8,128)(2,1)}, u32[]{:S(2)}, u32[]{:S(2)}) %collective-permute-start.3) | collective-permute-done | bytes 589856 | tf_op jit(solution)/shard_map/ppermute | solution.py:27
  29.9 2.4 %select_select_fusion.1 = bf16[2,576,512]{2,1,0:T(8,128)(2,1)} fusion(bf16[2,576,512]{2,1,0:T(8,128)(2,1)S(1)} %copy-done.5, bf16[2,576,512]{2,1,0:T(8,128)(2,1)S(1)} %collective-permute-done.4, pred[]{:T(512)S(6)} %eq.137, pred[]{:T(512)S(6)} %eq.136, bf16[576,512]{1,0:T(8,128)(2,1)} %collective-permute-done.3), kind=kLoop, calls=%fused_computation.14 | loop fusion | flops 1179648 | bytes 4128770 | tf_op jit(solution)/shard_map/jit(_where)/select_n | solution.py:323
  32.3 1.1 collective-permute-done.1
  33.4 2.4 %select_select_fusion.2 = bf16[2,576,512]{2,1,0:T(8,128)(2,1)} fusion(bf16[2,576,512]{2,1,0:T(8,128)(2,1)S(1)} %copy-done.4, bf16[2,576,512]{2,1,0:T(8,128)(2,1)S(1)} %collective-permute-done.2, pred[]{:T(512)S(6)} %eq.136, pred[]{:T(512)S(6)} %eq.135, bf16[576,512]{1,0:T(8,128)(2,1)} %collective-permute-done.1), kind=kLoop, calls=%fused_computation.15 | loop fusion | flops 1179648 | bytes 4128770 | tf_op jit(solution)/shard_map/jit(_where)/select_n | solution.py:322
  35.8 3.2 %collective-permute-start.9 = (bf16[2,576,512]{2,1,0:T(8,128)(2,1)}, bf16[2,576,512]{2,1,0:T(8,128)(2,1)}, u32[]{:S(2)}, u32[]{:S(2)}) collective-permute-start(bf16[2,576,512]{2,1,0:T(8,128)(2,1)} %select_select_fusion.1), channel_id=1, source_target_pairs={{0,48},{16,0},{32,16},{48,32},{1,49},{17,1},{33,17},{49,33},{2,50}... | collective-permute-start | bytes 3538952 | tf_op jit(solution)/shard_map/ppermute | solution.py:27
  40.2 3.1 %fusion.3 = f32[256]{0:T(256)S(1)} fusion(bf16[256,8192]{1,0:T(8,128)(2,1)} %collective-permute-done.5), kind=kLoop, calls=%fused_computation.7 | loop fusion | flops 6291200 | bytes 4195328 | tf_op jit(solution)/shard_map/reduce_sum | solution.py:61
  43.3 4.0 %fusion.5 = (bf16[256,8192]{1,0:T(8,128)(2,1)S(1)}, bf16[256,8192]{1,0:T(8,128)(2,1)S(1)}) fusion(bf16[256,8192]{1,0:T(8,128)(2,1)} %collective-permute-done.5, f32[256]{0:T(256)S(1)} %add_rsqrt_fusion, f32[8192]{0:T(1024)S(1)} %copy-done.16, f32[256]{0:T(256)S(1)} %add_rsqrt_fusion.1, bf16[256,8192]{1,0:T(8,128)(2,1)S(1)} %copy-done.3), kind=kLoop, calls=%fused_computation.9 | loop fusion | flops 16777216 | bytes 16812032 | tf_op jit(solution)/shard_map/convert_element_type | solution.py:62
  47.5 1.8 copy-done.1
  51.7 10.8 %gram.1 = (bf16[2,512,256]{2,1,0:T(8,128)(2,1)}, bf16[2,512,256]{2,1,0:T(8,128)(2,1)}, f32[12,512,256]{2,1,0:T(8,128)}) custom-call(s32[4,16]{1,0:T(4,128)} %pad_add_fusion.table, bf16[256,8192]{1,0:T(8,128)(2,1)} %copy-done.2, bf16[256,8192]{1,0:T(8,128)(2,1)} %copy-done.2, bf16[256,8192]{1,0:T(8,128)(2,1)} %copy-done.2, bf16[256,8192]{1,0:T(8,128)(2,1)} %copy-done.2, ...), custom_call_target="tpu_custom_call" | custom-call | flops 4294967296 | bytes 16777216 | tf_op jit(solution)/shard_map/gram/pallas_call | solution.py:138
  62.5 2.7 %collective-permute-done.8 = bf16[2,576,512]{2,1,0:T(8,128)(2,1)S(1)} collective-permute-done((bf16[2,576,512]{2,1,0:T(8,128)(2,1)}, bf16[2,576,512]{2,1,0:T(8,128)(2,1)S(1)}, u32[]{:S(2)}, u32[]{:S(2)}) %collective-permute-start.8) | collective-permute-done | bytes 1179680 | tf_op jit(solution)/shard_map/ppermute | solution.py:27
  65.3 1.5 select_select_fusion
  66.9 1.6 collective-permute-start.13
  68.9 1.1 collective-permute-start.12
  70.0 1.2 collective-permute-start.10
  71.2 2.0 collective-permute-start.11
  73.2 2.5 %fusion.30 = (f32[4,512,256]{2,1,0:T(8,128)S(1)}, f32[4,512,256]{2,1,0:T(8,128)S(1)}) fusion(f32[12,512,256]{2,1,0:T(8,128)} %get-tuple-element.89), kind=kLoop, calls=%fused_computation.106 | loop fusion | bytes 8388608 | tf_op jit(solution)/shard_map/slice | solution.py:362
  75.8 8.0 %collective-permute-done.10 = bf16[2,512,256]{2,1,0:T(8,128)(2,1)S(1)} collective-permute-done((bf16[2,512,256]{2,1,0:T(8,128)(2,1)S(1)}, bf16[2,512,256]{2,1,0:T(8,128)(2,1)S(1)}, u32[]{:S(2)}, u32[]{:S(2)}) %collective-permute-start.10) | collective-permute-done | bytes 524320 | tf_op jit(solution)/shard_map/ppermute | solution.py:27
  85.5 1.7 collective-permute-start.15
  87.3 1.6 collective-permute-start.16
  92.2 21.4 %collective-permute-done.17 = bf16[256,256]{1,0:T(8,128)(2,1)} collective-permute-done((bf16[256,256]{1,0:T(8,128)(2,1)}, bf16[256,256]{1,0:T(8,128)(2,1)}, u32[]{:S(2)}, u32[]{:S(2)}) %collective-permute-start.17) | collective-permute-done | bytes 131104 | tf_op jit(solution)/shard_map/ppermute | solution.py:31
  115.4 3.4 %fusion.10 = (bf16[512,256]{1,0:T(8,128)(2,1)}, bf16[512,256]{1,0:T(8,128)(2,1)S(1)}, bf16[512,256]{1,0:T(8,128)(2,1)}, f32[512,256]{1,0:T(8,128)S(1)}) fusion(f32[12,512,256]{2,1,0:T(8,128)} %get-tuple-element.89, bf16[4,512,256]{2,1,0:T(8,128)(2,1)} %bitcast.24, bf16[4,512,256]{2,1,0:T(8,128)(2,1)} %bitcast.23), kind=kLoop, calls=%fused_computation.32 | loop fusion | flops 2490368 | bytes 5505024 | tf_op jit(solution)/shard_map/convert_element_type | solution.py:371
  119.7 2.4 %collective-permute-start.20 = (bf16[2,288,512]{2,1,0:T(8,128)(2,1)S(1)}, bf16[2,288,512]{2,1,0:T(8,128)(2,1)S(1)}, u32[]{:S(2)}, u32[]{:S(2)}) collective-permute-start(bf16[2,288,512]{2,1,0:T(8,128)(2,1)S(1)} %broadcast_select_fusion.1.refs_8_), channel_id=1, source_target_pairs={{0,48},{16,0},{32,16},{48,32},{1,49},{17,1},{33,17},{49,33},{2,50}... | collective-permute-start | bytes 1769480 | tf_op jit(solution)/shard_map/ppermute | solution.py:27
  123.6 14.2 %collective-permute-done.21 = bf16[256,256]{1,0:T(8,128)(2,1)S(1)} collective-permute-done((bf16[256,256]{1,0:T(8,128)(2,1)S(1)}, bf16[256,256]{1,0:T(8,128)(2,1)S(1)}, u32[]{:S(2)}, u32[]{:S(2)}) %collective-permute-start.21) | collective-permute-done | bytes 131104 | tf_op jit(solution)/shard_map/ppermute | solution.py:31
  140.0 2.3 %collective-permute-start.23 = (bf16[2,288,512]{2,1,0:T(8,128)(2,1)S(1)}, bf16[2,288,512]{2,1,0:T(8,128)(2,1)S(1)}, u32[]{:S(2)}, u32[]{:S(2)}) collective-permute-start(bf16[2,288,512]{2,1,0:T(8,128)(2,1)S(1)} %collective-permute-done.18.refs_9_), channel_id=1, source_target_pairs={{0,48},{16,0},{32,16},{48,32},{1,49},{17,1},{33,17},{49,33},{2,50}... | collective-permute-start | bytes 1769480 | tf_op jit(solution)/shard_map/ppermute | solution.py:27
  142.4 2.1 %collective-permute-start.24 = (bf16[512,256]{1,0:T(8,128)(2,1)S(1)}, bf16[512,256]{1,0:T(8,128)(2,1)S(1)}, u32[]{:S(2)}, u32[]{:S(2)}) collective-permute-start(bf16[512,256]{1,0:T(8,128)(2,1)S(1)} %get-tuple-element.111), channel_id=1, source_target_pairs={{0,128},{64,192},{128,0},{192,64},{1,129},{65,193},{129,1},{193,65... | collective-permute-start | bytes 786440 | tf_op jit(solution)/shard_map/ppermute | solution.py:27
  145.0 4.2 %project.3 = (f32[256,640]{1,0:T(8,128)}, f32[256,640]{1,0:T(8,128)}) custom-call(s32[4]{0:T(128)} %get-tuple-element.167.table, bf16[256,8192]{1,0:T(8,128)(2,1)} %copy-done.2, bf16[256,8192]{1,0:T(8,128)(2,1)} %copy-done.2, bf16[256,8192]{1,0:T(8,128)(2,1)} %copy-done.2, bf16[256,8192]{1,0:T(8,128)(2,1)} %copy-done.2, bf16[256,8192]{1,0:T(8,128)(2,1)} %copy-done.1, ...), custom_call_target="tpu_custom_call" | custom-call | flops 536870912 | bytes 2621440 | tf_op jit(solution)/shard_map/project/pallas_call | solution.py:190
  149.2 6.1 %collective-permute-done.24 = bf16[512,256]{1,0:T(8,128)(2,1)S(1)} collective-permute-done((bf16[512,256]{1,0:T(8,128)(2,1)S(1)}, bf16[512,256]{1,0:T(8,128)(2,1)S(1)}, u32[]{:S(2)}, u32[]{:S(2)}) %collective-permute-start.24) | collective-permute-done | bytes 262176 | tf_op jit(solution)/shard_map/ppermute | solution.py:27
  156.3 3.0 %collective-permute-start.26 = (bf16[2,288,512]{2,1,0:T(8,128)(2,1)}, bf16[2,288,512]{2,1,0:T(8,128)(2,1)S(1)}, u32[]{:S(2)}, u32[]{:S(2)}) collective-permute-start(bf16[2,288,512]{2,1,0:T(8,128)(2,1)} %copy-done.13), channel_id=1, source_target_pairs={{0,48},{16,0},{32,16},{48,32},{1,49},{17,1},{33,17},{49,33},{2,50}... | collective-permute-start | bytes 1769480 | tf_op jit(solution)/shard_map/ppermute | solution.py:27
  159.7 3.5 %collective-permute-start.28 = (bf16[512,256]{1,0:T(8,128)(2,1)}, bf16[512,256]{1,0:T(8,128)(2,1)}, u32[]{:S(2)}, u32[]{:S(2)}) collective-permute-start(bf16[512,256]{1,0:T(8,128)(2,1)} %get-tuple-element.120), channel_id=1, source_target_pairs={{0,192},{64,0},{128,64},{192,128},{1,193},{65,1},{129,65},{193,129... | collective-permute-start | bytes 786440 | tf_op jit(solution)/shard_map/ppermute | solution.py:27
  163.8 6.3 %project.4 = (f32[256,640]{1,0:T(8,128)}, f32[256,640]{1,0:T(8,128)}) custom-call(s32[8]{0:T(128)} %pad_add_fusion.2.table, bf16[256,8192]{1,0:T(8,128)(2,1)} %copy-done.2, bf16[256,8192]{1,0:T(8,128)(2,1)} %copy-done.2, bf16[256,8192]{1,0:T(8,128)(2,1)} %copy-done.2, bf16[256,8192]{1,0:T(8,128)(2,1)} %copy-done.2, bf16[256,8192]{1,0:T(8,128)(2,1)} %copy-done.2, ...), custom_call_target="tpu_custom_call" | custom-call | flops 1073741824 | bytes 4718592 | tf_op jit(solution)/shard_map/project/pallas_call | solution.py:190
  170.6 1.5 collective-permute-done.28
  172.1 1.6 fusion.29
  173.8 4.8 %project.5 = (f32[256,640]{1,0:T(8,128)}, f32[256,640]{1,0:T(8,128)}) custom-call(s32[4]{0:T(128)} %get-tuple-element.168.table, bf16[256,8192]{1,0:T(8,128)(2,1)} %copy-done.2, bf16[256,8192]{1,0:T(8,128)(2,1)} %copy-done.2, bf16[256,8192]{1,0:T(8,128)(2,1)} %copy-done.2, bf16[256,8192]{1,0:T(8,128)(2,1)} %copy-done.2, bf16[256,8192]{1,0:T(8,128)(2,1)} %copy-done.1, ...), custom_call_target="tpu_custom_call" | custom-call | flops 536870912 | bytes 2621440 | tf_op jit(solution)/shard_map/project/pallas_call | solution.py:190
  179.1 8.7 %collective-permute-start.31 = (bf16[256,256]{1,0:T(8,128)(2,1)S(1)}, bf16[256,256]{1,0:T(8,128)(2,1)S(1)}, u32[]{:S(2)}, u32[]{:S(2)}) collective-permute-start(bf16[256,256]{1,0:T(8,128)(2,1)S(1)} %get-tuple-element.160), channel_id=1, source_target_pairs={{0,0},{1,56},{2,88},{3,120},{4,152},{5,184},{6,216},{7,248},{8,8},... | collective-permute-start | bytes 393224 | tf_op jit(solution)/shard_map/ppermute | solution.py:408
  187.9 19.5 %collective-permute-done.30.r0 = bf16[256,256]{1,0:T(8,128)(2,1)S(1)} collective-permute-done((bf16[256,256]{1,0:T(8,128)(2,1)S(1)}, bf16[256,256]{1,0:T(8,128)(2,1)S(1)}, u32[]{:S(2)}, u32[]{:S(2)}) %collective-permute-start.30) | collective-permute-done | bytes 131104 | tf_op jit(solution)/shard_map/ppermute | solution.py:408
  207.4 4.2 %collective-permute-done.31.r1 = bf16[256,256]{1,0:T(8,128)(2,1)S(1)} collective-permute-done((bf16[256,256]{1,0:T(8,128)(2,1)S(1)}, bf16[256,256]{1,0:T(8,128)(2,1)S(1)}, u32[]{:S(2)}, u32[]{:S(2)}) %collective-permute-start.31) | collective-permute-done | bytes 131104 | tf_op jit(solution)/shard_map/ppermute | solution.py:408
  211.6 1.7 assemble.1
  213.3 1.1 rope.1
  (129 shorter events, 21.1 us)
Async XLA Ops:
  2.8 3.1 %collective-permute-start = (bf16[2,576,512]{2,1,0:T(8,128)(2,1)}, bf16[2,576,512]{2,1,0:T(8,128)(2,1)S(1)}, u32[]{:S(2)}, u32[]{:S(2)}) collective-permute-start(bf16[2,576,512]{2,1,0:T(8,128)(2,1)} %pack.8), channel_id=1, source_target_pairs={{0,8},{8,0},{1,9},{9,1},{2,10},{10,2},{3,11},{11,3},{4,12},{12,4},... | collective-permute-start | bytes 3538952 | tf_op jit(solution)/shard_map/ppermute | solution.py:27
  10.4 2.7 %copy-start.18 = (s32[4]{0:T(128)S(1)}, s32[4]{0:T(128)}, u32[]{:S(2)}) copy-start(s32[4]{0:T(128)} %constant.318.clone) | copy-start | bytes 52
  12.6 27.6 %collective-permute-start.5 = (bf16[256,8192]{1,0:T(8,128)(2,1)}, bf16[256,8192]{1,0:T(8,128)(2,1)}, u32[]{:S(2)}, u32[]{:S(2)}) collective-permute-start(bf16[256,8192]{1,0:T(8,128)(2,1)} %param.7), channel_id=1, source_target_pairs={{0,8},{8,0},{1,9},{9,1},{2,10},{10,2},{3,11},{11,3},{4,12},{12,4},... | collective-permute-start | bytes 12582920 | tf_op jit(solution)/shard_map/ppermute | solution.py:27
  12.9 17.1 %collective-permute-start.4 = (bf16[2,576,512]{2,1,0:T(8,128)(2,1)}, bf16[2,576,512]{2,1,0:T(8,128)(2,1)S(1)}, u32[]{:S(2)}, u32[]{:S(2)}) collective-permute-start(bf16[2,576,512]{2,1,0:T(8,128)(2,1)} %pack.11), channel_id=1, source_target_pairs={{0,8},{8,0},{1,9},{9,1},{2,10},{10,2},{3,11},{11,3},{4,12},{12,4},... | collective-permute-start | bytes 3538952 | tf_op jit(solution)/shard_map/ppermute | solution.py:27
  13.1 20.4 %collective-permute-start.2 = (bf16[2,576,512]{2,1,0:T(8,128)(2,1)}, bf16[2,576,512]{2,1,0:T(8,128)(2,1)S(1)}, u32[]{:S(2)}, u32[]{:S(2)}) collective-permute-start(bf16[2,576,512]{2,1,0:T(8,128)(2,1)} %pack.10), channel_id=1, source_target_pairs={{0,8},{8,0},{1,9},{9,1},{2,10},{10,2},{3,11},{11,3},{4,12},{12,4},... | collective-permute-start | bytes 3538952 | tf_op jit(solution)/shard_map/ppermute | solution.py:27
  13.6 16.3 %collective-permute-start.3 = (bf16[576,512]{1,0:T(8,128)(2,1)}, bf16[576,512]{1,0:T(8,128)(2,1)}, u32[]{:S(2)}, u32[]{:S(2)}) collective-permute-start(bf16[576,512]{1,0:T(8,128)(2,1)} %get-tuple-element.81), channel_id=1, source_target_pairs={{0,48},{16,0},{32,16},{48,32},{1,49},{17,1},{33,17},{49,33},{2,50}... | collective-permute-start | bytes 1769480 | tf_op jit(solution)/shard_map/ppermute | solution.py:27
  16.7 16.7 %collective-permute-start.1 = (bf16[576,512]{1,0:T(8,128)(2,1)}, bf16[576,512]{1,0:T(8,128)(2,1)}, u32[]{:S(2)}, u32[]{:S(2)}) collective-permute-start(bf16[576,512]{1,0:T(8,128)(2,1)} %get-tuple-element.76), channel_id=1, source_target_pairs={{0,16},{16,32},{32,48},{48,0},{1,17},{17,33},{33,49},{49,1},{2,18}... | collective-permute-start | bytes 1769480 | tf_op jit(solution)/shard_map/ppermute | solution.py:27
  23.9 6.1 %copy-start.5 = (bf16[2,576,512]{2,1,0:T(8,128)(2,1)S(1)}, bf16[2,576,512]{2,1,0:T(8,128)(2,1)}, u32[]{:S(2)}) copy-start(bf16[2,576,512]{2,1,0:T(8,128)(2,1)} %pack.13) | copy-start | bytes 3538948
  26.2 7.3 %copy-start.4 = (bf16[2,576,512]{2,1,0:T(8,128)(2,1)S(1)}, bf16[2,576,512]{2,1,0:T(8,128)(2,1)}, u32[]{:S(2)}) copy-start(bf16[2,576,512]{2,1,0:T(8,128)(2,1)} %pack.12) | copy-start | bytes 3538948
  29.9 10.1 %collective-permute-start.7 = (bf16[2,576,512]{2,1,0:T(8,128)(2,1)}, bf16[2,576,512]{2,1,0:T(8,128)(2,1)S(1)}, u32[]{:S(2)}, u32[]{:S(2)}) collective-permute-start(bf16[2,576,512]{2,1,0:T(8,128)(2,1)} %pack.15), channel_id=1, source_target_pairs={{0,8},{8,0},{1,9},{9,1},{2,10},{10,2},{3,11},{11,3},{4,12},{12,4},... | collective-permute-start | bytes 3538952 | tf_op jit(solution)/shard_map/ppermute | solution.py:27
  29.9 9.1 %copy-start.3 = (bf16[256,8192]{1,0:T(8,128)(2,1)S(1)}, bf16[256,8192]{1,0:T(8,128)(2,1)}, u32[]{:S(2)}) copy-start(bf16[256,8192]{1,0:T(8,128)(2,1)} %param.7) | copy-start | bytes 12582916
  35.8 4.2 %copy-start.6 = (bf16[2,576,512]{2,1,0:T(8,128)(2,1)S(1)}, bf16[2,576,512]{2,1,0:T(8,128)(2,1)}, u32[]{:S(2)}) copy-start(bf16[2,576,512]{2,1,0:T(8,128)(2,1)} %pack.14) | copy-start | bytes 3538948
  35.8 29.4 %collective-permute-start.8 = (bf16[2,576,512]{2,1,0:T(8,128)(2,1)}, bf16[2,576,512]{2,1,0:T(8,128)(2,1)S(1)}, u32[]{:S(2)}, u32[]{:S(2)}) collective-permute-start(bf16[2,576,512]{2,1,0:T(8,128)(2,1)} %select_select_fusion.2), channel_id=1, source_target_pairs={{0,16},{16,32},{32,48},{48,0},{1,17},{17,33},{33,49},{49,1},{2,18}... | collective-permute-start | bytes 3538952 | tf_op jit(solution)/shard_map/ppermute | solution.py:27
  35.8 29.4 %collective-permute-start.9 = (bf16[2,576,512]{2,1,0:T(8,128)(2,1)}, bf16[2,576,512]{2,1,0:T(8,128)(2,1)}, u32[]{:S(2)}, u32[]{:S(2)}) collective-permute-start(bf16[2,576,512]{2,1,0:T(8,128)(2,1)} %select_select_fusion.1), channel_id=1, source_target_pairs={{0,48},{16,0},{32,16},{48,32},{1,49},{17,1},{33,17},{49,33},{2,50}... | collective-permute-start | bytes 3538952 | tf_op jit(solution)/shard_map/ppermute | solution.py:27
  40.1 3.1 %copy-start.16 = (f32[8192]{0:T(1024)S(1)}, f32[8192]{0:T(1024)}, u32[]{:S(2)}) copy-start(f32[8192]{0:T(1024)} %param.8) | copy-start | bytes 98308
  47.3 2.0 copy-start.1
  47.3 3.3 %copy-start.2 = (bf16[256,8192]{1,0:T(8,128)(2,1)}, bf16[256,8192]{1,0:T(8,128)(2,1)S(1)}, u32[]{:S(2)}) copy-start(bf16[256,8192]{1,0:T(8,128)(2,1)S(1)} %get-tuple-element.163.refs_0_.refs_1_.refs_2_.refs_3_.refs_8_.refs_4_.refs_5_.refs_6_.refs_7_) | copy-start | bytes 12582916
  50.6 11.8 %collective-permute-start.6 = (bf16[256,256]{1,0:T(8,128)(2,1)S(1)}, bf16[256,256]{1,0:T(8,128)(2,1)S(1)}, u32[]{:S(2)}, u32[]{:S(2)}) collective-permute-start(bf16[256,256]{1,0:T(8,128)(2,1)S(1)} %get-tuple-element.171), channel_id=1, source_target_pairs={{0,64},{64,0},{128,192},{192,128},{1,65},{65,1},{129,193},{193,129... | collective-permute-start | bytes 393224 | tf_op jit(solution)/shard_map/ppermute | solution.py:31
  66.9 8.9 %collective-permute-start.13 = (bf16[256,256]{1,0:T(8,128)(2,1)S(1)}, bf16[256,256]{1,0:T(8,128)(2,1)S(1)}, u32[]{:S(2)}, u32[]{:S(2)}) collective-permute-start(bf16[256,256]{1,0:T(8,128)(2,1)S(1)} %convert_element_type.155), channel_id=1, source_target_pairs={{0,128},{64,192},{128,0},{192,64},{1,129},{65,193},{129,1},{193,65... | collective-permute-start | bytes 393224 | tf_op jit(solution)/shard_map/ppermute | solution.py:31
  68.5 2.7 %copy-start.19 = (bf16[2,512,256]{2,1,0:T(8,128)(2,1)S(1)}, bf16[2,512,256]{2,1,0:T(8,128)(2,1)}, u32[]{:S(2)}) copy-start(bf16[2,512,256]{2,1,0:T(8,128)(2,1)} %get-tuple-element.97) | copy-start | bytes 1572868
  68.9 16.6 %collective-permute-start.12 = (bf16[2,288,512]{2,1,0:T(8,128)(2,1)S(1)}, bf16[2,288,512]{2,1,0:T(8,128)(2,1)S(1)}, u32[]{:S(2)}, u32[]{:S(2)}) collective-permute-start(bf16[2,288,512]{2,1,0:T(8,128)(2,1)S(1)} %dynamic-slice_bitcast_fusion), channel_id=1, source_target_pairs={{0,64},{64,0},{128,192},{192,128},{1,65},{65,1},{129,193},{193,129... | collective-permute-start | bytes 1769480 | tf_op jit(solution)/shard_map/ppermute | solution.py:31
  70.0 13.8 %collective-permute-start.10 = (bf16[2,512,256]{2,1,0:T(8,128)(2,1)S(1)}, bf16[2,512,256]{2,1,0:T(8,128)(2,1)S(1)}, u32[]{:S(2)}, u32[]{:S(2)}) collective-permute-start(bf16[2,512,256]{2,1,0:T(8,128)(2,1)S(1)} %copy-done.20), channel_id=1, source_target_pairs={{0,16},{16,32},{32,48},{48,0},{1,17},{17,33},{33,49},{49,1},{2,18}... | collective-permute-start | bytes 1572872 | tf_op jit(solution)/shard_map/ppermute | solution.py:27
  71.2 12.7 %collective-permute-start.11 = (bf16[2,512,256]{2,1,0:T(8,128)(2,1)S(1)}, bf16[2,512,256]{2,1,0:T(8,128)(2,1)S(1)}, u32[]{:S(2)}, u32[]{:S(2)}) collective-permute-start(bf16[2,512,256]{2,1,0:T(8,128)(2,1)S(1)} %copy-done.19), channel_id=1, source_target_pairs={{0,48},{16,0},{32,16},{48,32},{1,49},{17,1},{33,17},{49,33},{2,50}... | collective-permute-start | bytes 1572872 | tf_op jit(solution)/shard_map/ppermute | solution.py:27
  84.0 5.7 %copy-start.17 = (s32[256]{0:T(256)S(1)}, s32[256]{0:T(256)}, u32[]{:S(2)}) copy-start(s32[256]{0:T(256)} %param.9) | copy-start | bytes 3076
  85.5 29.8 %collective-permute-start.15 = (bf16[2,2,512,256]{3,2,1,0:T(8,128)(2,1)S(1)}, bf16[2,2,512,256]{3,2,1,0:T(8,128)(2,1)}, u32[]{:S(2)}, u32[]{:S(2)}) collective-permute-start(bf16[2,2,512,256]{3,2,1,0:T(8,128)(2,1)S(1)} %get-tuple-element.101), channel_id=1, source_target_pairs={{0,16},{16,32},{32,48},{48,0},{1,17},{17,33},{33,49},{49,1},{2,18}... | collective-permute-start | bytes 3145736 | tf_op jit(solution)/shard_map/ppermute | solution.py:27
  87.3 28.1 %collective-permute-start.16 = (bf16[2,2,512,256]{3,2,1,0:T(8,128)(2,1)S(1)}, bf16[2,2,512,256]{3,2,1,0:T(8,128)(2,1)}, u32[]{:S(2)}, u32[]{:S(2)}) collective-permute-start(bf16[2,2,512,256]{3,2,1,0:T(8,128)(2,1)S(1)} %get-tuple-element.102), channel_id=1, source_target_pairs={{0,48},{16,0},{32,16},{48,32},{1,49},{17,1},{33,17},{49,33},{2,50}... | collective-permute-start | bytes 3145736 | tf_op jit(solution)/shard_map/ppermute | solution.py:27
  88.9 26.4 %collective-permute-start.14 = (bf16[2,288,512]{2,1,0:T(8,128)(2,1)S(1)}, bf16[2,288,512]{2,1,0:T(8,128)(2,1)S(1)}, u32[]{:S(2)}, u32[]{:S(2)}) collective-permute-start(bf16[2,288,512]{2,1,0:T(8,128)(2,1)S(1)} %bitcast_select_fusion), channel_id=1, source_target_pairs={{0,128},{64,192},{128,0},{192,64},{1,129},{65,193},{129,1},{193,65... | collective-permute-start | bytes 1769480 | tf_op jit(solution)/shard_map/ppermute | solution.py:31
  90.9 22.7 %collective-permute-start.17 = (bf16[256,256]{1,0:T(8,128)(2,1)}, bf16[256,256]{1,0:T(8,128)(2,1)}, u32[]{:S(2)}, u32[]{:S(2)}) collective-permute-start(bf16[256,256]{1,0:T(8,128)(2,1)} %convert_element_type.171), channel_id=1, source_target_pairs={{0,16},{16,0},{32,48},{48,32},{1,17},{17,1},{33,49},{49,33},{2,18}... | collective-permute-start | bytes 393224 | tf_op jit(solution)/shard_map/ppermute | solution.py:31
  115.4 4.3 %copy-start.7 = (bf16[2,288,512]{2,1,0:T(8,128)(2,1)}, bf16[2,288,512]{2,1,0:T(8,128)(2,1)S(1)}, u32[]{:S(2)}) copy-start(bf16[2,288,512]{2,1,0:T(8,128)(2,1)S(1)} %broadcast_select_fusion.1.refs_8_) | copy-start | bytes 1769476
  118.8 18.9 %collective-permute-start.18 = (bf16[2,288,512]{2,1,0:T(8,128)(2,1)S(1)}, bf16[2,288,512]{2,1,0:T(8,128)(2,1)S(1)}, u32[]{:S(2)}, u32[]{:S(2)}) collective-permute-start(bf16[2,288,512]{2,1,0:T(8,128)(2,1)S(1)} %broadcast_select_fusion.1.refs_8_), channel_id=1, source_target_pairs={{0,64},{64,0},{128,192},{192,128},{1,65},{65,1},{129,193},{193,129... | collective-permute-start | bytes 1769480 | tf_op jit(solution)/shard_map/ppermute | solution.py:31
  118.8 19.3 %collective-permute-start.19 = (bf16[2,288,512]{2,1,0:T(8,128)(2,1)S(1)}, bf16[2,288,512]{2,1,0:T(8,128)(2,1)S(1)}, u32[]{:S(2)}, u32[]{:S(2)}) collective-permute-start(bf16[2,288,512]{2,1,0:T(8,128)(2,1)S(1)} %broadcast_select_fusion.1.refs_8_), channel_id=1, source_target_pairs={{0,16},{16,32},{32,48},{48,0},{1,17},{17,33},{33,49},{49,1},{2,18}... | collective-permute-start | bytes 1769480 | tf_op jit(solution)/shard_map/ppermute | solution.py:27
  119.7 18.5 %collective-permute-start.20 = (bf16[2,288,512]{2,1,0:T(8,128)(2,1)S(1)}, bf16[2,288,512]{2,1,0:T(8,128)(2,1)S(1)}, u32[]{:S(2)}, u32[]{:S(2)}) collective-permute-start(bf16[2,288,512]{2,1,0:T(8,128)(2,1)S(1)} %broadcast_select_fusion.1.refs_8_), channel_id=1, source_target_pairs={{0,48},{16,0},{32,16},{48,32},{1,49},{17,1},{33,17},{49,33},{2,50}... | collective-permute-start | bytes 1769480 | tf_op jit(solution)/shard_map/ppermute | solution.py:27
  122.2 15.5 %collective-permute-start.21 = (bf16[256,256]{1,0:T(8,128)(2,1)S(1)}, bf16[256,256]{1,0:T(8,128)(2,1)S(1)}, u32[]{:S(2)}, u32[]{:S(2)}) collective-permute-start(bf16[256,256]{1,0:T(8,128)(2,1)S(1)} %convert_element_type.173), channel_id=1, source_target_pairs={{0,32},{16,48},{32,0},{48,16},{1,33},{17,49},{33,1},{49,17},{2,34}... | collective-permute-start | bytes 393224 | tf_op jit(solution)/shard_map/ppermute | solution.py:31
  137.8 7.3 %copy-start.8 = (bf16[2,288,512]{2,1,0:T(8,128)(2,1)}, bf16[2,288,512]{2,1,0:T(8,128)(2,1)S(1)}, u32[]{:S(2)}) copy-start(bf16[2,288,512]{2,1,0:T(8,128)(2,1)S(1)} %collective-permute-done.18.refs_9_) | copy-start | bytes 1769476
  138.2 17.1 %copy-start.11 = (bf16[2,288,512]{2,1,0:T(8,128)(2,1)}, bf16[2,288,512]{2,1,0:T(8,128)(2,1)S(1)}, u32[]{:S(2)}) copy-start(bf16[2,288,512]{2,1,0:T(8,128)(2,1)S(1)} %collective-permute-done.19.refs_16_) | copy-start | bytes 1769476
  139.0 16.2 %collective-permute-start.22 = (bf16[2,288,512]{2,1,0:T(8,128)(2,1)S(1)}, bf16[2,288,512]{2,1,0:T(8,128)(2,1)}, u32[]{:S(2)}, u32[]{:S(2)}) collective-permute-start(bf16[2,288,512]{2,1,0:T(8,128)(2,1)S(1)} %collective-permute-done.18.refs_9_), channel_id=1, source_target_pairs={{0,16},{16,32},{32,48},{48,0},{1,17},{17,33},{33,49},{49,1},{2,18}... | collective-permute-start | bytes 1769480 | tf_op jit(solution)/shard_map/ppermute | solution.py:27
  140.0 15.3 %collective-permute-start.23 = (bf16[2,288,512]{2,1,0:T(8,128)(2,1)S(1)}, bf16[2,288,512]{2,1,0:T(8,128)(2,1)S(1)}, u32[]{:S(2)}, u32[]{:S(2)}) collective-permute-start(bf16[2,288,512]{2,1,0:T(8,128)(2,1)S(1)} %collective-permute-done.18.refs_9_), channel_id=1, source_target_pairs={{0,48},{16,0},{32,16},{48,32},{1,49},{17,1},{33,17},{49,33},{2,50}... | collective-permute-start | bytes 1769480 | tf_op jit(solution)/shard_map/ppermute | solution.py:27
  142.4 12.9 %collective-permute-start.24 = (bf16[512,256]{1,0:T(8,128)(2,1)S(1)}, bf16[512,256]{1,0:T(8,128)(2,1)S(1)}, u32[]{:S(2)}, u32[]{:S(2)}) collective-permute-start(bf16[512,256]{1,0:T(8,128)(2,1)S(1)} %get-tuple-element.111), channel_id=1, source_target_pairs={{0,128},{64,192},{128,0},{192,64},{1,129},{65,193},{129,1},{193,65... | collective-permute-start | bytes 786440 | tf_op jit(solution)/shard_map/ppermute | solution.py:27
  155.2 14.8 %copy-start.14 = (bf16[512,256]{1,0:T(8,128)(2,1)}, bf16[512,256]{1,0:T(8,128)(2,1)S(1)}, u32[]{:S(2)}) copy-start(bf16[512,256]{1,0:T(8,128)(2,1)S(1)} %collective-permute-done.24) | copy-start | bytes 786436
  156.1 16.0 %collective-permute-start.25 = (bf16[2,288,512]{2,1,0:T(8,128)(2,1)S(1)}, bf16[2,288,512]{2,1,0:T(8,128)(2,1)S(1)}, u32[]{:S(2)}, u32[]{:S(2)}) collective-permute-start(bf16[2,288,512]{2,1,0:T(8,128)(2,1)S(1)} %collective-permute-done.19.refs_16_), channel_id=1, source_target_pairs={{0,16},{16,32},{32,48},{48,0},{1,17},{17,33},{33,49},{49,1},{2,18}... | collective-permute-start | bytes 1769480 | tf_op jit(solution)/shard_map/ppermute | solution.py:27
  156.3 15.8 %collective-permute-start.26 = (bf16[2,288,512]{2,1,0:T(8,128)(2,1)}, bf16[2,288,512]{2,1,0:T(8,128)(2,1)S(1)}, u32[]{:S(2)}, u32[]{:S(2)}) collective-permute-start(bf16[2,288,512]{2,1,0:T(8,128)(2,1)} %copy-done.13), channel_id=1, source_target_pairs={{0,48},{16,0},{32,16},{48,32},{1,49},{17,1},{33,17},{49,33},{2,50}... | collective-permute-start | bytes 1769480 | tf_op jit(solution)/shard_map/ppermute | solution.py:27
  159.4 11.3 %collective-permute-start.27 = (bf16[512,256]{1,0:T(8,128)(2,1)}, bf16[512,256]{1,0:T(8,128)(2,1)S(1)}, u32[]{:S(2)}, u32[]{:S(2)}) collective-permute-start(bf16[512,256]{1,0:T(8,128)(2,1)} %get-tuple-element.119), channel_id=1, source_target_pairs={{0,64},{64,128},{128,192},{192,0},{1,65},{65,129},{129,193},{193,1... | collective-permute-start | bytes 786440 | tf_op jit(solution)/shard_map/ppermute | solution.py:27
  159.7 12.4 %collective-permute-start.28 = (bf16[512,256]{1,0:T(8,128)(2,1)}, bf16[512,256]{1,0:T(8,128)(2,1)}, u32[]{:S(2)}, u32[]{:S(2)}) collective-permute-start(bf16[512,256]{1,0:T(8,128)(2,1)} %get-tuple-element.120), channel_id=1, source_target_pairs={{0,192},{64,0},{128,64},{192,128},{1,193},{65,1},{129,65},{193,129... | collective-permute-start | bytes 786440 | tf_op jit(solution)/shard_map/ppermute | solution.py:27
  172.1 1.7 copy-start.10
  178.6 34.7 %collective-permute-start.29 = (f32[256,640]{1,0:T(8,128)}, f32[256,640]{1,0:T(8,128)S(1)}, u32[]{:S(2)}, u32[]{:S(2)}) collective-permute-start(f32[256,640]{1,0:T(8,128)} %get-tuple-element.138), channel_id=1, source_target_pairs={{0,8},{8,0},{1,9},{9,1},{2,10},{10,2},{3,11},{11,3},{4,12},{12,4},... | collective-permute-start | bytes 1966088 | tf_op jit(solution)/shard_map/ppermute | solution.py:27
  178.6 34.7 %copy-start = (f32[256,640]{1,0:T(8,128)S(1)}, f32[256,640]{1,0:T(8,128)}, u32[]{:S(2)}) copy-start(f32[256,640]{1,0:T(8,128)} %get-tuple-element.137.a) | copy-start | bytes 1966084
  179.0 28.4 %collective-permute-start.30 = (bf16[256,256]{1,0:T(8,128)(2,1)S(1)}, bf16[256,256]{1,0:T(8,128)(2,1)S(1)}, u32[]{:S(2)}, u32[]{:S(2)}) collective-permute-start(bf16[256,256]{1,0:T(8,128)(2,1)S(1)} %get-tuple-element.161), channel_id=1, source_target_pairs={{0,8},{1,40},{2,72},{3,104},{4,136},{5,168},{6,200},{7,232},{8,16}... | collective-permute-start | bytes 393224 | tf_op jit(solution)/shard_map/ppermute | solution.py:408
  179.1 32.5 %collective-permute-start.31 = (bf16[256,256]{1,0:T(8,128)(2,1)S(1)}, bf16[256,256]{1,0:T(8,128)(2,1)S(1)}, u32[]{:S(2)}, u32[]{:S(2)}) collective-permute-start(bf16[256,256]{1,0:T(8,128)(2,1)S(1)} %get-tuple-element.160), channel_id=1, source_target_pairs={{0,0},{1,56},{2,88},{3,120},{4,152},{5,184},{6,216},{7,248},{8,8},... | collective-permute-start | bytes 393224 | tf_op jit(solution)/shard_map/ppermute | solution.py:408
  (5 other events, 6.4 us)
